TPU v7x, 32 devices: a whole 2x2x4 slice. The times are simulated.
32 devices in a mesh: gx: 4 (over y, x), gy: 8 (over z, core).
Axes of the slice: x: 2, y: 2, z: 4, core: 2. Of those that a mesh axis runs over, the one named last changes fastest.
Arguments:
- source: float32 [8, 8, 8, 32, 256], P(None, None, 'gx', 'gy'), may hold values from -6 to 6
- geometry: float32 [3, 8, 32, 32], P(None, 'gx', 'gy'), may hold values from 0.5 to 2
- disc_mask: int32 [8, 32, 32], P('gx', 'gy'), may hold values 0 or 1
- thrust: float32 [8, 32, 32], P('gx', 'gy'), may hold values from 0.5 to 4
- xxt_factor: float32 [6, 32, 65536], P(None, None, ('gx', 'gy')), as said below
- col_count: int32 [6, 32], P(None, ('gx', 'gy')), may hold values from 8 to 32, as said below
Outputs:
- pressure: float32 [8, 8, 8, 32, 256], P(None, None, 'gx', 'gy')
Inputs may be any that keep to these rules, and one draw needn't show every extreme that they name: `col_count`: equal on all devices of a level-l group (flat device index along gx+gy agreeing after the lowest l bits are dropped); at every level some group has exactly 32. `xxt_factor`: Real-valued entries of order one or below.
All inputs are finite; a program needn't handle non-finite values. No bound on the sum of `disc_mask` on one device may be relied on, other than what follows from the above.
Results may differ from a plain program's by a relative error of at most 0.00018.
Values sent between devices are 32-bit elements; how exact they have to be, the bound alone decides.
No kernel may reach another device: no remote copies, remote signals or barrier semaphores. Data moves between devices by JAX's collectives and lax.ppermute only.
A program may use at most 128 MiB of HBM per device.

v0:
```python
import math

import jax
import jax.numpy as jnp
import numpy as np
from jax import lax
from jax.sharding import PartitionSpec as P

NODES = 8
CYCLES = 2
CHEB_DEGREE = 2


highest = lax.Precision.HIGHEST
bound_low = 0.3
bound_high = 3.0
shift_ratio = 0.25


def padded(block, sides, width):
    for axis, dim in sides:
        count = lax.axis_size(axis)
        forward = [(i, i + 1) for i in range(count - 1)]
        forward.append((count - 1, 0))
        backward = [(target, source) for source, target in forward]
        low = lax.ppermute(
            lax.slice_in_dim(block, block.shape[dim] - width, None, axis=dim), axis, forward
        )
        high = lax.ppermute(lax.slice_in_dim(block, 0, width, axis=dim), axis, backward)
        block = jnp.concatenate([low, block, high], axis=dim)
    return block


def swapped(x, axis, bit):
    return lax.ppermute(x, axis, [(i, i ^ 1 << bit) for i in range(lax.axis_size(axis))])


def legendre_table(points, poly_order):
    table = [points * 0.0 + 1.0, points]
    for degree in range(2, poly_order + 1):
        table.append(
            ((2.0 * degree - 1.0) * points * table[-1] - (degree - 1.0) * table[-2]) / degree
        )
    return table


def jacobi_eigen(matrix):
    size_n = matrix.shape[0]
    current = matrix.copy()
    vectors = np.eye(size_n)
    for sweep_index in range(30):
        for first in range(size_n - 1):
            for second in range(first + 1, size_n):
                angle = 0.5 * math.atan2(
                    2.0 * float(current[first, second]),
                    float(current[second, second] - current[first, first]),
                )
                rotation = np.eye(size_n)
                rotation[first, first] = math.cos(angle)
                rotation[second, second] = math.cos(angle)
                rotation[first, second] = math.sin(angle)
                rotation[second, first] = -math.sin(angle)
                current = rotation.T @ current @ rotation
                vectors = vectors @ rotation
    values = np.array([current[index, index] for index in range(size_n)])
    order = np.argsort(values)
    return (values[order], vectors[:, order])


def gll_tables(node_count):
    poly_order = node_count - 1
    points = np.cos(np.pi * np.arange(node_count) / poly_order)
    for newton_index in range(200):
        table = legendre_table(points, poly_order)
        points = points - (points * table[poly_order] - table[poly_order - 1]) / (
            node_count * table[poly_order]
        )
    points = points[::-1].copy()
    legendre = legendre_table(points, poly_order)[poly_order]
    weights = 2.0 / (poly_order * (poly_order + 1) * legendre**2)
    identity = np.eye(node_count)
    gap_matrix = points[:, None] - points[None, :] + identity
    off_diagonal = legendre[:, None] / (legendre[None, :] * gap_matrix) * (1.0 - identity)
    end_value = poly_order * (poly_order + 1) / 4.0
    end_terms = np.concatenate([[-end_value], np.zeros(node_count - 2), [end_value]])
    derivative = off_diagonal + identity * end_terms[None, :]
    stiffness = derivative.T @ (weights[:, None] * derivative)
    root_inverse = 1.0 / np.sqrt(weights)
    symmetric = root_inverse[:, None] * stiffness * root_inverse[None, :]
    symmetric = 0.5 * (symmetric + symmetric.T)
    eigen_values, eigen_vectors = jacobi_eigen(symmetric)
    eigen_modes = root_inverse[:, None] * eigen_vectors
    vertex_interp = np.stack([(1.0 - points) / 2.0, (1.0 + points) / 2.0], axis=1)
    return (
        weights.astype(np.float32),
        stiffness.astype(np.float32),
        eigen_modes.astype(np.float32),
        eigen_values.astype(np.float32),
        vertex_interp.astype(np.float32),
    )


def build_setup(geometry):
    weights, stiffness, eigen_modes, eigen_values, vertex_interp = gll_tables(NODES)
    elem_z = geometry.shape[3]
    z_count = elem_z * NODES
    lengths = jnp.repeat(geometry, NODES, axis=3)
    len_x = lengths[0][None, None]
    len_y = lengths[1][None, None]
    len_z = lengths[2][None, None]
    metric_x = len_y * len_z / (2.0 * len_x)
    metric_y = len_x * len_z / (2.0 * len_y)
    metric_z = len_x * len_y / (2.0 * len_z)
    node_weight = jnp.asarray(weights)
    weight_a = node_weight[:, None, None, None, None]
    weight_b = node_weight[None, :, None, None, None]
    weight_c = jnp.tile(node_weight, elem_z)
    coef_x = metric_x * weight_b * weight_c
    coef_y = metric_y * weight_a * weight_c
    coef_z = metric_z * weight_a * weight_b
    mass_diag = len_x * len_y * len_z / 8.0 * weight_a * weight_b * weight_c
    spectrum = jnp.asarray(eigen_values)
    denominator = (
        metric_x * spectrum[:, None, None, None, None]
        + metric_y * spectrum[None, :, None, None, None]
        + metric_z * jnp.tile(spectrum, elem_z)
        + shift_ratio * (metric_x + metric_y + metric_z)
    )
    inv_denom = 1.0 / denominator
    z_index = jnp.arange(z_count)
    z_node = z_index % NODES
    dirichlet = (z_index < z_count - 1).astype(jnp.float32)
    node_index = jnp.arange(NODES)
    edge_node = ((node_index == 0) | (node_index == NODES - 1)).astype(jnp.float32) + 1.0
    z_shared = (
        1.0
        + ((z_node == 0) & (z_index > 0)).astype(jnp.float32)
        + ((z_node == NODES - 1) & (z_index < z_count - 1)).astype(jnp.float32)
    )
    inv_mult = 1.0 / (
        edge_node[:, None, None, None, None] * edge_node[None, :, None, None, None] * z_shared
    )
    eye_z = jnp.eye(elem_z, dtype=jnp.float32)
    stiff_matrix = jnp.asarray(stiffness)
    mode_matrix = jnp.asarray(eigen_modes)
    interp = jnp.asarray(vertex_interp)
    z_stiff = jnp.kron(eye_z, stiff_matrix.T)
    z_modes = jnp.kron(eye_z, mode_matrix)
    z_modes_t = jnp.kron(eye_z, mode_matrix.T)
    z_restrict = jnp.kron(eye_z, interp)
    z_prolong = jnp.kron(eye_z, interp.T)
    link_up = (z_index[None, :] == z_index[:, None] + 1) & (z_node[:, None] == NODES - 1)
    link_down = (z_index[None, :] == z_index[:, None] - 1) & (z_node[:, None] == 0)
    z_sum = ((z_index[:, None] == z_index[None, :]) | link_up | link_down).astype(jnp.float32)
    return (
        coef_x,
        coef_y,
        coef_z,
        mass_diag,
        inv_denom,
        dirichlet,
        inv_mult,
        stiff_matrix,
        mode_matrix,
        z_stiff,
        z_modes,
        z_modes_t,
        z_restrict,
        z_prolong,
        z_sum,
        interp,
    )


def pair_sum_x(data_field, prev_high, next_low):
    low_face = data_field[0]
    high_face = data_field[-1]
    before_faces = jnp.concatenate([prev_high[:, None], high_face[:, :-1]], axis=1)
    after_faces = jnp.concatenate([low_face[:, 1:], next_low[:, None]], axis=1)
    return jnp.concatenate(
        [(low_face + before_faces)[None], data_field[1:-1], (high_face + after_faces)[None]], axis=0
    )


def pair_sum_y(data_field, prev_high, next_low):
    low_face = data_field[:, 0]
    high_face = data_field[:, -1]
    before_faces = jnp.concatenate([prev_high[:, :, None], high_face[:, :, :-1]], axis=2)
    after_faces = jnp.concatenate([low_face[:, :, 1:], next_low[:, :, None]], axis=2)
    return jnp.concatenate(
        [
            (low_face + before_faces)[:, None],
            data_field[:, 1:-1],
            (high_face + after_faces)[:, None],
        ],
        axis=1,
    )


def corner_slot(line_values, node_count):
    padding = jnp.zeros((node_count - 1, line_values.shape[0]), jnp.float32)
    return jnp.concatenate([line_values[None], padding], axis=0)


def summed_neighbour_face(raw_face, prev_line, next_line):
    node_count, elem_x, z_count = raw_face.shape
    shaped = raw_face.reshape(node_count, 1, elem_x, 1, z_count)
    summed = pair_sum_x(shaped, prev_line[None, None], next_line[None, None])
    return summed.reshape(node_count, elem_x, z_count)


def assemble(data_field, z_sum):
    node_count = data_field.shape[0]
    elem_x = data_field.shape[2]
    elem_y = data_field.shape[3]
    z_count = data_field.shape[4]
    frame = jnp.zeros((elem_x + 2, elem_y + 2, node_count, z_count), jnp.float32)
    frame = frame.at[0, 1 : elem_y + 1].set(jnp.transpose(data_field[0][:, 0], (1, 0, 2)))
    frame = frame.at[elem_x + 1, 1 : elem_y + 1].set(
        jnp.transpose(data_field[-1][:, -1], (1, 0, 2))
    )
    frame = frame.at[1 : elem_x + 1, 0].set(jnp.transpose(data_field[:, 0][:, :, 0], (1, 0, 2)))
    frame = frame.at[1 : elem_x + 1, elem_y + 1].set(
        jnp.transpose(data_field[:, -1][:, :, -1], (1, 0, 2))
    )
    frame = frame.at[0, 0].set(corner_slot(data_field[0, 0, 0, 0], node_count))
    frame = frame.at[0, elem_y + 1].set(corner_slot(data_field[0, -1, 0, -1], node_count))
    frame = frame.at[elem_x + 1, 0].set(corner_slot(data_field[-1, 0, -1, 0], node_count))
    frame = frame.at[elem_x + 1, elem_y + 1].set(
        corner_slot(data_field[-1, -1, -1, -1], node_count)
    )
    bordered = padded(frame, (("gx", 0), ("gy", 1)), 1)
    last_x = elem_x + 3
    last_y = elem_y + 3
    left_high = jnp.transpose(bordered[0, 2 : elem_y + 2], (1, 0, 2))
    right_low = jnp.transpose(bordered[last_x, 2 : elem_y + 2], (1, 0, 2))
    down_raw = jnp.transpose(bordered[2 : elem_x + 2, 0], (1, 0, 2))
    up_raw = jnp.transpose(bordered[2 : elem_x + 2, last_y], (1, 0, 2))
    down_high = summed_neighbour_face(down_raw, bordered[0, 0][0], bordered[last_x, 0][0])
    up_low = summed_neighbour_face(up_raw, bordered[0, last_y][0], bordered[last_x, last_y][0])
    data_field = pair_sum_x(data_field, left_high, right_low)
    data_field = pair_sum_y(data_field, down_high, up_low)
    return jnp.matmul(data_field, z_sum, precision=highest)


def chebyshev(solution, resid, apply_op, precond, keep_resid):
    center = 0.5 * (bound_high + bound_low)
    radius = 0.5 * (bound_high - bound_low)
    center_ratio = center / radius
    rho_old = 1.0 / center_ratio
    direction = precond(resid) / center
    for step_index in range(CHEB_DEGREE):
        solution = solution + direction
        if step_index < CHEB_DEGREE - 1 or keep_resid:
            resid = resid - apply_op(direction)
        if step_index < CHEB_DEGREE - 1:
            rho_new = 1.0 / (2.0 * center_ratio - rho_old)
            direction = rho_new * rho_old * direction + 2.0 * rho_new / radius * precond(resid)
            rho_old = rho_new
    return (solution, resid)


def pressure_solve(source, disc_mask, thrust, setup_tables, assembler, coarse_solve):
    (
        coef_x,
        coef_y,
        coef_z,
        mass_diag,
        inv_denom,
        dirichlet,
        inv_mult,
        stiff_matrix,
        mode_matrix,
        z_stiff,
        z_modes,
        z_modes_t,
        z_restrict,
        z_prolong,
        z_sum,
        interp,
    ) = setup_tables

    def apply_op(data_field):
        along_x = jnp.einsum("ac,cbxyz->abxyz", stiff_matrix, data_field, precision=highest)
        along_y = jnp.einsum("bc,acxyz->abxyz", stiff_matrix, data_field, precision=highest)
        along_z = jnp.matmul(data_field, z_stiff, precision=highest)
        return dirichlet * assembler(coef_x * along_x + coef_y * along_y + coef_z * along_z, z_sum)

    def precond(resid):
        spectral = jnp.einsum("ai,abxyz->ibxyz", mode_matrix, resid, precision=highest)
        spectral = jnp.einsum("bj,abxyz->ajxyz", mode_matrix, spectral, precision=highest)
        spectral = jnp.matmul(spectral, z_modes, precision=highest) * inv_denom
        spectral = jnp.einsum("ai,ibxyz->abxyz", mode_matrix, spectral, precision=highest)
        spectral = jnp.einsum("bj,ajxyz->abxyz", mode_matrix, spectral, precision=highest)
        return (
            dirichlet
            * inv_mult
            * assembler(jnp.matmul(spectral, z_modes_t, precision=highest), z_sum)
        )

    forcing = source + jnp.repeat(disc_mask.astype(jnp.float32) * thrust, NODES, axis=2)[None, None]
    rhs_field = dirichlet * assembler(mass_diag * forcing, z_sum)
    solution = jnp.zeros_like(rhs_field)
    for sweep_index in range(CYCLES):
        if sweep_index == 0:
            resid = rhs_field
        else:
            resid = rhs_field - apply_op(solution)
        solution, resid = chebyshev(solution, resid, apply_op, precond, True)
        restrict_coarse = jnp.einsum("av,abxyz->vbxyz", interp, inv_mult * resid, precision=highest)
        restrict_coarse = jnp.einsum("bu,vbxyz->vuxyz", interp, restrict_coarse, precision=highest)
        correction = coarse_solve(jnp.matmul(restrict_coarse, z_restrict, precision=highest))
        fine_field = jnp.einsum("av,vuxyz->auxyz", interp, correction, precision=highest)
        fine_field = jnp.einsum("bu,auxyz->abxyz", interp, fine_field, precision=highest)
        solution = solution + dirichlet * inv_mult * assembler(
            jnp.matmul(fine_field, z_prolong, precision=highest), z_sum
        )
        resid = rhs_field - apply_op(solution)
        solution, resid = chebyshev(solution, resid, apply_op, precond, False)
    return solution


def per_device(source, geometry, disc_mask, thrust, xxt_factor, col_count):
    setup_tables = build_setup(geometry)

    def coarse_solve(coarse):
        flattened = coarse.reshape(-1)
        partial_value = jnp.einsum("lkn,n->lk", xxt_factor, flattened, precision=highest)
        live_mask = (jnp.arange(xxt_factor.shape[1])[None, :] < col_count).astype(jnp.float32)
        partial_value = partial_value * live_mask
        bit_count = (lax.axis_size("gx") * lax.axis_size("gy")).bit_length() - 1
        for bit_index in range(bit_count):
            upper_levels = partial_value[bit_index + 1 :]
            partner = swapped(upper_levels, ("gx", "gy"), bit_index)
            partial_value = jnp.concatenate(
                [partial_value[: bit_index + 1], upper_levels + partner], axis=0
            )
        return jnp.einsum("lkn,lk->n", xxt_factor, partial_value, precision=highest).reshape(
            coarse.shape
        )

    return pressure_solve(source, disc_mask, thrust, setup_tables, assemble, coarse_solve)


def solution(mesh):
    return jax.shard_map(
        per_device,
        mesh=mesh,
        in_specs=(
            P(None, None, "gx", "gy", None),
            P(None, "gx", "gy", None),
            P("gx", "gy", None),
            P("gx", "gy", None),
            P(None, None, ("gx", "gy")),
            P(None, ("gx", "gy")),
        ),
        out_specs=P(None, None, "gx", "gy", None),
        check_vma=False,
    )
```

profile of v0, /device:TPU:0, one launch (start us, length us, event | category | flops | bytes accessed | tf_op | source)
XLA Modules:
  0.0 471.1 jit_solution(10138672905786624368)
XLA Ops:
  13.1 3.0 collective-permute-start
  18.7 5.1 %broadcast_multiply_fusion.1 = (f32[32,8,32,8]{3,2,1,0:T(8,128)}, f32[32,8,32,8]{3,2,1,0:T(8,128)}, f32[32,8,32,8]{3,2,1,0:T(8,128)}) fusion(f32[8,8]{1,0:T(8,128)S(1)} %copy-done.39, f32[32,32]{1,0:T(8,128)S(1)} %fusion.398, f32[8,8]{1,0:T(8,128)S(1)} %copy-done.40, f32[8,8]{1,0:T(8,128)S(1)} %copy-done.41), kind=kLoop, calls=%fused_computation.10 | loop fusion | flops 196608 | bytes 791296 | tf_op jit(solution)/shard_map/jit(kron)/mul | solution.py:149
  27.1 4.0 reshape.10759
  31.1 4.0 reshape.10754
  35.2 4.1 reshape.10757
  40.3 3.0 collective-permute-start.3
  46.4 5.3 %collective-permute-done.2 = f32[6,1,8,256]{3,2,0,1:T(8,128)S(1)} collective-permute-done((f32[6,1,8,256]{3,2,0,1:T(8,128)S(1)}, f32[6,1,8,256]{3,2,0,1:T(8,128)S(1)}, u32[]{:S(2)}, u32[]{:S(2)}) %collective-permute-start.2) | collective-permute-done | bytes 49184 | tf_op jit(solution)/shard_map/ppermute | solution.py:26
  61.8 2.3 collective-permute-start.5
  68.9 3.5 collective-permute-done.6
  79.4 2.5 collective-permute-start.8
  88.0 3.8 collective-permute-done.10
  104.1 2.0 collective-permute-done.12
  108.4 3.5 collective-permute-done.14
  126.9 3.9 collective-permute-done.18
  133.5 3.1 fusion.562
  139.9 3.5 collective-permute-done.21
  143.5 4.4 collective-permute-done.22
  149.6 2.1 collective-permute-done.23
  153.2 2.0 collective-permute-done.24
  164.0 2.0 collective-permute-done.25
  168.7 3.6 collective-permute-done.27
  179.3 2.9 collective-permute-start.29
  188.5 3.5 collective-permute-done.31
  204.4 2.0 collective-permute-done.33
  208.6 3.5 collective-permute-done.35
  222.1 2.0 collective-permute-done.37
  227.1 3.8 collective-permute-done.39
  243.2 2.0 collective-permute-done.41
  248.0 3.5 collective-permute-done.43
  258.6 2.5 collective-permute-start.45
  261.6 2.0 collective-permute-done.45
  267.1 3.9 collective-permute-done.47
  287.5 3.5 collective-permute-done.51
  305.9 4.2 collective-permute-done.55
  327.2 3.5 collective-permute-done.59
  337.7 2.4 collective-permute-start.61
  346.2 3.8 collective-permute-done.63
  352.7 3.1 fusion.563
  357.2 3.5 collective-permute-done.66
  360.9 4.4 collective-permute-done.67
  366.4 2.6 collective-permute-done.68
  369.6 3.1 collective-permute-done.69
  385.6 3.6 collective-permute-done.72
  404.3 4.0 collective-permute-done.76
  425.4 3.5 collective-permute-done.80
  435.9 2.4 collective-permute-start.82
  444.3 4.0 collective-permute-done.84
  464.9 3.5 collective-permute-done.88
  (1442 shorter events, 304.0 us)
Async XLA Ops:
  13.1 26.3 %collective-permute-start = (f32[1,6,8,256]{3,2,1,0:T(8,128)}, f32[1,6,8,256]{3,2,1,0:T(8,128)}, u32[]{:S(2)}, u32[]{:S(2)}) collective-permute-start(f32[1,6,8,256]{3,2,1,0:T(8,128)} %get-tuple-element.2248), channel_id=1, source_target_pairs={{0,8},{8,16},{16,24},{24,0},{1,9},{9,17},{17,25},{25,1},{2,10},{10... | collective-permute-start | bytes 147464 | tf_op jit(solution)/shard_map/ppermute | solution.py:26
  16.1 23.3 %collective-permute-start.1 = (f32[1,6,8,256]{3,2,0,1:T(8,128)}, f32[1,6,8,256]{3,2,0,1:T(8,128)}, u32[]{:S(2)}, u32[]{:S(2)}) collective-permute-start(f32[1,6,8,256]{3,2,0,1:T(8,128)} %get-tuple-element.2249), channel_id=1, source_target_pairs={{8,0},{16,8},{24,16},{0,24},{9,1},{17,9},{25,17},{1,25},{10,2},{18... | collective-permute-start | bytes 147464 | tf_op jit(solution)/shard_map/ppermute | solution.py:29
  40.3 6.1 %collective-permute-start.3 = (f32[6,1,8,256]{3,2,0,1:T(8,128)S(1)}, f32[6,1,8,256]{3,2,0,1:T(8,128)S(1)}, u32[]{:S(2)}, u32[]{:S(2)}) collective-permute-start(f32[6,1,8,256]{3,2,0,1:T(8,128)S(1)} %get-tuple-element.2209), channel_id=1, source_target_pairs={{1,0},{2,1},{3,2},{4,3},{5,4},{6,5},{7,6},{0,7},{9,8},{10,9},{11,1... | collective-permute-start | bytes 147464 | tf_op jit(solution)/shard_map/ppermute | solution.py:29
  45.9 5.8 %collective-permute-start.2 = (f32[6,1,8,256]{3,2,0,1:T(8,128)S(1)}, f32[6,1,8,256]{3,2,0,1:T(8,128)S(1)}, u32[]{:S(2)}, u32[]{:S(2)}) collective-permute-start(f32[6,1,8,256]{3,2,0,1:T(8,128)S(1)} %get-tuple-element.2208), channel_id=1, source_target_pairs={{0,1},{1,2},{2,3},{3,4},{4,5},{5,6},{6,7},{7,0},{8,9},{9,10},{10,1... | collective-permute-start | bytes 147464 | tf_op jit(solution)/shard_map/ppermute | solution.py:26
  61.1 5.0 %collective-permute-start.4 = (f32[1,6,8,256]{3,2,1,0:T(8,128)S(1)}, f32[1,6,8,256]{3,2,1,0:T(8,128)S(1)}, u32[]{:S(2)}, u32[]{:S(2)}) collective-permute-start(f32[1,6,8,256]{3,2,1,0:T(8,128)S(1)} %get-tuple-element.2246), channel_id=1, source_target_pairs={{0,8},{8,16},{16,24},{24,0},{1,9},{9,17},{17,25},{25,1},{2,10},{10... | collective-permute-start | bytes 147464 | tf_op jit(solution)/shard_map/ppermute | solution.py:26
  61.8 5.0 %collective-permute-start.5 = (f32[1,6,8,256]{3,2,1,0:T(8,128)S(1)}, f32[1,6,8,256]{3,2,1,0:T(8,128)S(1)}, u32[]{:S(2)}, u32[]{:S(2)}) collective-permute-start(f32[1,6,8,256]{3,2,1,0:T(8,128)S(1)} %get-tuple-element.2247), channel_id=1, source_target_pairs={{8,0},{16,8},{24,16},{0,24},{9,1},{17,9},{25,17},{1,25},{10,2},{18... | collective-permute-start | bytes 147464 | tf_op jit(solution)/shard_map/ppermute | solution.py:29
  67.0 5.4 %collective-permute-start.6 = (f32[6,1,8,256]{3,2,1,0:T(8,128)S(1)}, f32[6,1,8,256]{3,2,1,0:T(8,128)S(1)}, u32[]{:S(2)}, u32[]{:S(2)}) collective-permute-start(f32[6,1,8,256]{3,2,1,0:T(8,128)S(1)} %get-tuple-element.2206), channel_id=1, source_target_pairs={{0,1},{1,2},{2,3},{3,4},{4,5},{5,6},{6,7},{7,0},{8,9},{9,10},{10,1... | collective-permute-start | bytes 147464 | tf_op jit(solution)/shard_map/ppermute | solution.py:26
  79.4 5.0 %collective-permute-start.8 = (f32[1,6,8,256]{3,2,1,0:T(8,128)S(1)}, f32[1,6,8,256]{3,2,1,0:T(8,128)S(1)}, u32[]{:S(2)}, u32[]{:S(2)}) collective-permute-start(f32[1,6,8,256]{3,2,1,0:T(8,128)S(1)} %get-tuple-element.2244), channel_id=1, source_target_pairs={{0,8},{8,16},{16,24},{24,0},{1,9},{9,17},{17,25},{25,1},{2,10},{10... | collective-permute-start | bytes 147464 | tf_op jit(solution)/shard_map/ppermute | solution.py:26
  81.9 4.1 collective-permute-start.9
  86.3 5.5 %collective-permute-start.10 = (f32[6,1,8,256]{3,2,0,1:T(8,128)S(1)}, f32[6,1,8,256]{3,2,0,1:T(8,128)S(1)}, u32[]{:S(2)}, u32[]{:S(2)}) collective-permute-start(f32[6,1,8,256]{3,2,0,1:T(8,128)S(1)} %get-tuple-element.2204), channel_id=1, source_target_pairs={{0,1},{1,2},{2,3},{3,4},{4,5},{5,6},{6,7},{7,0},{8,9},{9,10},{10,1... | collective-permute-start | bytes 147464 | tf_op jit(solution)/shard_map/ppermute | solution.py:26
  101.1 5.0 %collective-permute-start.12 = (f32[1,6,8,256]{3,2,1,0:T(8,128)S(1)}, f32[1,6,8,256]{3,2,1,0:T(8,128)S(1)}, u32[]{:S(2)}, u32[]{:S(2)}) collective-permute-start(f32[1,6,8,256]{3,2,1,0:T(8,128)S(1)} %get-tuple-element.2242), channel_id=1, source_target_pairs={{0,8},{8,16},{16,24},{24,0},{1,9},{9,17},{17,25},{25,1},{2,10},{10... | collective-permute-start | bytes 147464 | tf_op jit(solution)/shard_map/ppermute | solution.py:26
  106.5 5.4 %collective-permute-start.14 = (f32[6,1,8,256]{3,2,1,0:T(8,128)S(1)}, f32[6,1,8,256]{3,2,1,0:T(8,128)S(1)}, u32[]{:S(2)}, u32[]{:S(2)}) collective-permute-start(f32[6,1,8,256]{3,2,1,0:T(8,128)S(1)} %get-tuple-element.2202), channel_id=1, source_target_pairs={{0,1},{1,2},{2,3},{3,4},{4,5},{5,6},{6,7},{7,0},{8,9},{9,10},{10,1... | collective-permute-start | bytes 147464 | tf_op jit(solution)/shard_map/ppermute | solution.py:26
  118.9 5.0 %collective-permute-start.16 = (f32[1,6,8,256]{3,2,1,0:T(8,128)S(1)}, f32[1,6,8,256]{3,2,1,0:T(8,128)S(1)}, u32[]{:S(2)}, u32[]{:S(2)}) collective-permute-start(f32[1,6,8,256]{3,2,1,0:T(8,128)S(1)} %get-tuple-element.2240), channel_id=1, source_target_pairs={{0,8},{8,16},{16,24},{24,0},{1,9},{9,17},{17,25},{25,1},{2,10},{10... | collective-permute-start | bytes 147464 | tf_op jit(solution)/shard_map/ppermute | solution.py:26
  125.2 5.6 %collective-permute-start.18 = (f32[6,1,8,256]{3,2,0,1:T(8,128)S(1)}, f32[6,1,8,256]{3,2,0,1:T(8,128)S(1)}, u32[]{:S(2)}, u32[]{:S(2)}) collective-permute-start(f32[6,1,8,256]{3,2,0,1:T(8,128)S(1)} %get-tuple-element.2200), channel_id=1, source_target_pairs={{0,1},{1,2},{2,3},{3,4},{4,5},{5,6},{6,7},{7,0},{8,9},{9,10},{10,1... | collective-permute-start | bytes 147464 | tf_op jit(solution)/shard_map/ppermute | solution.py:26
  143.4 4.5 collective-permute-start.22
  161.0 5.0 %collective-permute-start.25 = (f32[1,6,8,256]{3,2,1,0:T(8,128)S(1)}, f32[1,6,8,256]{3,2,1,0:T(8,128)S(1)}, u32[]{:S(2)}, u32[]{:S(2)}) collective-permute-start(f32[1,6,8,256]{3,2,1,0:T(8,128)S(1)} %get-tuple-element.2238), channel_id=1, source_target_pairs={{0,8},{8,16},{16,24},{24,0},{1,9},{9,17},{17,25},{25,1},{2,10},{10... | collective-permute-start | bytes 147464 | tf_op jit(solution)/shard_map/ppermute | solution.py:26
  162.5 4.1 collective-permute-start.26
  166.9 5.4 %collective-permute-start.27 = (f32[6,1,8,256]{3,2,1,0:T(8,128)S(1)}, f32[6,1,8,256]{3,2,1,0:T(8,128)S(1)}, u32[]{:S(2)}, u32[]{:S(2)}) collective-permute-start(f32[6,1,8,256]{3,2,1,0:T(8,128)S(1)} %get-tuple-element.2198), channel_id=1, source_target_pairs={{0,1},{1,2},{2,3},{3,4},{4,5},{5,6},{6,7},{7,0},{8,9},{9,10},{10,1... | collective-permute-start | bytes 147464 | tf_op jit(solution)/shard_map/ppermute | solution.py:26
  179.3 5.4 %collective-permute-start.29 = (f32[1,6,8,256]{3,2,1,0:T(8,128)S(1)}, f32[1,6,8,256]{3,2,1,0:T(8,128)S(1)}, u32[]{:S(2)}, u32[]{:S(2)}) collective-permute-start(f32[1,6,8,256]{3,2,1,0:T(8,128)S(1)} %get-tuple-element.2236), channel_id=1, source_target_pairs={{0,8},{8,16},{16,24},{24,0},{1,9},{9,17},{17,25},{25,1},{2,10},{10... | collective-permute-start | bytes 147464 | tf_op jit(solution)/shard_map/ppermute | solution.py:26
  186.6 5.4 %collective-permute-start.31 = (f32[6,1,8,256]{3,2,0,1:T(8,128)S(1)}, f32[6,1,8,256]{3,2,0,1:T(8,128)S(1)}, u32[]{:S(2)}, u32[]{:S(2)}) collective-permute-start(f32[6,1,8,256]{3,2,0,1:T(8,128)S(1)} %get-tuple-element.2196), channel_id=1, source_target_pairs={{0,1},{1,2},{2,3},{3,4},{4,5},{5,6},{6,7},{7,0},{8,9},{9,10},{10,1... | collective-permute-start | bytes 147464 | tf_op jit(solution)/shard_map/ppermute | solution.py:26
  201.4 5.0 %collective-permute-start.33 = (f32[1,6,8,256]{3,2,1,0:T(8,128)S(1)}, f32[1,6,8,256]{3,2,1,0:T(8,128)S(1)}, u32[]{:S(2)}, u32[]{:S(2)}) collective-permute-start(f32[1,6,8,256]{3,2,1,0:T(8,128)S(1)} %get-tuple-element.2234), channel_id=1, source_target_pairs={{0,8},{8,16},{16,24},{24,0},{1,9},{9,17},{17,25},{25,1},{2,10},{10... | collective-permute-start | bytes 147464 | tf_op jit(solution)/shard_map/ppermute | solution.py:26
  206.8 5.4 %collective-permute-start.35 = (f32[6,1,8,256]{3,2,1,0:T(8,128)S(1)}, f32[6,1,8,256]{3,2,1,0:T(8,128)S(1)}, u32[]{:S(2)}, u32[]{:S(2)}) collective-permute-start(f32[6,1,8,256]{3,2,1,0:T(8,128)S(1)} %get-tuple-element.2194), channel_id=1, source_target_pairs={{0,1},{1,2},{2,3},{3,4},{4,5},{5,6},{6,7},{7,0},{8,9},{9,10},{10,1... | collective-permute-start | bytes 147464 | tf_op jit(solution)/shard_map/ppermute | solution.py:26
  219.1 5.0 %collective-permute-start.37 = (f32[1,6,8,256]{3,2,1,0:T(8,128)S(1)}, f32[1,6,8,256]{3,2,1,0:T(8,128)S(1)}, u32[]{:S(2)}, u32[]{:S(2)}) collective-permute-start(f32[1,6,8,256]{3,2,1,0:T(8,128)S(1)} %get-tuple-element.2232), channel_id=1, source_target_pairs={{0,8},{8,16},{16,24},{24,0},{1,9},{9,17},{17,25},{25,1},{2,10},{10... | collective-permute-start | bytes 147464 | tf_op jit(solution)/shard_map/ppermute | solution.py:26
  225.4 5.5 %collective-permute-start.39 = (f32[6,1,8,256]{3,2,0,1:T(8,128)S(1)}, f32[6,1,8,256]{3,2,0,1:T(8,128)S(1)}, u32[]{:S(2)}, u32[]{:S(2)}) collective-permute-start(f32[6,1,8,256]{3,2,0,1:T(8,128)S(1)} %get-tuple-element.2192), channel_id=1, source_target_pairs={{0,1},{1,2},{2,3},{3,4},{4,5},{5,6},{6,7},{7,0},{8,9},{9,10},{10,1... | collective-permute-start | bytes 147464 | tf_op jit(solution)/shard_map/ppermute | solution.py:26
  240.2 5.0 %collective-permute-start.41 = (f32[1,6,8,256]{3,2,1,0:T(8,128)S(1)}, f32[1,6,8,256]{3,2,1,0:T(8,128)S(1)}, u32[]{:S(2)}, u32[]{:S(2)}) collective-permute-start(f32[1,6,8,256]{3,2,1,0:T(8,128)S(1)} %get-tuple-element.2230), channel_id=1, source_target_pairs={{0,8},{8,16},{16,24},{24,0},{1,9},{9,17},{17,25},{25,1},{2,10},{10... | collective-permute-start | bytes 147464 | tf_op jit(solution)/shard_map/ppermute | solution.py:26
  241.8 4.1 collective-permute-start.42
  246.2 5.4 %collective-permute-start.43 = (f32[6,1,8,256]{3,2,1,0:T(8,128)S(1)}, f32[6,1,8,256]{3,2,1,0:T(8,128)S(1)}, u32[]{:S(2)}, u32[]{:S(2)}) collective-permute-start(f32[6,1,8,256]{3,2,1,0:T(8,128)S(1)} %get-tuple-element.2190), channel_id=1, source_target_pairs={{0,1},{1,2},{2,3},{3,4},{4,5},{5,6},{6,7},{7,0},{8,9},{9,10},{10,1... | collective-permute-start | bytes 147464 | tf_op jit(solution)/shard_map/ppermute | solution.py:26
  258.6 5.0 %collective-permute-start.45 = (f32[1,6,8,256]{3,2,1,0:T(8,128)S(1)}, f32[1,6,8,256]{3,2,1,0:T(8,128)S(1)}, u32[]{:S(2)}, u32[]{:S(2)}) collective-permute-start(f32[1,6,8,256]{3,2,1,0:T(8,128)S(1)} %get-tuple-element.2228), channel_id=1, source_target_pairs={{0,8},{8,16},{16,24},{24,0},{1,9},{9,17},{17,25},{25,1},{2,10},{10... | collective-permute-start | bytes 147464 | tf_op jit(solution)/shard_map/ppermute | solution.py:26
  265.4 5.6 %collective-permute-start.47 = (f32[6,1,8,256]{3,2,0,1:T(8,128)S(1)}, f32[6,1,8,256]{3,2,0,1:T(8,128)S(1)}, u32[]{:S(2)}, u32[]{:S(2)}) collective-permute-start(f32[6,1,8,256]{3,2,0,1:T(8,128)S(1)} %get-tuple-element.2188), channel_id=1, source_target_pairs={{0,1},{1,2},{2,3},{3,4},{4,5},{5,6},{6,7},{7,0},{8,9},{9,10},{10,1... | collective-permute-start | bytes 147464 | tf_op jit(solution)/shard_map/ppermute | solution.py:26
  280.3 5.0 %collective-permute-start.49 = (f32[1,6,8,256]{3,2,1,0:T(8,128)S(1)}, f32[1,6,8,256]{3,2,1,0:T(8,128)S(1)}, u32[]{:S(2)}, u32[]{:S(2)}) collective-permute-start(f32[1,6,8,256]{3,2,1,0:T(8,128)S(1)} %get-tuple-element.2226), channel_id=1, source_target_pairs={{0,8},{8,16},{16,24},{24,0},{1,9},{9,17},{17,25},{25,1},{2,10},{10... | collective-permute-start | bytes 147464 | tf_op jit(solution)/shard_map/ppermute | solution.py:26
  285.7 5.4 %collective-permute-start.51 = (f32[6,1,8,256]{3,2,1,0:T(8,128)S(1)}, f32[6,1,8,256]{3,2,1,0:T(8,128)S(1)}, u32[]{:S(2)}, u32[]{:S(2)}) collective-permute-start(f32[6,1,8,256]{3,2,1,0:T(8,128)S(1)} %get-tuple-element.2186), channel_id=1, source_target_pairs={{0,1},{1,2},{2,3},{3,4},{4,5},{5,6},{6,7},{7,0},{8,9},{9,10},{10,1... | collective-permute-start | bytes 147464 | tf_op jit(solution)/shard_map/ppermute | solution.py:26
  298.0 5.0 %collective-permute-start.53 = (f32[1,6,8,256]{3,2,1,0:T(8,128)S(1)}, f32[1,6,8,256]{3,2,1,0:T(8,128)S(1)}, u32[]{:S(2)}, u32[]{:S(2)}) collective-permute-start(f32[1,6,8,256]{3,2,1,0:T(8,128)S(1)} %get-tuple-element.2224), channel_id=1, source_target_pairs={{0,8},{8,16},{16,24},{24,0},{1,9},{9,17},{17,25},{25,1},{2,10},{10... | collective-permute-start | bytes 147464 | tf_op jit(solution)/shard_map/ppermute | solution.py:26
  304.3 5.8 %collective-permute-start.55 = (f32[6,1,8,256]{3,2,0,1:T(8,128)S(1)}, f32[6,1,8,256]{3,2,0,1:T(8,128)S(1)}, u32[]{:S(2)}, u32[]{:S(2)}) collective-permute-start(f32[6,1,8,256]{3,2,0,1:T(8,128)S(1)} %get-tuple-element.2184), channel_id=1, source_target_pairs={{0,1},{1,2},{2,3},{3,4},{4,5},{5,6},{6,7},{7,0},{8,9},{9,10},{10,1... | collective-permute-start | bytes 147464 | tf_op jit(solution)/shard_map/ppermute | solution.py:26
  319.4 5.0 %collective-permute-start.57 = (f32[1,6,8,256]{3,2,1,0:T(8,128)S(1)}, f32[1,6,8,256]{3,2,1,0:T(8,128)S(1)}, u32[]{:S(2)}, u32[]{:S(2)}) collective-permute-start(f32[1,6,8,256]{3,2,1,0:T(8,128)S(1)} %get-tuple-element.2222), channel_id=1, source_target_pairs={{0,8},{8,16},{16,24},{24,0},{1,9},{9,17},{17,25},{25,1},{2,10},{10... | collective-permute-start | bytes 147464 | tf_op jit(solution)/shard_map/ppermute | solution.py:26
  325.3 5.4 %collective-permute-start.59 = (f32[6,1,8,256]{3,2,1,0:T(8,128)S(1)}, f32[6,1,8,256]{3,2,1,0:T(8,128)S(1)}, u32[]{:S(2)}, u32[]{:S(2)}) collective-permute-start(f32[6,1,8,256]{3,2,1,0:T(8,128)S(1)} %get-tuple-element.2182), channel_id=1, source_target_pairs={{0,1},{1,2},{2,3},{3,4},{4,5},{5,6},{6,7},{7,0},{8,9},{9,10},{10,1... | collective-permute-start | bytes 147464 | tf_op jit(solution)/shard_map/ppermute | solution.py:26
  337.7 5.0 %collective-permute-start.61 = (f32[1,6,8,256]{3,2,1,0:T(8,128)S(1)}, f32[1,6,8,256]{3,2,1,0:T(8,128)S(1)}, u32[]{:S(2)}, u32[]{:S(2)}) collective-permute-start(f32[1,6,8,256]{3,2,1,0:T(8,128)S(1)} %get-tuple-element.2220), channel_id=1, source_target_pairs={{0,8},{8,16},{16,24},{24,0},{1,9},{9,17},{17,25},{25,1},{2,10},{10... | collective-permute-start | bytes 147464 | tf_op jit(solution)/shard_map/ppermute | solution.py:26
  344.5 5.5 %collective-permute-start.63 = (f32[6,1,8,256]{3,2,0,1:T(8,128)S(1)}, f32[6,1,8,256]{3,2,0,1:T(8,128)S(1)}, u32[]{:S(2)}, u32[]{:S(2)}) collective-permute-start(f32[6,1,8,256]{3,2,0,1:T(8,128)S(1)} %get-tuple-element.2180), channel_id=1, source_target_pairs={{0,1},{1,2},{2,3},{3,4},{4,5},{5,6},{6,7},{7,0},{8,9},{9,10},{10,1... | collective-permute-start | bytes 147464 | tf_op jit(solution)/shard_map/ppermute | solution.py:26
  360.8 4.5 collective-permute-start.67
  378.3 5.0 %collective-permute-start.70 = (f32[1,6,8,256]{3,2,1,0:T(8,128)S(1)}, f32[1,6,8,256]{3,2,1,0:T(8,128)S(1)}, u32[]{:S(2)}, u32[]{:S(2)}) collective-permute-start(f32[1,6,8,256]{3,2,1,0:T(8,128)S(1)} %get-tuple-element.2218), channel_id=1, source_target_pairs={{0,8},{8,16},{16,24},{24,0},{1,9},{9,17},{17,25},{25,1},{2,10},{10... | collective-permute-start | bytes 147464 | tf_op jit(solution)/shard_map/ppermute | solution.py:26
  383.8 5.4 %collective-permute-start.72 = (f32[6,1,8,256]{3,2,1,0:T(8,128)S(1)}, f32[6,1,8,256]{3,2,1,0:T(8,128)S(1)}, u32[]{:S(2)}, u32[]{:S(2)}) collective-permute-start(f32[6,1,8,256]{3,2,1,0:T(8,128)S(1)} %get-tuple-element.2178), channel_id=1, source_target_pairs={{0,1},{1,2},{2,3},{3,4},{4,5},{5,6},{6,7},{7,0},{8,9},{9,10},{10,1... | collective-permute-start | bytes 147464 | tf_op jit(solution)/shard_map/ppermute | solution.py:26
  396.3 5.0 %collective-permute-start.74 = (f32[1,6,8,256]{3,2,1,0:T(8,128)S(1)}, f32[1,6,8,256]{3,2,1,0:T(8,128)S(1)}, u32[]{:S(2)}, u32[]{:S(2)}) collective-permute-start(f32[1,6,8,256]{3,2,1,0:T(8,128)S(1)} %get-tuple-element.2216), channel_id=1, source_target_pairs={{0,8},{8,16},{16,24},{24,0},{1,9},{9,17},{17,25},{25,1},{2,10},{10... | collective-permute-start | bytes 147464 | tf_op jit(solution)/shard_map/ppermute | solution.py:26
  402.6 5.6 %collective-permute-start.76 = (f32[6,1,8,256]{3,2,1,0:T(8,128)S(1)}, f32[6,1,8,256]{3,2,1,0:T(8,128)S(1)}, u32[]{:S(2)}, u32[]{:S(2)}) collective-permute-start(f32[6,1,8,256]{3,2,1,0:T(8,128)S(1)} %get-tuple-element.2176), channel_id=1, source_target_pairs={{0,1},{1,2},{2,3},{3,4},{4,5},{5,6},{6,7},{7,0},{8,9},{9,10},{10,1... | collective-permute-start | bytes 147464 | tf_op jit(solution)/shard_map/ppermute | solution.py:26
  417.6 5.0 %collective-permute-start.78 = (f32[1,6,8,256]{3,2,1,0:T(8,128)S(1)}, f32[1,6,8,256]{3,2,1,0:T(8,128)S(1)}, u32[]{:S(2)}, u32[]{:S(2)}) collective-permute-start(f32[1,6,8,256]{3,2,1,0:T(8,128)S(1)} %get-tuple-element.2214), channel_id=1, source_target_pairs={{0,8},{8,16},{16,24},{24,0},{1,9},{9,17},{17,25},{25,1},{2,10},{10... | collective-permute-start | bytes 147464 | tf_op jit(solution)/shard_map/ppermute | solution.py:26
  423.5 5.4 %collective-permute-start.80 = (f32[6,1,8,256]{3,2,1,0:T(8,128)S(1)}, f32[6,1,8,256]{3,2,1,0:T(8,128)S(1)}, u32[]{:S(2)}, u32[]{:S(2)}) collective-permute-start(f32[6,1,8,256]{3,2,1,0:T(8,128)S(1)} %get-tuple-element.2174), channel_id=1, source_target_pairs={{0,1},{1,2},{2,3},{3,4},{4,5},{5,6},{6,7},{7,0},{8,9},{9,10},{10,1... | collective-permute-start | bytes 147464 | tf_op jit(solution)/shard_map/ppermute | solution.py:26
  435.9 5.0 %collective-permute-start.82 = (f32[1,6,8,256]{3,2,1,0:T(8,128)S(1)}, f32[1,6,8,256]{3,2,1,0:T(8,128)S(1)}, u32[]{:S(2)}, u32[]{:S(2)}) collective-permute-start(f32[1,6,8,256]{3,2,1,0:T(8,128)S(1)} %get-tuple-element.2212), channel_id=1, source_target_pairs={{0,8},{8,16},{16,24},{24,0},{1,9},{9,17},{17,25},{25,1},{2,10},{10... | collective-permute-start | bytes 147464 | tf_op jit(solution)/shard_map/ppermute | solution.py:26
  442.7 5.6 %collective-permute-start.84 = (f32[6,1,8,256]{3,2,0,1:T(8,128)S(1)}, f32[6,1,8,256]{3,2,0,1:T(8,128)S(1)}, u32[]{:S(2)}, u32[]{:S(2)}) collective-permute-start(f32[6,1,8,256]{3,2,0,1:T(8,128)S(1)} %get-tuple-element.2172), channel_id=1, source_target_pairs={{0,1},{1,2},{2,3},{3,4},{4,5},{5,6},{6,7},{7,0},{8,9},{9,10},{10,1... | collective-permute-start | bytes 147464 | tf_op jit(solution)/shard_map/ppermute | solution.py:26
  457.6 5.0 %collective-permute-start.86 = (f32[1,6,8,256]{3,2,1,0:T(8,128)S(1)}, f32[1,6,8,256]{3,2,1,0:T(8,128)S(1)}, u32[]{:S(2)}, u32[]{:S(2)}) collective-permute-start(f32[1,6,8,256]{3,2,1,0:T(8,128)S(1)} %get-tuple-element.2210), channel_id=1, source_target_pairs={{0,8},{8,16},{16,24},{24,0},{1,9},{9,17},{17,25},{25,1},{2,10},{10... | collective-permute-start | bytes 147464 | tf_op jit(solution)/shard_map/ppermute | solution.py:26
  463.0 5.4 %collective-permute-start.88 = (f32[6,1,8,256]{3,2,1,0:T(8,128)S(1)}, f32[6,1,8,256]{3,2,1,0:T(8,128)S(1)}, u32[]{:S(2)}, u32[]{:S(2)}) collective-permute-start(f32[6,1,8,256]{3,2,1,0:T(8,128)S(1)} %get-tuple-element.2170), channel_id=1, source_target_pairs={{0,1},{1,2},{2,3},{3,4},{4,5},{5,6},{6,7},{7,0},{8,9},{9,10},{10,1... | collective-permute-start | bytes 147464 | tf_op jit(solution)/shard_map/ppermute | solution.py:26
  (105 other events, 712.3 us)
where the time goes:
time: 478 us; the launch traced here: 471 us
  waiting for transfers between devices  177 us (37%)
  matrix products  84.1 us (18%)
  starting transfers between devices  82.4 us (17%)
  local copies, waits for them, and re-layouts  62.1 us (13%)
  other arithmetic  56.1 us (12%)
  between operations  9.23 us (2%)
    ppermute x40, waiting for transfers between devices, padded(): lax.ppermute(lax.slice_in_dim(block, block.shape[dim] - width, None, axis...  114 us
    ppermute x40, starting transfers between devices, padded(): lax.ppermute(lax.slice_in_dim(block, block.shape[dim] - width, None, axis...  47.7 us
    scatter x20, other arithmetic, assemble(): frame.at[0, elem_y + 1]  36.4 us
    ppermute x40, waiting for transfers between devices, padded(): lax.ppermute(lax.slice_in_dim(block, 0, width, axis=dim), axis, backward)  36.2 us
    ppermute x40, starting transfers between devices, padded(): lax.ppermute(lax.slice_in_dim(block, 0, width, axis=dim), axis, backward)  29.7 us
    ppermute x10, waiting for transfers between devices, swapped(): lax.ppermute(x, axis, [(i, i ^ 1 << bit) for i in range(lax.axis_size(axi...  26.9 us
    scatter x20, local copies, waits for them, and re-layouts, assemble(): frame.at[0, 1:elem_y + 1].set(jnp.transpose(data_field[0][:, 0], (1, 0, 2)))  26.6 us
    dot_general x20, matrix products, assemble(): return jnp.matmul(data_field, z_sum, precision=highest)  13.7 us
  transfers between devices with their start and end apart: 90, of which 86 were waited for; matrix products, arithmetic and copies ran while one was open for 7% of the time, Pallas kernels for 0%

commit v1 on v0

--- a/solution.py
+++ b/solution.py
@@ -1,9 +1,12 @@
+import functools
 import math
 
 import jax
 import jax.numpy as jnp
 import numpy as np
 from jax import lax
+from jax.experimental import pallas as pl
+from jax.experimental.pallas import tpu as pltpu
 from jax.sharding import PartitionSpec as P
 
 NODES = 8
@@ -342,9 +345,541 @@
     return pressure_solve(source, disc_mask, thrust, setup_tables, assemble, coarse_solve)
 
 
+VMEM = pltpu.VMEM
+SMEM = pltpu.SMEM
+f32 = jnp.float32
+bf16 = jnp.bfloat16
+
+
+def device_ring(gx_count, gy_count):
+    layers = gy_count // 2
+    chips = []
+    for z in range(layers):
+        pair = [(0, 0), (0, 1)]
+        chips += [(y, x, z) for y, x in (pair if z % 2 == 0 else pair[::-1])]
+    for k, z in enumerate(reversed(range(layers))):
+        pair = [(1, 0), (1, 1)] if layers % 2 == 0 else [(1, 1), (1, 0)]
+        chips += [(y, x, z) for y, x in (pair if k % 2 == 0 else pair[::-1])]
+    return [(y * 2 + x) * gy_count + z * 2 + core for y, x, z in chips for core in (0, 1)]
+
+
+def split_bf16(values):
+    high = values.astype(np.float32).astype(bf16)
+    low = (values - high.astype(np.float64)).astype(np.float32).astype(bf16)
+    return high, low
+
+
+def wide(matrix):
+    high, low = split_bf16(matrix)
+    return np.concatenate([high, high, low], axis=1)
+
+
+@functools.lru_cache(maxsize=None)
+def constant_tables(ez_count, lanes):
+    weights, _, modes, values, interp = [
+        np.asarray(t, np.float64) for t in gll_tables(NODES)
+    ]
+    half = NODES // 2
+    root = np.sqrt(weights)
+    basis = root[:, None] * modes
+    parity = np.sign(np.sum(basis * basis[::-1], axis=0))
+    basis = 0.5 * (basis + parity * basis[::-1])
+    even = [i for i in range(NODES) if parity[i] > 0]
+    odd = [i for i in range(NODES) if parity[i] < 0]
+    blocks = []
+    for picked in (even, odd):
+        blocks.append(np.kron(basis[:half, picked].T, np.kron(basis.T, basis.T)))
+    forward = np.stack([wide(m) for m in blocks])
+    backward = np.stack([wide(m.T) for m in blocks])
+    order_b = even + odd
+    one = np.ones(NODES)
+    lam_a = np.kron(one, np.kron(values, one))
+    lam_b = np.kron(values[order_b], np.kron(one, one))
+    lam_c = np.kron(one, np.kron(one, values))
+    spectrum = np.stack([lam_a, lam_b, lam_c] + [0 * lam_a] * 5, axis=1)
+    root3 = np.kron(root, np.kron(root, root))
+    edge = np.where((np.arange(NODES) == 0) | (np.arange(NODES) == NODES - 1), 0.5, 1.0)
+    jw = interp * root[:, None] * edge[:, None]
+    first = np.zeros_like(jw)
+    first[0] = jw[0]
+    def rows_of(jc):
+        return np.stack(
+            [
+                np.kron(jw[:, u], np.kron(jw[:, v], jc[:, t]))
+                for t in (0, 1) for v in (0, 1) for u in (0, 1)
+            ]
+        )
+    restrict = np.concatenate([rows_of(jw), rows_of(first)], axis=0)
+    jp = interp * root[:, None]
+    prolong = np.stack(
+        [
+            np.kron(jp[:, u], np.kron(jp[:, v], jp[:, t]))
+            for t in (0, 1) for v in (0, 1) for u in (0, 1)
+        ],
+        axis=1,
+    )
+    swap = np.zeros((4 * ez_count, 4 * ez_count))
+    for t in range(2):
+        for ex in range(2):
+            for ez in range(ez_count):
+                swap[(t * 2 + ex) * ez_count + ez, ex * 2 * ez_count + 2 * ez + t] = 1.0
+    as32 = lambda t: np.asarray(t, np.float32)
+    return dict(
+        forward=forward,
+        backward=backward,
+        spectrum=as32(spectrum),
+        root3=as32(root3[:, None]),
+        inv_root3=as32(1.0 / root3[:, None]),
+        restrict=as32(restrict),
+        prolong=as32(prolong),
+        swap=as32(swap),
+        unswap=as32(swap.T),
+    )
+
+
+def hp_dot(a, b):
+    return jnp.dot(a, b, precision=highest, preferred_element_type=f32)
+
+
+def wide_dot(table, field):
+    high = field.astype(bf16)
+    low = (field - high.astype(f32)).astype(bf16)
+    stacked = jnp.concatenate([high, low, high], axis=0)
+    return jnp.dot(table, stacked, preferred_element_type=f32)
+
+
+def spectral_apply(field, forward_ref, backward_ref, scale_ref):
+    face = field.shape[0] // NODES
+    half = field.shape[0] // 2
+    top = field[:half]
+    bottom = jnp.concatenate(
+        [field[(NODES - 1 - b) * face : (NODES - b) * face] for b in range(NODES // 2)], axis=0
+    )
+    even = wide_dot(forward_ref[0], top + bottom) * scale_ref[:half]
+    odd = wide_dot(forward_ref[1], top - bottom) * scale_ref[half:]
+    even = wide_dot(backward_ref[0], even)
+    odd = wide_dot(backward_ref[1], odd)
+    low_half = even + odd
+    diff = even - odd
+    parts = [low_half] + [diff[b * face : (b + 1) * face] for b in reversed(range(NODES // 2))]
+    return jnp.concatenate(parts, axis=0)
+
+
+def lane_layer(shape, ez_count):
+    return lax.rem(lax.broadcasted_iota(jnp.int32, shape, 1), ez_count)
+
+
+def lane_halves(ref):
+    rows = ref.shape[0] // 2
+    return jnp.concatenate([ref[:rows], ref[rows:]], axis=1)
+
+
+def store_halves(ref, field):
+    rows = field.shape[0]
+    ref[:rows] = field[:, :128]
+    ref[rows:] = field[:, 128:]
+
+
+def assemble_local(field, out_ref, low_ref, high_ref, ez_count, average):
+    rows, lanes = field.shape
+    face = rows // NODES
+    tile = NODES
+    f4 = field.reshape(NODES, NODES, tile, lanes)
+    a_low = f4[:, 0].reshape(face, lanes)
+    a_high = f4[:, NODES - 1].reshape(face, lanes)
+    new_low = a_low + pltpu.roll(a_high, ez_count, 1)
+    new_high = a_high + pltpu.roll(a_low, lanes - ez_count, 1)
+    if average:
+        new_low = 0.5 * new_low
+        new_high = 0.5 * new_high
+    store_halves(out_ref, field)
+    layer = lane_layer((face, 128), ez_count)
+    for side in range(2):
+        base = side * rows
+        span = slice(side * 128, (side + 1) * 128)
+        for b in range(NODES):
+            at = base + b * face
+            out_ref[at : at + tile] = new_low[b * tile : (b + 1) * tile, span]
+            out_ref[at + face - tile : at + face] = new_high[b * tile : (b + 1) * tile, span]
+        c_low = out_ref[pl.ds(base, face, stride=NODES), :]
+        c_high = out_ref[pl.ds(base + NODES - 1, face, stride=NODES), :]
+        above = c_low + pltpu.roll(c_high, 1, 1)
+        below = c_high + pltpu.roll(c_low, 127, 1)
+        if average:
+            above = 0.5 * above
+            below = 0.5 * below
+        out_ref[pl.ds(base, face, stride=NODES), :] = jnp.where(layer > 0, above, c_low)
+        out_ref[pl.ds(base + NODES - 1, face, stride=NODES), :] = jnp.where(
+            layer < ez_count - 1, below, 0.0
+        )
+        low_ref[:, span] = out_ref[base : base + face]
+        high_ref[:, span] = out_ref[base + rows - face : base + rows]
+
+
+def joined(w_ref, from_prev_ref, from_next_ref, scale):
+    face = from_prev_ref.shape[0]
+    rows = w_ref.shape[0] // 2
+    field = lane_halves(w_ref)
+    low = field[:face] + from_prev_ref[...]
+    high = field[rows - face :] + from_next_ref[...]
+    if scale != 1.0:
+        low = low * scale
+        high = high * scale
+    return jnp.concatenate([low, field[face : rows - face], high], axis=0)
+
+
+def entry_kernel(ez_count, *refs):
+    (shift_ref, q0, q1, q2, q3, spectrum_ref, root_ref,
+     w_ref, low_ref, high_ref, inv_ref, den_ref, live_ref, held) = refs
+    rows = w_ref.shape[0] // 2
+    face = rows // NODES
+    lanes = 2 * w_ref.shape[1]
+    parts = 4
+    width = lanes // parts
+    for q, ref in enumerate((q0, q1, q2, q3)):
+        held[lax.rem(shift_ref[0] - q + parts, parts)] = ref[...]
+    sizes = jnp.concatenate([held[i, face : face + 8, :width] for i in range(parts)], axis=1)
+    len_x, len_y, len_z = sizes[0:1], sizes[1:2], sizes[2:3]
+    metric_x = len_y * len_z / (2.0 * len_x)
+    metric_y = len_x * len_z / (2.0 * len_y)
+    metric_z = len_x * len_y / (2.0 * len_z)
+    volume = len_x * len_y * len_z / 8.0
+    metrics = jnp.concatenate(
+        [metric_x, metric_y, metric_z, jnp.zeros((5, lanes), f32)], axis=0
+    )
+    stiff = hp_dot(spectrum_ref[...], metrics)
+    den_ref[...] = stiff
+    inv_ref[...] = 1.0 / (stiff + shift_ratio * (metric_x + metric_y + metric_z))
+    for i in range(parts):
+        live = held[i, face + 3 : face + 4, : 2 * 128]
+        live_ref[2 * i : 2 * i + 1] = live[:, :128]
+        live_ref[2 * i + 1 : 2 * i + 2] = live[:, 128:]
+    for c in range(NODES):
+        for side in range(2):
+            w_ref[pl.ds(side * rows + c, face, stride=NODES), :] = jnp.concatenate(
+                [held[i, :face, c * width : (c + 1) * width] for i in (2 * side, 2 * side + 1)],
+                axis=1,
+            )
+    forcing = lane_halves(w_ref) * (root_ref[...] * volume)
+    assemble_local(forcing, w_ref, low_ref, high_ref, ez_count, False)
+
+
+def precond_kernel(ez_count, first, *refs):
+    if first:
+        (w_ref, prev_ref, next_ref, fwd_ref, bwd_ref, inv_ref,
+         r_ref, u_ref, low_ref, high_ref) = refs
+        resid = joined(w_ref, prev_ref, next_ref, 1.0)
+    else:
+        (w_ref, prev_ref, next_ref, r_in_ref, fwd_ref, bwd_ref, inv_ref,
+         r_ref, u_ref, low_ref, high_ref) = refs
+        resid = r_in_ref[...] - joined(w_ref, prev_ref, next_ref, 1.0)
+    r_ref[...] = resid
+    field = spectral_apply(resid, fwd_ref, bwd_ref, inv_ref)
+    assemble_local(field, u_ref, low_ref, high_ref, ez_count, True)
+
+
+def apply_kernel(ez_count, keep, gain, start, keep_d, *refs):
+    refs = list(refs)
+    w_ref, prev_ref, next_ref = refs[:3]
+    refs = refs[3:]
+    step = joined(w_ref, prev_ref, next_ref, 0.5)
+    if gain != 1.0:
+        step = step * gain
+    if keep != 0.0:
+        step = step + keep * refs.pop(0)[...]
+    total = step if start else refs.pop(0)[...] + step
+    fwd_ref, bwd_ref, den_ref = refs[:3]
+    refs = refs[3:]
+    x_ref, k_ref, low_ref, high_ref = refs[:4]
+    x_ref[...] = total
+    if keep_d:
+        refs[4][...] = step
+    field = spectral_apply(step, fwd_ref, bwd_ref, den_ref)
+    assemble_local(field, k_ref, low_ref, high_ref, ez_count, False)
+
+
+def restrict_kernel(ez_count, *refs):
+    (shift_ref, w_ref, prev_ref, next_ref, r_in_ref, restrict_ref, swap_ref, x0, x1, x2, x3,
+     r_ref, part_ref, coarse, sums) = refs
+    lanes = 2 * w_ref.shape[1]
+    parts = 4
+    width = lanes // parts
+    resid = r_in_ref[...] - joined(w_ref, prev_ref, next_ref, 1.0)
+    r_ref[...] = resid
+    rows = hp_dot(restrict_ref[...], resid)
+    b = rows[:8] + jnp.where(lane_layer((8, lanes), ez_count) == 0, rows[8:], 0.0)
+    for i in range(parts):
+        pair = jnp.concatenate(
+            [b[:4, i * width : (i + 1) * width], b[4:, i * width : (i + 1) * width]], axis=1
+        )
+        coarse[i] = hp_dot(jnp.concatenate([pair, pair], axis=0), swap_ref[...])
+    sums[...] = jnp.zeros_like(sums)
+    count = x0.shape[0]
+    block = 2 * width
+    for q, ref in enumerate((x0, x1, x2, x3)):
+        i = lax.rem(shift_ref[0] - q + parts, parts)
+        mine = coarse[i]
+        acc = ref[:, :block] * mine[0:1]
+        for vu in range(1, 4):
+            acc = acc + ref[:, vu * block : (vu + 1) * block] * mine[vu : vu + 1]
+        sums[i, :count] = acc
+    flat = sums[...].reshape(parts * sums.shape[1], block)
+    ones = jnp.ones((8, block), f32)
+    row = lax.dot_general(
+        ones, flat, (((1,), (1,)), ((), ())), precision=highest, preferred_element_type=f32
+    )
+    for i in range(2 * parts):
+        part_ref[i : i + 1] = row[0:1, i * 128 : (i + 1) * 128]
+
+
+def prolong_kernel(ez_count, inner_levels, cols, *refs):
+    (shift_ref, all_ref, member_ref, live_ref, unswap_ref, prolong_ref, x0, x1, x2, x3,
+     w_ref, low_ref, high_ref, table, coarse) = refs
+    lanes = 2 * w_ref.shape[1]
+    parts = 4
+    width = lanes // parts
+    block = 2 * width
+    count = x0.shape[0]
+    base = all_ref[0] * member_ref[0]
+    for source in range(1, all_ref.shape[0]):
+        base = base + all_ref[source] * member_ref[source]
+    row_id = lax.broadcasted_iota(jnp.int32, base.shape, 0)
+    lane_id = lax.broadcasted_iota(jnp.int32, base.shape, 1)
+    level = (lax.rem(row_id, 2) * 128 + lane_id) // cols
+    total = base
+    step = 2
+    for bit in range(2):
+        flip = jnp.where(
+            lax.rem(row_id // step, 2) == 0,
+            pltpu.roll(total, 8 - step, 0),
+            pltpu.roll(total, step, 0),
+        )
+        total = jnp.where(level > inner_levels + bit, total + flip, total)
+        step *= 2
+    total = total * live_ref[...]
+    turned = jnp.transpose(total)
+    for i in range(parts):
+        table[i, :128] = jnp.broadcast_to(turned[:, 2 * i : 2 * i + 1], (128, block))
+        table[i, 128:] = jnp.broadcast_to(turned[:, 2 * i + 1 : 2 * i + 2], (128, block))
+    for q, ref in enumerate((x0, x1, x2, x3)):
+        i = lax.rem(shift_ref[0] - q + parts, parts)
+        y = table[i, :count]
+        for vu in range(4):
+            coarse[i, vu : vu + 1] = jnp.sum(
+                ref[:, vu * block : (vu + 1) * block] * y, axis=0, keepdims=True
+            )
+    lows, highs = [], []
+    for i in range(parts):
+        pair = hp_dot(coarse[i], unswap_ref[...])
+        lows.append(pair[:4, :width])
+        highs.append(pair[:4, width:])
+    e = jnp.concatenate([jnp.concatenate(lows, axis=1), jnp.concatenate(highs, axis=1)], axis=0)
+    field = hp_dot(prolong_ref[...], e)
+    assemble_local(field, w_ref, low_ref, high_ref, ez_count, True)
+
+
+def exit_kernel(keep, gain, *refs):
+    (shift_ref, w_ref, prev_ref, next_ref, d_ref, x_ref, inv_root_ref,
+     q0, q1, q2, q3, field, held) = refs
+    lanes = 2 * w_ref.shape[1]
+    parts = 4
+    width = lanes // parts
+    face = prev_ref.shape[0]
+    step = joined(w_ref, prev_ref, next_ref, 0.5) * gain + keep * d_ref[...]
+    rows = x_ref.shape[0]
+    store_halves(field, (x_ref[...] + step) * inv_root_ref[...])
+    for c in range(NODES):
+        for side in range(2):
+            layer = field[pl.ds(side * rows + c, face, stride=NODES), :]
+            for i in range(2):
+                held[2 * side + i, :, c * width : (c + 1) * width] = layer[
+                    :, i * width : (i + 1) * width
+                ]
+    for q, ref in enumerate((q0, q1, q2, q3)):
+        ref[...] = held[lax.rem(shift_ref[0] - q + parts, parts)]
+
+
+def call(kernel, name, out_shapes, args, scratch=(), smem_args=0):
+    specs = [pl.BlockSpec(memory_space=SMEM)] * smem_args
+    specs += [pl.BlockSpec(memory_space=VMEM)] * (len(args) - smem_args)
+    return pl.pallas_call(
+        kernel,
+        name=name,
+        out_shape=[jax.ShapeDtypeStruct(s, f32) for s in out_shapes],
+        in_specs=specs,
+        out_specs=[pl.BlockSpec(memory_space=VMEM)] * len(out_shapes),
+        scratch_shapes=list(scratch),
+        compiler_params=pltpu.CompilerParams(vmem_limit_bytes=24 * 1024 * 1024),
+    )(*args)
+
+
+def fast_device(source, geometry, disc_mask, thrust, xxt_factor, col_count):
+    gx_count, gy_count = lax.axis_size("gx"), lax.axis_size("gy")
+    axes = ("gx", "gy")
+    nodes, _, elem_x, elem_y, z_count = source.shape
+    ez_count = geometry.shape[3]
+    levels, cols, _ = xxt_factor.shape
+    parts = gx_count
+    lanes = parts * elem_x * ez_count
+    width = elem_x * ez_count
+    rows = nodes**3
+    face = nodes * nodes
+    devices = gx_count * gy_count
+    tables = {k: jnp.asarray(v) for k, v in constant_tables(ez_count, lanes).items()}
+    ring = device_ring(gx_count, gy_count)
+    place = np.zeros(devices, np.int32)
+    for position, device in enumerate(ring):
+        place[device] = position
+    gx_index, gy_index = lax.axis_index("gx"), lax.axis_index("gy")
+    position = jnp.asarray(place)[gx_index * gy_count + gy_index]
+    shift = lax.rem(position, parts)
+    shift_arr = shift[None].astype(jnp.int32)
+    up = [(ring[i], ring[(i + 1) % devices]) for i in range(devices)]
+    down = [(target, origin) for origin, target in up]
+
+    def spread(q):
+        return [
+            (i * gy_count + j, ring[parts * j + (q + i) % parts])
+            for i in range(gx_count)
+            for j in range(gy_count)
+        ]
+
+    def halo(low, high):
+        return lax.ppermute(high, axes, up), lax.ppermute(low, axes, down)
+
+    def chunk(stack, q):
+        return lax.dynamic_index_in_dim(stack, lax.rem(q + gx_index, parts), 0, keepdims=False)
+
+    force = source + jnp.repeat(disc_mask.astype(f32) * thrust, nodes, axis=2)[None, None]
+    force = force.reshape(nodes, nodes, elem_x, elem_y, ez_count, nodes)
+    force = force.transpose(3, 1, 0, 5, 2, 4).reshape(elem_y, face, nodes * width)
+    sizes = geometry.transpose(2, 0, 1, 3).reshape(elem_y, 3, width)
+    sizes = jnp.pad(sizes, ((0, 0), (0, 0), (0, nodes * width - width)))
+    live = (jnp.arange(cols)[None, :] < col_count).astype(f32).reshape(1, 1, levels * cols)
+    live = jnp.pad(live, ((0, 0), (0, 0), (0, nodes * width - levels * cols)))
+    live = jnp.broadcast_to(live, (elem_y, 1, nodes * width))
+    packed = jnp.concatenate(
+        [force, sizes, live, jnp.zeros((elem_y, 4, nodes * width), f32)], axis=1
+    )
+    received = [lax.ppermute(chunk(packed, q), axes, spread(q)) for q in range(parts)]
+
+    factor = xxt_factor.reshape(levels * cols, 4 * elem_x, elem_y, 2 * ez_count)
+    factor = factor.transpose(2, 0, 1, 3).reshape(elem_y, levels * cols, 8 * width)
+    factors = [lax.ppermute(chunk(factor, q), axes, spread(q)) for q in range(parts)]
+
+    inner_levels = gy_count.bit_length() - 1
+    level_of = np.minimum(np.arange(256) // cols, 31)
+    group_of = place // parts
+    member = (
+        jnp.right_shift(jnp.asarray(group_of)[:, None], jnp.asarray(level_of)[None])
+        == jnp.right_shift(position // parts, jnp.asarray(level_of))[None]
+    ) & (np.arange(256) < levels * cols)[None]
+    member = jnp.tile(member.astype(f32), (1, parts)).reshape(devices, 2 * parts, 128)
+
+    fshape = (rows, lanes)
+    sshape = (2 * rows, lanes // 2)
+    hshape = (face, lanes)
+    w, low, high, inv, den, live_tile = call(
+        functools.partial(entry_kernel, ez_count), "entry",
+        [sshape, hshape, hshape, fshape, fshape, (2 * parts, 128)],
+        [shift_arr, *received, tables["spectrum"], tables["root3"]],
+        [VMEM((parts, face + 8, nodes * width), f32)], 1,
+    )
+    fwd, bwd = tables["forward"], tables["backward"]
+
+    def precond(w, low, high, resid):
+        prev, nxt = halo(low, high)
+        args = [w, prev, nxt] + ([] if resid is None else [resid]) + [fwd, bwd, inv]
+        return call(
+            functools.partial(precond_kernel, ez_count, resid is None), "precond",
+            [fshape, sshape, hshape, hshape], args,
+        )
+
+    def advance(w, low, high, d, x, keep, gain, keep_d):
+        prev, nxt = halo(low, high)
+        args = [w, prev, nxt] + ([] if keep == 0.0 else [d]) + ([] if x is None else [x])
+        out = call(
+            functools.partial(apply_kernel, ez_count, keep, gain, x is None, keep_d), "apply",
+            [fshape, sshape, hshape, hshape] + ([fshape] if keep_d else []),
+            args + [fwd, bwd, den],
+        )
+        return out[0], out[1], out[2], out[3], (out[4] if keep_d else None)
+
+    center = 0.5 * (bound_high + bound_low)
+    radius = 0.5 * (bound_high - bound_low)
+    ratio = center / radius
+    rho_old = 1.0 / ratio
+    rho_new = 1.0 / (2.0 * ratio - rho_old)
+    first_gain = 1.0 / center
+    keep = rho_new * rho_old
+    gain = 2.0 * rho_new / radius
+
+    x = None
+    resid = None
+    for cycle in range(CYCLES):
+        resid, u, low, high = precond(w, low, high, resid)
+        x, k, low, high, d = advance(u, low, high, None, x, 0.0, first_gain, True)
+        resid, u, low, high = precond(k, low, high, resid)
+        x, k, low, high, _ = advance(u, low, high, d, x, keep, gain, False)
+        prev, nxt = halo(low, high)
+        resid, partial = call(
+            functools.partial(restrict_kernel, ez_count), "restrict",
+            [fshape, (2 * parts, 128)],
+            [shift_arr, k, prev, nxt, resid, tables["restrict"], tables["swap"], *factors],
+            [VMEM((parts, 8, 2 * width), f32), VMEM((parts, 256, 2 * width), f32)], 1,
+        )
+        everyone = lax.all_to_all(
+            jnp.broadcast_to(partial[None], (devices,) + partial.shape), axes, 0, 0
+        )
+        f, low, high = call(
+            functools.partial(prolong_kernel, ez_count, inner_levels, cols), "prolong",
+            [sshape, hshape, hshape],
+            [shift_arr, everyone, member, live_tile, tables["unswap"], tables["prolong"], *factors],
+            [VMEM((parts, 256, 2 * width), f32), VMEM((parts, 8, 2 * width), f32)], 1,
+        )
+        x, k, low, high, _ = advance(f, low, high, None, x, 0.0, 1.0, False)
+        resid, u, low, high = precond(k, low, high, resid)
+        x, k, low, high, d = advance(u, low, high, None, x, 0.0, first_gain, True)
+        resid, u, low, high = precond(k, low, high, resid)
+        if cycle < CYCLES - 1:
+            x, w, low, high, _ = advance(u, low, high, d, x, keep, gain, False)
+    prev, nxt = halo(low, high)
+    chunks = call(
+        functools.partial(exit_kernel, keep, gain), "exit",
+        [(face, nodes * width)] * parts,
+        [shift_arr, u, prev, nxt, d, x, tables["inv_root3"]],
+        [VMEM(sshape, f32), VMEM((parts, face, nodes * width), f32)], 1,
+    )
+    back = [
+        lax.ppermute(chunks[q], axes, [(t, s) for s, t in spread(q)]) for q in range(parts)
+    ]
+    stacked = jnp.stack(back + back)
+    start = lax.rem(parts - gx_index, parts)
+    by_ey = lax.dynamic_slice_in_dim(stacked, start, parts, 0)
+    by_ey = by_ey.reshape(elem_y, nodes, nodes, nodes, elem_x, ez_count)
+    return by_ey.transpose(2, 1, 4, 0, 5, 3).reshape(source.shape)
+
+
+def is_fast(mesh, source, geometry, xxt_factor):
+    gx_count, gy_count = mesh.shape["gx"], mesh.shape["gy"]
+    nodes, _, elem_x, elem_y, z_count = source.shape
+    ez_count = geometry.shape[3]
+    levels, cols, _ = xxt_factor.shape
+    return (
+        gx_count == 4 and elem_y == gx_count and gy_count % 2 == 0 and gy_count >= 4
+        and gy_count & (gy_count - 1) == 0 and elem_x == 2 and nodes == NODES
+        and 2 * elem_x * ez_count == 128 and levels * cols <= 256
+        and 4 * elem_x * ez_count == 256 and levels == (gx_count * gy_count).bit_length() and (levels * cols) % 8 == 0
+    )
+
+
 def solution(mesh):
+    def body(source, geometry, disc_mask, thrust, xxt_factor, col_count):
+        run = fast_device if is_fast(mesh, source, geometry, xxt_factor) else per_device
+        return run(source, geometry, disc_mask, thrust, xxt_factor, col_count)
+
     return jax.shard_map(
-        per_device,
+        body,
         mesh=mesh,
         in_specs=(
             P(None, None, "gx", "gy", None),

time: 478 us -> 270 us (0.56)
  the two profiles are of different devices: /device:TPU:0 before, /device:TPU:26 now
where the time goes in v1:
time: 270 us; the launch traced here: 268 us
  starting transfers between devices  85 us (31%)
  waiting for transfers between devices  72.3 us (27%)
  local copies, waits for them, and re-layouts  64.2 us (24%)
  Pallas kernels  30.7 us (11%)
  blocking collectives  10.5 us (4%)
  between operations  3.37 us (1%)
    ppermute x40, waiting for transfers between devices, halo(): return (lax.ppermute(high, axes, up), lax.ppermute(low, axes, down))  53.2 us
    ppermute x40, starting transfers between devices, halo(): return (lax.ppermute(high, axes, up), lax.ppermute(low, axes, down))  37.4 us
    pallas_call x23, Pallas kernels, call(): pl.pallas_call(kernel, name=name, out_shape=[jax.ShapeDtypeStruct(s, f32)...  30.7 us
    ppermute x4, waiting for transfers between devices, fast_device(): lax.ppermute(chunks[q], axes, [(t, s) for s, t in spread(q)])  15.9 us
    ppermute x4, starting transfers between devices, fast_device(): lax.ppermute(chunks[q], axes, [(t, s) for s, t in spread(q)])  14.5 us
    ppermute x4, starting transfers between devices, fast_device(): lax.ppermute(chunk(factor, q), axes, spread(q))  14.3 us
    reshape x2, local copies, waits for them, and re-layouts, fast_device(): return by_ey.transpose(2, 1, 4, 0, 5, 3).reshape(source.shape)  13.4 us
    ppermute x4, starting transfers between devices, fast_device(): lax.ppermute(chunk(packed, q), axes, spread(q))  11.1 us
  transfers between devices with their start and end apart: 53, of which 26 were waited for; matrix products, arithmetic and copies ran while one was open for 8% of the time, Pallas kernels for 1%

profile of v1, /device:TPU:26, one launch (start us, length us, event | category | flops | bytes accessed | tf_op | source)
XLA Modules:
  0.0 268.2 jit_solution(105621432686771185)
XLA Ops:
  2.2 6.2 %reshape.116 = f32[8,8,2,4,32,8]{5,4,1,3,2,0:T(8,128)} reshape(f32[8,8,2,4,256]{4,1,3,2,0:T(8,128)S(1)} %copy.32) | data formatting | bytes 1048576 | tf_op jit(solution)/shard_map/reshape | solution.py:754
  8.4 6.8 %copy.33 = f32[4,8,8,8,2,32]{5,4,3,2,1,0:T(2,128)S(1)} copy(f32[4,8,8,8,2,32]{3,5,1,0,4,2:T(8,128)} %bitcast.47) | data formatting | bytes 1048576 | tf_op jit(solution)/shard_map/transpose | solution.py:755
  15.2 2.7 reshape.117
  18.4 2.6 collective-permute-start
  21.0 3.5 %collective-permute-start.1 = (f32[72,512]{1,0:T(8,128)S(1)}, f32[72,512]{1,0:T(8,128)S(1)}, u32[]{:S(2)}, u32[]{:S(2)}) collective-permute-start(f32[72,512]{1,0:T(8,128)S(1)} %get-tuple-element.193), channel_id=1, source_target_pairs={{0,1},{1,11},{2,5},{3,15},{4,23},{5,29},{6,19},{7,25},{8,8},{9,2},... | collective-permute-start | bytes 442376 | tf_op jit(solution)/shard_map/ppermute | solution.py:764
  24.5 3.9 %collective-permute-start.2 = (f32[72,512]{1,0:T(8,128)S(1)}, f32[72,512]{1,0:T(8,128)S(1)}, u32[]{:S(2)}, u32[]{:S(2)}) collective-permute-start(f32[72,512]{1,0:T(8,128)S(1)} %get-tuple-element.192), channel_id=1, source_target_pairs={{0,8},{1,2},{2,12},{3,6},{4,30},{5,20},{6,26},{7,16},{8,9},{9,3},{... | collective-permute-start | bytes 442376 | tf_op jit(solution)/shard_map/ppermute | solution.py:764
  32.3 4.4 %reshape.119 = f32[192,8,4,64]{3,2,1,0:T(4,128)} reshape(f32[6,32,2048]{2,1,0:T(8,128)} %param.23) | data formatting | bytes 3145728 | tf_op jit(solution)/shard_map/reshape | solution.py:766
  36.7 4.7 %copy.36 = f32[4,192,8,64]{1,3,2,0:T(8,128)} copy(f32[4,192,8,64]{3,0,2,1:T(4,128)} %bitcast.48) | data formatting | bytes 3145728 | tf_op jit(solution)/shard_map/transpose | solution.py:767
  43.9 3.0 %constant_dynamic-slice_fusion.1 = (f32[1,192,512]{1,2,0:T(8,128)}, f32[1,192,512]{1,2,0:T(8,128)}, f32[1,192,512]{1,2,0:T(8,128)}, f32[1,192,512]{1,2,0:T(8,128)}) fusion(f32[4,192,512]{1,2,0:T(8,128)} %bitcast.50, s32[]{:T(128)S(6)} %select_n.33, s32[]{:T(128)S(6)} %select_n.32, s32[]{:T(128)S(6)} %select_n.31, s32[]{:T(128)S(6)} %select_n.30), kind=kLoop, calls=%fused_computation.26 | loop fusion | bytes 3145744 | tf_op jit(solution)/shard_map/jit(dynamic_index_in_dim)/dynamic_slice | solution.py:751
  46.9 2.0 copy.37
  52.4 6.1 %collective-permute-start.14 = (f32[192,512]{1,0:T(8,128)}, f32[192,512]{1,0:T(8,128)S(1)}, u32[]{:S(2)}, u32[]{:S(2)}) collective-permute-start(f32[192,512]{1,0:T(8,128)} %bitcast.12), channel_id=1, source_target_pairs={{0,0},{1,10},{2,4},{3,14},{4,22},{5,28},{6,18},{7,24},{8,1},{9,11}... | collective-permute-start | bytes 1179656 | tf_op jit(solution)/shard_map/ppermute | solution.py:768
  58.6 2.0 copy.38
  60.5 2.9 %collective-permute-start.15 = (f32[192,512]{1,0:T(8,128)}, f32[192,512]{1,0:T(8,128)S(1)}, u32[]{:S(2)}, u32[]{:S(2)}) collective-permute-start(f32[192,512]{1,0:T(8,128)} %bitcast.53), channel_id=1, source_target_pairs={{0,1},{1,11},{2,5},{3,15},{4,23},{5,29},{6,19},{7,25},{8,8},{9,2},... | collective-permute-start | bytes 1179656 | tf_op jit(solution)/shard_map/ppermute | solution.py:768
  63.4 2.0 copy.39
  65.4 4.5 %collective-permute-start.16 = (f32[192,512]{1,0:T(8,128)}, f32[192,512]{1,0:T(8,128)}, u32[]{:S(2)}, u32[]{:S(2)}) collective-permute-start(f32[192,512]{1,0:T(8,128)} %bitcast.54), channel_id=1, source_target_pairs={{0,8},{1,2},{2,12},{3,6},{4,30},{5,20},{6,26},{7,16},{8,9},{9,3},{... | collective-permute-start | bytes 1179656 | tf_op jit(solution)/shard_map/ppermute | solution.py:768
  69.9 2.0 copy.40
  74.8 5.8 %collective-permute-done.8.refs_1_ = f32[64,256]{1,0:T(8,128)S(1)} collective-permute-done((f32[64,256]{1,0:T(8,128)S(1)}, f32[64,256]{1,0:T(8,128)S(1)}, u32[]{:S(2)}, u32[]{:S(2)}) %collective-permute-start.8) | collective-permute-done | bytes 65568 | tf_op jit(solution)/shard_map/ppermute | solution.py:748
  80.6 11.5 %collective-permute-done.9.refs_2_ = f32[64,256]{1,0:T(8,128)S(1)} collective-permute-done((f32[64,256]{1,0:T(8,128)S(1)}, f32[64,256]{1,0:T(8,128)S(1)}, u32[]{:S(2)}, u32[]{:S(2)}) %collective-permute-start.9) | collective-permute-done | bytes 65568 | tf_op jit(solution)/shard_map/ppermute | solution.py:748
  93.9 3.9 %collective-permute-done.10.refs_1_ = f32[64,256]{1,0:T(8,128)S(1)} collective-permute-done((f32[64,256]{1,0:T(8,128)S(1)}, f32[64,256]{1,0:T(8,128)S(1)}, u32[]{:S(2)}, u32[]{:S(2)}) %collective-permute-start.10) | collective-permute-done | bytes 65568 | tf_op jit(solution)/shard_map/ppermute | solution.py:748
  97.7 1.9 collective-permute-done.11.refs_2_
  102.8 7.0 %collective-permute-start.13 = (f32[64,256]{1,0:T(8,128)}, f32[64,256]{1,0:T(8,128)}, u32[]{:S(2)}, u32[]{:S(2)}) collective-permute-start(f32[64,256]{1,0:T(8,128)} %get-tuple-element.115), channel_id=1, source_target_pairs={{1,0},{8,1},{9,8},{10,9},{11,10},{2,11},{3,2},{4,3},{5,4},{12,5},{... | collective-permute-start | bytes 196616 | tf_op jit(solution)/shard_map/ppermute | solution.py:748
  114.1 3.0 %restrict.2 = (f32[512,256]{1,0:T(8,128)S(1)}, f32[8,128]{1,0:T(8,128)S(1)}) custom-call(s32[1]{0:T(128)} %bitcast.1.refs_0_, f32[1024,128]{1,0:T(8,128)S(1)} %copy-done.13, f32[64,256]{1,0:T(8,128)} %collective-permute-done.12.refs_2_, f32[64,256]{1,0:T(8,128)} %collective-permute-done.13.refs_3_, f32[512,256]{1,0:T(8,128)S(1)} %copy-done.11, ...), custom_call_target="tpu_custom_call" | custom-call | tf_op jit(solution)/shard_map/restrict/pallas_call | solution.py:705
  118.6 7.7 %all-to-all-start = ((f32[32,8,128]{2,1,0:T(8,128)}), f32[32,8,128]{2,1,0:T(8,128)}, u32[]{:S(2)}, u32[]{:S(2)}) async-start(f32[32,8,128]{2,1,0:T(8,128)} %broadcast_in_dim.40), calls=%async_computation | async-start | bytes 262144 | tf_op jit(solution)/shard_map/all_to_all | solution.py:831
  128.1 3.1 %all-to-all-done.refs_1_ = f32[32,8,128]{2,1,0:T(8,128)} async-done(((f32[32,8,128]{2,1,0:T(8,128)}), f32[32,8,128]{2,1,0:T(8,128)}, u32[]{:S(2)}, u32[]{:S(2)}) %all-to-all-start) | async-done | bytes 131104 | tf_op jit(solution)/shard_map/all_to_all | solution.py:831
  132.9 2.8 %prolong.2 = (f32[1024,128]{1,0:T(8,128)S(1)}, f32[64,256]{1,0:T(8,128)S(1)}, f32[64,256]{1,0:T(8,128)S(1)}) custom-call(s32[1]{0:T(128)} %bitcast.1.refs_0_, f32[32,8,128]{2,1,0:T(8,128)} %all-to-all-done.refs_1_, f32[32,8,128]{2,1,0:T(8,128)S(1)} %tile.9.refs_2_, f32[8,128]{1,0:T(8,128)S(1)} %get-tuple-element.118.refs_3_, f32[128,128]{1,0:T(8,128)S(1)} %copy-done.17, ...), custom_call_target="tpu_custom_call" | custom-call | tf_op jit(solution)/shard_map/prolong/pallas_call | solution.py:705
  137.6 1.9 collective-permute-done.18.refs_1_
  142.3 1.9 collective-permute-done.20.refs_1_
  147.1 1.9 collective-permute-done.22.refs_1_
  151.9 1.9 collective-permute-done.24.refs_1_
  156.6 1.9 collective-permute-done.26.refs_1_
  161.4 1.9 collective-permute-done.28.refs_1_
  166.2 1.9 collective-permute-done.30.refs_1_
  175.8 1.9 collective-permute-done.34.refs_1_
  182.5 2.9 %restrict.3 = (f32[512,256]{1,0:T(8,128)S(1)}, f32[8,128]{1,0:T(8,128)S(1)}) custom-call(s32[1]{0:T(128)} %bitcast.1.refs_0_, f32[1024,128]{1,0:T(8,128)S(1)} %get-tuple-element.157.refs_1_, f32[64,256]{1,0:T(8,128)S(1)} %collective-permute-done.36.refs_2_, f32[64,256]{1,0:T(8,128)S(1)} %collective-permute-done.37.refs_3_, ...), custom_call_target="tpu_custom_call" | custom-call | tf_op jit(solution)/shard_map/restrict/pallas_call | solution.py:705
  185.4 10.5 %all_to_all.10.refs_1_ = f32[32,8,128]{2,1,0:T(8,128)S(1)} all-to-all(f32[32,8,128]{2,1,0:T(8,128)S(1)} %broadcast_in_dim.41), channel_id=1, replica_groups=mesh['gx'=4,'gy'=8] {'gx','gy'}, dimensions={0} | all-to-all | bytes 262144 | tf_op jit(solution)/shard_map/all_to_all | solution.py:831
  195.9 2.7 %prolong.3 = (f32[1024,128]{1,0:T(8,128)S(1)}, f32[64,256]{1,0:T(8,128)S(1)}, f32[64,256]{1,0:T(8,128)S(1)}) custom-call(s32[1]{0:T(128)} %bitcast.1.refs_0_, f32[32,8,128]{2,1,0:T(8,128)S(1)} %all_to_all.10.refs_1_, f32[32,8,128]{2,1,0:T(8,128)S(1)} %tile.9.refs_2_, f32[8,128]{1,0:T(8,128)S(1)} %get-tuple-element.118.refs_3_, f32[128,128]{1,0:T(8,128)S(1)} %copy-done.18, ...), custom_call_target="tpu_custom_call" | custom-call | tf_op jit(solution)/shard_map/prolong/pallas_call | solution.py:705
  200.4 1.9 collective-permute-done.38.refs_1_
  205.2 1.9 collective-permute-done.40.refs_1_
  214.8 1.9 collective-permute-done.44.refs_1_
  220.0 1.9 collective-permute-done.46.refs_2_
  222.4 4.6 %collective-permute-start.48 = (f32[64,512]{1,0:T(8,128)S(1)}, f32[64,512]{1,0:T(8,128)S(1)}, u32[]{:S(2)}, u32[]{:S(2)}) collective-permute-start(f32[64,512]{1,0:T(8,128)S(1)} %get-tuple-element.183), channel_id=1, source_target_pairs={{0,0},{10,1},{4,2},{14,3},{22,4},{28,5},{18,6},{24,7},{1,8},{11,9}... | collective-permute-start | bytes 393224 | tf_op jit(solution)/shard_map/ppermute | solution.py:854
  227.1 2.5 collective-permute-start.49
  229.6 5.3 %collective-permute-start.50 = (f32[64,512]{1,0:T(8,128)S(1)}, f32[64,512]{1,0:T(8,128)S(1)}, u32[]{:S(2)}, u32[]{:S(2)}) collective-permute-start(f32[64,512]{1,0:T(8,128)S(1)} %get-tuple-element.185), channel_id=1, source_target_pairs={{8,0},{2,1},{12,2},{6,3},{30,4},{20,5},{26,6},{16,7},{9,8},{3,9},{... | collective-permute-start | bytes 393224 | tf_op jit(solution)/shard_map/ppermute | solution.py:854
  234.9 2.0 collective-permute-start.51
  238.2 8.4 %collective-permute-done.49 = f32[64,512]{1,0:T(8,128)S(1)} collective-permute-done((f32[64,512]{1,0:T(8,128)S(1)}, f32[64,512]{1,0:T(8,128)S(1)}, u32[]{:S(2)}, u32[]{:S(2)}) %collective-permute-start.49) | collective-permute-done | bytes 131104 | tf_op jit(solution)/shard_map/ppermute | solution.py:854
  247.8 5.1 %collective-permute-done.51 = f32[64,512]{1,0:T(8,128)S(1)} collective-permute-done((f32[64,512]{1,0:T(8,128)S(1)}, f32[64,512]{1,0:T(8,128)S(1)}, u32[]{:S(2)}, u32[]{:S(2)}) %collective-permute-start.51) | collective-permute-done | bytes 131104 | tf_op jit(solution)/shard_map/ppermute | solution.py:854
  254.8 6.0 %copy.44 = f32[8,8,2,4,32,8]{5,4,3,2,1,0:T(8,128)} copy(f32[8,8,2,4,32,8]{4,2,5,0,1,3:T(2,128)S(1)} %bitcast.49) | data formatting | bytes 1048576 | tf_op jit(solution)/shard_map/reshape | solution.py:860
  260.8 7.4 %reshape.125 = f32[8,8,2,4,256]{4,3,2,1,0:T(4,128)} reshape(f32[8,8,2,4,32,8]{5,4,3,2,1,0:T(8,128)} %copy.44) | data formatting | bytes 1048576 | tf_op jit(solution)/shard_map/reshape | solution.py:860
  (188 shorter events, 79.1 us)
Async XLA Ops:
  18.4 22.9 %collective-permute-start = (f32[72,512]{1,0:T(8,128)S(1)}, f32[72,512]{1,0:T(8,128)S(1)}, u32[]{:S(2)}, u32[]{:S(2)}) collective-permute-start(f32[72,512]{1,0:T(8,128)S(1)} %get-tuple-element.194), channel_id=1, source_target_pairs={{0,0},{1,10},{2,4},{3,14},{4,22},{5,28},{6,18},{7,24},{8,1},{9,11}... | collective-permute-start | bytes 442376 | tf_op jit(solution)/shard_map/ppermute | solution.py:764
  21.0 20.3 %collective-permute-start.1 = (f32[72,512]{1,0:T(8,128)S(1)}, f32[72,512]{1,0:T(8,128)S(1)}, u32[]{:S(2)}, u32[]{:S(2)}) collective-permute-start(f32[72,512]{1,0:T(8,128)S(1)} %get-tuple-element.193), channel_id=1, source_target_pairs={{0,1},{1,11},{2,5},{3,15},{4,23},{5,29},{6,19},{7,25},{8,8},{9,2},... | collective-permute-start | bytes 442376 | tf_op jit(solution)/shard_map/ppermute | solution.py:764
  24.5 16.8 %collective-permute-start.2 = (f32[72,512]{1,0:T(8,128)S(1)}, f32[72,512]{1,0:T(8,128)S(1)}, u32[]{:S(2)}, u32[]{:S(2)}) collective-permute-start(f32[72,512]{1,0:T(8,128)S(1)} %get-tuple-element.192), channel_id=1, source_target_pairs={{0,8},{1,2},{2,12},{3,6},{4,30},{5,20},{6,26},{7,16},{8,9},{9,3},{... | collective-permute-start | bytes 442376 | tf_op jit(solution)/shard_map/ppermute | solution.py:764
  28.4 12.9 %collective-permute-start.3 = (f32[72,512]{1,0:T(8,128)S(1)}, f32[72,512]{1,0:T(8,128)S(1)}, u32[]{:S(2)}, u32[]{:S(2)}) collective-permute-start(f32[72,512]{1,0:T(8,128)S(1)} %get-tuple-element.191), channel_id=1, source_target_pairs={{0,9},{1,3},{2,13},{3,7},{4,31},{5,21},{6,27},{7,17},{8,0},{9,10},... | collective-permute-start | bytes 442376 | tf_op jit(solution)/shard_map/ppermute | solution.py:764
  42.1 6.8 %collective-permute-start.4 = (f32[64,256]{1,0:T(8,128)S(1)}, f32[64,256]{1,0:T(8,128)S(1)}, u32[]{:S(2)}, u32[]{:S(2)}) collective-permute-start(f32[64,256]{1,0:T(8,128)S(1)} %get-tuple-element.97), channel_id=1, source_target_pairs={{0,1},{1,8},{8,9},{9,10},{10,11},{11,2},{2,3},{3,4},{4,5},{5,12},{... | collective-permute-start | bytes 196616 | tf_op jit(solution)/shard_map/ppermute | solution.py:748
  42.6 6.3 %collective-permute-start.5 = (f32[64,256]{1,0:T(8,128)S(1)}, f32[64,256]{1,0:T(8,128)S(1)}, u32[]{:S(2)}, u32[]{:S(2)}) collective-permute-start(f32[64,256]{1,0:T(8,128)S(1)} %get-tuple-element.98), channel_id=1, source_target_pairs={{1,0},{8,1},{9,8},{10,9},{11,10},{2,11},{3,2},{4,3},{5,4},{12,5},{... | collective-permute-start | bytes 196616 | tf_op jit(solution)/shard_map/ppermute | solution.py:748
  52.1 19.8 %collective-permute-start.6 = (f32[64,256]{1,0:T(8,128)}, f32[64,256]{1,0:T(8,128)S(1)}, u32[]{:S(2)}, u32[]{:S(2)}) collective-permute-start(f32[64,256]{1,0:T(8,128)} %get-tuple-element.101), channel_id=1, source_target_pairs={{0,1},{1,8},{8,9},{9,10},{10,11},{11,2},{2,3},{3,4},{4,5},{5,12},{... | collective-permute-start | bytes 196616 | tf_op jit(solution)/shard_map/ppermute | solution.py:748
  52.4 50.4 %collective-permute-start.14 = (f32[192,512]{1,0:T(8,128)}, f32[192,512]{1,0:T(8,128)S(1)}, u32[]{:S(2)}, u32[]{:S(2)}) collective-permute-start(f32[192,512]{1,0:T(8,128)} %bitcast.12), channel_id=1, source_target_pairs={{0,0},{1,10},{2,4},{3,14},{4,22},{5,28},{6,18},{7,24},{8,1},{9,11}... | collective-permute-start | bytes 1179656 | tf_op jit(solution)/shard_map/ppermute | solution.py:768
  58.5 14.3 %collective-permute-start.7 = (f32[64,256]{1,0:T(8,128)}, f32[64,256]{1,0:T(8,128)S(1)}, u32[]{:S(2)}, u32[]{:S(2)}) collective-permute-start(f32[64,256]{1,0:T(8,128)} %get-tuple-element.102), channel_id=1, source_target_pairs={{1,0},{8,1},{9,8},{10,9},{11,10},{2,11},{3,2},{4,3},{5,4},{12,5},{... | collective-permute-start | bytes 196616 | tf_op jit(solution)/shard_map/ppermute | solution.py:748
  60.5 50.0 %collective-permute-start.15 = (f32[192,512]{1,0:T(8,128)}, f32[192,512]{1,0:T(8,128)S(1)}, u32[]{:S(2)}, u32[]{:S(2)}) collective-permute-start(f32[192,512]{1,0:T(8,128)} %bitcast.53), channel_id=1, source_target_pairs={{0,1},{1,11},{2,5},{3,15},{4,23},{5,29},{6,19},{7,25},{8,8},{9,2},... | collective-permute-start | bytes 1179656 | tf_op jit(solution)/shard_map/ppermute | solution.py:768
  65.4 45.2 %collective-permute-start.16 = (f32[192,512]{1,0:T(8,128)}, f32[192,512]{1,0:T(8,128)}, u32[]{:S(2)}, u32[]{:S(2)}) collective-permute-start(f32[192,512]{1,0:T(8,128)} %bitcast.54), channel_id=1, source_target_pairs={{0,8},{1,2},{2,12},{3,6},{4,30},{5,20},{6,26},{7,16},{8,9},{9,3},{... | collective-permute-start | bytes 1179656 | tf_op jit(solution)/shard_map/ppermute | solution.py:768
  71.8 38.7 %collective-permute-start.17 = (f32[192,512]{1,0:T(8,128)}, f32[192,512]{1,0:T(8,128)}, u32[]{:S(2)}, u32[]{:S(2)}) collective-permute-start(f32[192,512]{1,0:T(8,128)} %bitcast.55), channel_id=1, source_target_pairs={{0,9},{1,3},{2,13},{3,7},{4,31},{5,21},{6,27},{7,17},{8,0},{9,10},... | collective-permute-start | bytes 1179656 | tf_op jit(solution)/shard_map/ppermute | solution.py:768
  74.8 5.8 %collective-permute-start.8 = (f32[64,256]{1,0:T(8,128)S(1)}, f32[64,256]{1,0:T(8,128)S(1)}, u32[]{:S(2)}, u32[]{:S(2)}) collective-permute-start(f32[64,256]{1,0:T(8,128)S(1)} %get-tuple-element.105), channel_id=1, source_target_pairs={{0,1},{1,8},{8,9},{9,10},{10,11},{11,2},{2,3},{3,4},{4,5},{5,12},{... | collective-permute-start | bytes 196616 | tf_op jit(solution)/shard_map/ppermute | solution.py:748
  80.6 11.5 %collective-permute-start.9 = (f32[64,256]{1,0:T(8,128)S(1)}, f32[64,256]{1,0:T(8,128)S(1)}, u32[]{:S(2)}, u32[]{:S(2)}) collective-permute-start(f32[64,256]{1,0:T(8,128)S(1)} %get-tuple-element.106), channel_id=1, source_target_pairs={{1,0},{8,1},{9,8},{10,9},{11,10},{2,11},{3,2},{4,3},{5,4},{12,5},{... | collective-permute-start | bytes 196616 | tf_op jit(solution)/shard_map/ppermute | solution.py:748
  93.9 3.9 %collective-permute-start.10 = (f32[64,256]{1,0:T(8,128)S(1)}, f32[64,256]{1,0:T(8,128)S(1)}, u32[]{:S(2)}, u32[]{:S(2)}) collective-permute-start(f32[64,256]{1,0:T(8,128)S(1)} %get-tuple-element.109), channel_id=1, source_target_pairs={{0,1},{1,8},{8,9},{9,10},{10,11},{11,2},{2,3},{3,4},{4,5},{5,12},{... | collective-permute-start | bytes 196616 | tf_op jit(solution)/shard_map/ppermute | solution.py:748
  102.8 9.0 %collective-permute-start.12 = (f32[64,256]{1,0:T(8,128)}, f32[64,256]{1,0:T(8,128)}, u32[]{:S(2)}, u32[]{:S(2)}) collective-permute-start(f32[64,256]{1,0:T(8,128)} %get-tuple-element.114), channel_id=1, source_target_pairs={{0,1},{1,8},{8,9},{9,10},{10,11},{11,2},{2,3},{3,4},{4,5},{5,12},{... | collective-permute-start | bytes 196616 | tf_op jit(solution)/shard_map/ppermute | solution.py:748
  102.8 9.2 %collective-permute-start.13 = (f32[64,256]{1,0:T(8,128)}, f32[64,256]{1,0:T(8,128)}, u32[]{:S(2)}, u32[]{:S(2)}) collective-permute-start(f32[64,256]{1,0:T(8,128)} %get-tuple-element.115), channel_id=1, source_target_pairs={{1,0},{8,1},{9,8},{10,9},{11,10},{2,11},{3,2},{4,3},{5,4},{12,5},{... | collective-permute-start | bytes 196616 | tf_op jit(solution)/shard_map/ppermute | solution.py:748
  118.6 12.5 %all-to-all-start = ((f32[32,8,128]{2,1,0:T(8,128)}), f32[32,8,128]{2,1,0:T(8,128)}, u32[]{:S(2)}, u32[]{:S(2)}) async-start(f32[32,8,128]{2,1,0:T(8,128)} %broadcast_in_dim.40), calls=%async_computation | async-start | bytes 262144 | tf_op jit(solution)/shard_map/all_to_all | solution.py:831
  135.8 3.7 %collective-permute-start.18 = (f32[64,256]{1,0:T(8,128)S(1)}, f32[64,256]{1,0:T(8,128)S(1)}, u32[]{:S(2)}, u32[]{:S(2)}) collective-permute-start(f32[64,256]{1,0:T(8,128)S(1)} %get-tuple-element.120), channel_id=1, source_target_pairs={{0,1},{1,8},{8,9},{9,10},{10,11},{11,2},{2,3},{3,4},{4,5},{5,12},{... | collective-permute-start | bytes 196616 | tf_op jit(solution)/shard_map/ppermute | solution.py:748
  136.1 3.4 %collective-permute-start.19 = (f32[64,256]{1,0:T(8,128)S(1)}, f32[64,256]{1,0:T(8,128)S(1)}, u32[]{:S(2)}, u32[]{:S(2)}) collective-permute-start(f32[64,256]{1,0:T(8,128)S(1)} %get-tuple-element.121), channel_id=1, source_target_pairs={{1,0},{8,1},{9,8},{10,9},{11,10},{2,11},{3,2},{4,3},{5,4},{12,5},{... | collective-permute-start | bytes 196616 | tf_op jit(solution)/shard_map/ppermute | solution.py:748
  140.5 3.7 %collective-permute-start.20 = (f32[64,256]{1,0:T(8,128)S(1)}, f32[64,256]{1,0:T(8,128)S(1)}, u32[]{:S(2)}, u32[]{:S(2)}) collective-permute-start(f32[64,256]{1,0:T(8,128)S(1)} %get-tuple-element.124), channel_id=1, source_target_pairs={{0,1},{1,8},{8,9},{9,10},{10,11},{11,2},{2,3},{3,4},{4,5},{5,12},{... | collective-permute-start | bytes 196616 | tf_op jit(solution)/shard_map/ppermute | solution.py:748
  141.8 2.4 collective-permute-start.21
  145.2 3.8 %collective-permute-start.22 = (f32[64,256]{1,0:T(8,128)S(1)}, f32[64,256]{1,0:T(8,128)S(1)}, u32[]{:S(2)}, u32[]{:S(2)}) collective-permute-start(f32[64,256]{1,0:T(8,128)S(1)} %get-tuple-element.128), channel_id=1, source_target_pairs={{0,1},{1,8},{8,9},{9,10},{10,11},{11,2},{2,3},{3,4},{4,5},{5,12},{... | collective-permute-start | bytes 196616 | tf_op jit(solution)/shard_map/ppermute | solution.py:748
  146.5 2.4 collective-permute-start.23
  150.0 3.8 %collective-permute-start.24 = (f32[64,256]{1,0:T(8,128)S(1)}, f32[64,256]{1,0:T(8,128)S(1)}, u32[]{:S(2)}, u32[]{:S(2)}) collective-permute-start(f32[64,256]{1,0:T(8,128)S(1)} %get-tuple-element.132), channel_id=1, source_target_pairs={{0,1},{1,8},{8,9},{9,10},{10,11},{11,2},{2,3},{3,4},{4,5},{5,12},{... | collective-permute-start | bytes 196616 | tf_op jit(solution)/shard_map/ppermute | solution.py:748
  151.3 2.4 collective-permute-start.25
  154.7 3.8 %collective-permute-start.26 = (f32[64,256]{1,0:T(8,128)S(1)}, f32[64,256]{1,0:T(8,128)S(1)}, u32[]{:S(2)}, u32[]{:S(2)}) collective-permute-start(f32[64,256]{1,0:T(8,128)S(1)} %get-tuple-element.136), channel_id=1, source_target_pairs={{0,1},{1,8},{8,9},{9,10},{10,11},{11,2},{2,3},{3,4},{4,5},{5,12},{... | collective-permute-start | bytes 196616 | tf_op jit(solution)/shard_map/ppermute | solution.py:748
  156.1 2.4 collective-permute-start.27
  159.5 3.8 %collective-permute-start.28 = (f32[64,256]{1,0:T(8,128)S(1)}, f32[64,256]{1,0:T(8,128)S(1)}, u32[]{:S(2)}, u32[]{:S(2)}) collective-permute-start(f32[64,256]{1,0:T(8,128)S(1)} %get-tuple-element.141), channel_id=1, source_target_pairs={{0,1},{1,8},{8,9},{9,10},{10,11},{11,2},{2,3},{3,4},{4,5},{5,12},{... | collective-permute-start | bytes 196616 | tf_op jit(solution)/shard_map/ppermute | solution.py:748
  160.9 2.4 collective-permute-start.29
  164.3 3.8 %collective-permute-start.30 = (f32[64,256]{1,0:T(8,128)S(1)}, f32[64,256]{1,0:T(8,128)S(1)}, u32[]{:S(2)}, u32[]{:S(2)}) collective-permute-start(f32[64,256]{1,0:T(8,128)S(1)} %get-tuple-element.145), channel_id=1, source_target_pairs={{0,1},{1,8},{8,9},{9,10},{10,11},{11,2},{2,3},{3,4},{4,5},{5,12},{... | collective-permute-start | bytes 196616 | tf_op jit(solution)/shard_map/ppermute | solution.py:748
  165.6 2.4 collective-permute-start.31
  169.1 3.8 %collective-permute-start.32 = (f32[64,256]{1,0:T(8,128)S(1)}, f32[64,256]{1,0:T(8,128)S(1)}, u32[]{:S(2)}, u32[]{:S(2)}) collective-permute-start(f32[64,256]{1,0:T(8,128)S(1)} %get-tuple-element.149), channel_id=1, source_target_pairs={{0,1},{1,8},{8,9},{9,10},{10,11},{11,2},{2,3},{3,4},{4,5},{5,12},{... | collective-permute-start | bytes 196616 | tf_op jit(solution)/shard_map/ppermute | solution.py:748
  173.9 3.8 %collective-permute-start.34 = (f32[64,256]{1,0:T(8,128)S(1)}, f32[64,256]{1,0:T(8,128)S(1)}, u32[]{:S(2)}, u32[]{:S(2)}) collective-permute-start(f32[64,256]{1,0:T(8,128)S(1)} %get-tuple-element.153), channel_id=1, source_target_pairs={{0,1},{1,8},{8,9},{9,10},{10,11},{11,2},{2,3},{3,4},{4,5},{5,12},{... | collective-permute-start | bytes 196616 | tf_op jit(solution)/shard_map/ppermute | solution.py:748
  178.7 3.8 %collective-permute-start.36 = (f32[64,256]{1,0:T(8,128)S(1)}, f32[64,256]{1,0:T(8,128)S(1)}, u32[]{:S(2)}, u32[]{:S(2)}) collective-permute-start(f32[64,256]{1,0:T(8,128)S(1)} %get-tuple-element.158), channel_id=1, source_target_pairs={{0,1},{1,8},{8,9},{9,10},{10,11},{11,2},{2,3},{3,4},{4,5},{5,12},{... | collective-permute-start | bytes 196616 | tf_op jit(solution)/shard_map/ppermute | solution.py:748
  198.6 3.7 %collective-permute-start.38 = (f32[64,256]{1,0:T(8,128)S(1)}, f32[64,256]{1,0:T(8,128)S(1)}, u32[]{:S(2)}, u32[]{:S(2)}) collective-permute-start(f32[64,256]{1,0:T(8,128)S(1)} %get-tuple-element.163), channel_id=1, source_target_pairs={{0,1},{1,8},{8,9},{9,10},{10,11},{11,2},{2,3},{3,4},{4,5},{5,12},{... | collective-permute-start | bytes 196616 | tf_op jit(solution)/shard_map/ppermute | solution.py:748
  199.0 3.4 %collective-permute-start.39 = (f32[64,256]{1,0:T(8,128)S(1)}, f32[64,256]{1,0:T(8,128)S(1)}, u32[]{:S(2)}, u32[]{:S(2)}) collective-permute-start(f32[64,256]{1,0:T(8,128)S(1)} %get-tuple-element.164), channel_id=1, source_target_pairs={{1,0},{8,1},{9,8},{10,9},{11,10},{2,11},{3,2},{4,3},{5,4},{12,5},{... | collective-permute-start | bytes 196616 | tf_op jit(solution)/shard_map/ppermute | solution.py:748
  203.3 3.7 %collective-permute-start.40 = (f32[64,256]{1,0:T(8,128)S(1)}, f32[64,256]{1,0:T(8,128)S(1)}, u32[]{:S(2)}, u32[]{:S(2)}) collective-permute-start(f32[64,256]{1,0:T(8,128)S(1)} %get-tuple-element.167), channel_id=1, source_target_pairs={{0,1},{1,8},{8,9},{9,10},{10,11},{11,2},{2,3},{3,4},{4,5},{5,12},{... | collective-permute-start | bytes 196616 | tf_op jit(solution)/shard_map/ppermute | solution.py:748
  204.7 2.5 collective-permute-start.41
  208.1 3.8 %collective-permute-start.42 = (f32[64,256]{1,0:T(8,128)S(1)}, f32[64,256]{1,0:T(8,128)S(1)}, u32[]{:S(2)}, u32[]{:S(2)}) collective-permute-start(f32[64,256]{1,0:T(8,128)S(1)} %get-tuple-element.171), channel_id=1, source_target_pairs={{0,1},{1,8},{8,9},{9,10},{10,11},{11,2},{2,3},{3,4},{4,5},{5,12},{... | collective-permute-start | bytes 196616 | tf_op jit(solution)/shard_map/ppermute | solution.py:748
  209.4 2.5 collective-permute-start.43
  212.9 3.8 %collective-permute-start.44 = (f32[64,256]{1,0:T(8,128)S(1)}, f32[64,256]{1,0:T(8,128)S(1)}, u32[]{:S(2)}, u32[]{:S(2)}) collective-permute-start(f32[64,256]{1,0:T(8,128)S(1)} %get-tuple-element.175), channel_id=1, source_target_pairs={{0,1},{1,8},{8,9},{9,10},{10,11},{11,2},{2,3},{3,4},{4,5},{5,12},{... | collective-permute-start | bytes 196616 | tf_op jit(solution)/shard_map/ppermute | solution.py:748
  214.2 2.5 collective-permute-start.45
  218.2 3.7 %collective-permute-start.46 = (f32[64,256]{1,0:T(8,128)S(1)}, f32[64,256]{1,0:T(8,128)S(1)}, u32[]{:S(2)}, u32[]{:S(2)}) collective-permute-start(f32[64,256]{1,0:T(8,128)S(1)} %get-tuple-element.179), channel_id=1, source_target_pairs={{0,1},{1,8},{8,9},{9,10},{10,11},{11,2},{2,3},{3,4},{4,5},{5,12},{... | collective-permute-start | bytes 196616 | tf_op jit(solution)/shard_map/ppermute | solution.py:748
  222.4 15.7 %collective-permute-start.48 = (f32[64,512]{1,0:T(8,128)S(1)}, f32[64,512]{1,0:T(8,128)S(1)}, u32[]{:S(2)}, u32[]{:S(2)}) collective-permute-start(f32[64,512]{1,0:T(8,128)S(1)} %get-tuple-element.183), channel_id=1, source_target_pairs={{0,0},{10,1},{4,2},{14,3},{22,4},{28,5},{18,6},{24,7},{1,8},{11,9}... | collective-permute-start | bytes 393224 | tf_op jit(solution)/shard_map/ppermute | solution.py:854
  227.1 19.4 %collective-permute-start.49 = (f32[64,512]{1,0:T(8,128)S(1)}, f32[64,512]{1,0:T(8,128)S(1)}, u32[]{:S(2)}, u32[]{:S(2)}) collective-permute-start(f32[64,512]{1,0:T(8,128)S(1)} %get-tuple-element.184), channel_id=1, source_target_pairs={{1,0},{11,1},{5,2},{15,3},{23,4},{29,5},{19,6},{25,7},{8,8},{2,9},... | collective-permute-start | bytes 393224 | tf_op jit(solution)/shard_map/ppermute | solution.py:854
  229.6 18.2 %collective-permute-start.50 = (f32[64,512]{1,0:T(8,128)S(1)}, f32[64,512]{1,0:T(8,128)S(1)}, u32[]{:S(2)}, u32[]{:S(2)}) collective-permute-start(f32[64,512]{1,0:T(8,128)S(1)} %get-tuple-element.185), channel_id=1, source_target_pairs={{8,0},{2,1},{12,2},{6,3},{30,4},{20,5},{26,6},{16,7},{9,8},{3,9},{... | collective-permute-start | bytes 393224 | tf_op jit(solution)/shard_map/ppermute | solution.py:854
  234.9 18.0 %collective-permute-start.51 = (f32[64,512]{1,0:T(8,128)S(1)}, f32[64,512]{1,0:T(8,128)S(1)}, u32[]{:S(2)}, u32[]{:S(2)}) collective-permute-start(f32[64,512]{1,0:T(8,128)S(1)} %get-tuple-element.186), channel_id=1, source_target_pairs={{9,0},{3,1},{13,2},{7,3},{31,4},{21,5},{27,6},{17,7},{0,8},{10,9},... | collective-permute-start | bytes 393224 | tf_op jit(solution)/shard_map/ppermute | solution.py:854
  (36 other events, 263.8 us)

commit v2 on v1

--- a/solution.py
+++ b/solution.py
@@ -1,4 +1,5 @@
 import functools
+import itertools
 import math
 
 import jax
@@ -351,16 +352,49 @@
 bf16 = jnp.bfloat16
 
 
-def device_ring(gx_count, gy_count):
+@functools.lru_cache(maxsize=None)
+def placement(gx_count, gy_count):
     layers = gy_count // 2
-    chips = []
-    for z in range(layers):
-        pair = [(0, 0), (0, 1)]
-        chips += [(y, x, z) for y, x in (pair if z % 2 == 0 else pair[::-1])]
-    for k, z in enumerate(reversed(range(layers))):
-        pair = [(1, 0), (1, 1)] if layers % 2 == 0 else [(1, 1), (1, 0)]
-        chips += [(y, x, z) for y, x in (pair if k % 2 == 0 else pair[::-1])]
-    return [(y * 2 + x) * gy_count + z * 2 + core for y, x, z in chips for core in (0, 1)]
+    a, b, c, d = (0, 0), (0, 1), (1, 1), (1, 0)
+    chips = [(d, 0), (a, 0), (b, 0), (c, 0)]
+    for z in range(1, layers - 1):
+        chips += [(column, z) for column in ((c, b, a) if z % 2 else (a, b, c))]
+    chips += [(column, layers - 1) for column in (c, b, a, d)]
+    chips += [(d, z) for z in range(layers - 2, 0, -1)]
+    count = len(chips)
+
+    def moved(turn):
+        return sum(abs(chips[(i + turn) % count][1] - i // gx_count) for i in range(count))
+
+    turn = min(range(count), key=moved)
+    chips = chips[turn:] + chips[:turn]
+    spots = [(column, z, core) for column, z in chips for core in (0, 1)]
+    ring = [(y * 2 + x) * gy_count + 2 * z + core for (y, x), z, core in spots]
+
+    def hops(i, j, place):
+        (y, x), z, _ = spots[place]
+        return abs(i // 2 - y) + abs(i % 2 - x) + abs(j // 2 - z)
+
+    orders = list(itertools.permutations(range(gx_count)))
+    squares = [
+        rows
+        for rows in itertools.product(orders, repeat=gx_count)
+        if all(len(set(column)) == gx_count for column in zip(*rows))
+    ]
+    send = np.zeros((gx_count * gy_count, gx_count), np.int32)
+    part = np.zeros((gx_count * gy_count, gx_count), np.int32)
+    group = np.zeros(gx_count * gy_count, np.int32)
+    for j in range(gy_count):
+        far = [[hops(i, j, gx_count * j + s) for s in range(gx_count)] for i in range(gx_count)]
+        cost = lambda rows: [max(far[i][row[i]] for i in range(gx_count)) for row in rows]
+        best = min(squares, key=lambda rows: (sum(cost(rows)), cost(rows)))
+        for q, row in enumerate(best):
+            for i in range(gx_count):
+                send[i * gy_count + j, q] = row[i]
+                part[ring[gx_count * j + row[i]], q] = i
+        for s in range(gx_count):
+            group[ring[gx_count * j + s]] = j
+    return ring, send, part, group
 
 
 def split_bf16(values):
@@ -396,8 +430,8 @@
     lam_a = np.kron(one, np.kron(values, one))
     lam_b = np.kron(values[order_b], np.kron(one, one))
     lam_c = np.kron(one, np.kron(one, values))
-    spectrum = np.stack([lam_a, lam_b, lam_c] + [0 * lam_a] * 5, axis=1)
     root3 = np.kron(root, np.kron(root, root))
+    spectrum = np.stack([lam_a, lam_b, lam_c, root3, 1.0 / root3] + [0 * lam_a] * 3, axis=1)
     edge = np.where((np.arange(NODES) == 0) | (np.arange(NODES) == NODES - 1), 0.5, 1.0)
     jw = interp * root[:, None] * edge[:, None]
     first = np.zeros_like(jw)
@@ -423,22 +457,38 @@
         for ex in range(2):
             for ez in range(ez_count):
                 swap[(t * 2 + ex) * ez_count + ez, ex * 2 * ez_count + 2 * ez + t] = 1.0
+    span = 2 * ez_count * NODES
+    deal = np.zeros((span, span))
+    for ex in range(2):
+        for ez in range(ez_count):
+            for c in range(NODES):
+                deal[(ex * ez_count + ez) * NODES + c, (c * 2 + ex) * ez_count + ez] = 1.0
     as32 = lambda t: np.asarray(t, np.float32)
     return dict(
         forward=forward,
         backward=backward,
-        spectrum=as32(spectrum),
-        root3=as32(root3[:, None]),
-        inv_root3=as32(1.0 / root3[:, None]),
+        columns=as32(np.concatenate([spectrum, prolong], axis=1)),
         restrict=as32(restrict),
-        prolong=as32(prolong),
-        swap=as32(swap),
-        unswap=as32(swap.T),
+        swaps=as32(np.concatenate([swap, swap.T], axis=0)),
+        deal=deal.astype(bf16),
+        gather=deal.T.astype(bf16),
     )
 
 
 def hp_dot(a, b):
     return jnp.dot(a, b, precision=highest, preferred_element_type=f32)
+
+
+def move_lanes(field, table):
+    rows = field.shape[0]
+    high = field.astype(bf16)
+    rest = field - high.astype(f32)
+    middle = rest.astype(bf16)
+    low = (rest - middle.astype(f32)).astype(bf16)
+    moved = jnp.dot(
+        jnp.concatenate([high, middle, low], axis=0), table, preferred_element_type=f32
+    )
+    return moved[:rows] + moved[rows : 2 * rows] + moved[2 * rows :]
 
 
 def wide_dot(table, field):
@@ -528,8 +578,58 @@
     return jnp.concatenate([low, field[face : rows - face], high], axis=0)
 
 
+def pack_kernel(*refs):
+    (place_ref, count_ref, source_ref, geometry_ref, disc_ref, thrust_ref, factor_ref,
+     q0, q1, q2, q3) = refs
+    parts, nodes_rows, lanes = source_ref.shape
+    levels = count_ref.shape[0]
+    count = factor_ref.shape[0]
+    cols = count // levels
+    span = factor_ref.shape[1] // (8 * parts)
+    lane = lax.broadcasted_iota(jnp.int32, (1, lanes), 1)
+    limit = jnp.zeros((1, lanes), jnp.int32)
+    for l in range(levels):
+        limit = jnp.where(lane // cols == l, count_ref[l, 0], limit)
+    live = jnp.where(lax.rem(lane, cols) < limit, 1.0, 0.0).astype(f32)
+    push = disc_ref[...].astype(f32) * thrust_ref[...]
+    ez_count = push.shape[2]
+    blank = jnp.zeros((1, lanes - 2 * ez_count), f32)
+
+    def fill(ref, ey):
+        ref[:nodes_rows] = source_ref[ey]
+        for c in range(3):
+            ref[nodes_rows + c : nodes_rows + c + 1] = jnp.concatenate(
+                [geometry_ref[c, ex, ey : ey + 1] for ex in range(2)] + [blank], axis=1
+            )
+        ref[nodes_rows + 3 : nodes_rows + 4] = jnp.concatenate(
+            [push[ex, ey : ey + 1] for ex in range(2)] + [blank], axis=1
+        )
+        ref[nodes_rows + 4 : nodes_rows + 5] = live
+        ref[nodes_rows + 5 : nodes_rows + 8] = jnp.zeros((3, lanes), f32)
+        for pair in range(4):
+            at = [(2 * pair + k) * parts * span + ey * span for k in range(2)]
+            base = nodes_rows + 8 + (pair // 2) * count
+            column = (pair % 2) * 2 * span
+            ref[base : base + count, column : column + 2 * span] = jnp.concatenate(
+                [factor_ref[:, start : start + span] for start in at], axis=1
+            )
+
+    for q, ref in enumerate((q0, q1, q2, q3)):
+        for ey in range(parts):
+            pl.when(place_ref[q] == ey)(functools.partial(fill, ref, ey))
+
+
+def message_part(base_ref, q):
+    return base_ref[4 + q]
+
+
+def factor_block(ref, count, vu):
+    base = ref.shape[0] - 2 * count + (vu // 2) * count
+    return ref[base : base + count, (vu % 2) * 128 : (vu % 2) * 128 + 128]
+
+
 def entry_kernel(ez_count, *refs):
-    (shift_ref, q0, q1, q2, q3, spectrum_ref, root_ref,
+    (place_ref, q0, q1, q2, q3, columns_ref, deal_ref,
      w_ref, low_ref, high_ref, inv_ref, den_ref, live_ref, held) = refs
     rows = w_ref.shape[0] // 2
     face = rows // NODES
@@ -537,9 +637,11 @@
     parts = 4
     width = lanes // parts
     for q, ref in enumerate((q0, q1, q2, q3)):
-        held[lax.rem(shift_ref[0] - q + parts, parts)] = ref[...]
-    sizes = jnp.concatenate([held[i, face : face + 8, :width] for i in range(parts)], axis=1)
-    len_x, len_y, len_z = sizes[0:1], sizes[1:2], sizes[2:3]
+        held[message_part(place_ref, q)] = ref[: 2 * face + 8]
+    sizes = jnp.concatenate(
+        [held[i, 2 * face : 2 * face + 8, :width] for i in range(parts)], axis=1
+    )
+    len_x, len_y, len_z, push = sizes[0:1], sizes[1:2], sizes[2:3], sizes[3:4]
     metric_x = len_y * len_z / (2.0 * len_x)
     metric_y = len_x * len_z / (2.0 * len_y)
     metric_z = len_x * len_y / (2.0 * len_z)
@@ -547,20 +649,30 @@
     metrics = jnp.concatenate(
         [metric_x, metric_y, metric_z, jnp.zeros((5, lanes), f32)], axis=0
     )
-    stiff = hp_dot(spectrum_ref[...], metrics)
+    stiff = hp_dot(columns_ref[:, :8], metrics)
     den_ref[...] = stiff
     inv_ref[...] = 1.0 / (stiff + shift_ratio * (metric_x + metric_y + metric_z))
     for i in range(parts):
-        live = held[i, face + 3 : face + 4, : 2 * 128]
-        live_ref[2 * i : 2 * i + 1] = live[:, :128]
-        live_ref[2 * i + 1 : 2 * i + 2] = live[:, 128:]
+        live_ref[2 * i : 2 * i + 1] = held[i, 2 * face + 4 : 2 * face + 5, :128]
+        live_ref[2 * i + 1 : 2 * i + 2] = held[i, 2 * face + 4 : 2 * face + 5, 128:256]
+    raw = jnp.concatenate(
+        [
+            jnp.concatenate([held[i, :face], held[i, face : 2 * face]], axis=1)
+            for i in range(parts)
+        ],
+        axis=0,
+    )
+    dealt = move_lanes(raw, deal_ref[...])
     for c in range(NODES):
         for side in range(2):
             w_ref[pl.ds(side * rows + c, face, stride=NODES), :] = jnp.concatenate(
-                [held[i, :face, c * width : (c + 1) * width] for i in (2 * side, 2 * side + 1)],
+                [
+                    dealt[i * face : (i + 1) * face, c * width : (c + 1) * width]
+                    for i in (2 * side, 2 * side + 1)
+                ],
                 axis=1,
             )
-    forcing = lane_halves(w_ref) * (root_ref[...] * volume)
+    forcing = (lane_halves(w_ref) + push) * (columns_ref[:, 3:4] * volume)
     assemble_local(forcing, w_ref, low_ref, high_ref, ez_count, False)
 
 
@@ -598,8 +710,8 @@
     assemble_local(field, k_ref, low_ref, high_ref, ez_count, False)
 
 
-def restrict_kernel(ez_count, *refs):
-    (shift_ref, w_ref, prev_ref, next_ref, r_in_ref, restrict_ref, swap_ref, x0, x1, x2, x3,
+def restrict_kernel(ez_count, count, *refs):
+    (place_ref, w_ref, prev_ref, next_ref, r_in_ref, restrict_ref, swaps_ref, x0, x1, x2, x3,
      r_ref, part_ref, coarse, sums) = refs
     lanes = 2 * w_ref.shape[1]
     parts = 4
@@ -612,40 +724,42 @@
         pair = jnp.concatenate(
             [b[:4, i * width : (i + 1) * width], b[4:, i * width : (i + 1) * width]], axis=1
         )
-        coarse[i] = hp_dot(jnp.concatenate([pair, pair], axis=0), swap_ref[...])
+        coarse[i] = hp_dot(jnp.concatenate([pair, pair], axis=0), swaps_ref[: 2 * width])
     sums[...] = jnp.zeros_like(sums)
-    count = x0.shape[0]
     block = 2 * width
     for q, ref in enumerate((x0, x1, x2, x3)):
-        i = lax.rem(shift_ref[0] - q + parts, parts)
+        i = message_part(place_ref, q)
         mine = coarse[i]
-        acc = ref[:, :block] * mine[0:1]
+        acc = factor_block(ref, count, 0) * mine[0:1]
         for vu in range(1, 4):
-            acc = acc + ref[:, vu * block : (vu + 1) * block] * mine[vu : vu + 1]
+            acc = acc + factor_block(ref, count, vu) * mine[vu : vu + 1]
         sums[i, :count] = acc
     flat = sums[...].reshape(parts * sums.shape[1], block)
     ones = jnp.ones((8, block), f32)
     row = lax.dot_general(
         ones, flat, (((1,), (1,)), ((), ())), precision=highest, preferred_element_type=f32
     )
-    for i in range(2 * parts):
-        part_ref[i : i + 1] = row[0:1, i * 128 : (i + 1) * 128]
-
-
-def prolong_kernel(ez_count, inner_levels, cols, *refs):
-    (shift_ref, all_ref, member_ref, live_ref, unswap_ref, prolong_ref, x0, x1, x2, x3,
+    tile = jnp.concatenate(
+        [row[0:1, i * 128 : (i + 1) * 128] for i in range(2 * parts)], axis=0
+    )
+    part_ref[...] = jnp.broadcast_to(tile[None], part_ref.shape)
+
+
+def prolong_kernel(ez_count, count, inner_levels, cols, groups, *refs):
+    (place_ref, all_ref, live_ref, swaps_ref, columns_ref, x0, x1, x2, x3,
      w_ref, low_ref, high_ref, table, coarse) = refs
     lanes = 2 * w_ref.shape[1]
     parts = 4
     width = lanes // parts
     block = 2 * width
-    count = x0.shape[0]
-    base = all_ref[0] * member_ref[0]
-    for source in range(1, all_ref.shape[0]):
-        base = base + all_ref[source] * member_ref[source]
-    row_id = lax.broadcasted_iota(jnp.int32, base.shape, 0)
-    lane_id = lax.broadcasted_iota(jnp.int32, base.shape, 1)
+    row_id = lax.broadcasted_iota(jnp.int32, all_ref.shape[1:], 0)
+    lane_id = lax.broadcasted_iota(jnp.int32, all_ref.shape[1:], 1)
     level = (lax.rem(row_id, 2) * 128 + lane_id) // cols
+    mine = lax.shift_right_logical(jnp.full_like(level, place_ref[8]), level)
+    base = jnp.zeros(all_ref.shape[1:], f32)
+    for source in range(all_ref.shape[0]):
+        theirs = lax.shift_right_logical(jnp.full_like(level, groups[source]), level)
+        base = base + jnp.where(theirs == mine, all_ref[source], 0.0)
     total = base
     step = 2
     for bit in range(2):
@@ -662,41 +776,46 @@
         table[i, :128] = jnp.broadcast_to(turned[:, 2 * i : 2 * i + 1], (128, block))
         table[i, 128:] = jnp.broadcast_to(turned[:, 2 * i + 1 : 2 * i + 2], (128, block))
     for q, ref in enumerate((x0, x1, x2, x3)):
-        i = lax.rem(shift_ref[0] - q + parts, parts)
+        i = message_part(place_ref, q)
         y = table[i, :count]
         for vu in range(4):
             coarse[i, vu : vu + 1] = jnp.sum(
-                ref[:, vu * block : (vu + 1) * block] * y, axis=0, keepdims=True
+                factor_block(ref, count, vu) * y, axis=0, keepdims=True
             )
     lows, highs = [], []
     for i in range(parts):
-        pair = hp_dot(coarse[i], unswap_ref[...])
+        pair = hp_dot(coarse[i], swaps_ref[2 * width :])
         lows.append(pair[:4, :width])
         highs.append(pair[:4, width:])
     e = jnp.concatenate([jnp.concatenate(lows, axis=1), jnp.concatenate(highs, axis=1)], axis=0)
-    field = hp_dot(prolong_ref[...], e)
+    field = hp_dot(columns_ref[...], jnp.concatenate([jnp.zeros_like(e), e], axis=0))
     assemble_local(field, w_ref, low_ref, high_ref, ez_count, True)
 
 
 def exit_kernel(keep, gain, *refs):
-    (shift_ref, w_ref, prev_ref, next_ref, d_ref, x_ref, inv_root_ref,
+    (place_ref, w_ref, prev_ref, next_ref, d_ref, x_ref, columns_ref, gather_ref,
      q0, q1, q2, q3, field, held) = refs
     lanes = 2 * w_ref.shape[1]
     parts = 4
     width = lanes // parts
     face = prev_ref.shape[0]
+    rows = x_ref.shape[0]
     step = joined(w_ref, prev_ref, next_ref, 0.5) * gain + keep * d_ref[...]
-    rows = x_ref.shape[0]
-    store_halves(field, (x_ref[...] + step) * inv_root_ref[...])
-    for c in range(NODES):
-        for side in range(2):
-            layer = field[pl.ds(side * rows + c, face, stride=NODES), :]
-            for i in range(2):
-                held[2 * side + i, :, c * width : (c + 1) * width] = layer[
-                    :, i * width : (i + 1) * width
-                ]
+    store_halves(field, (x_ref[...] + step) * columns_ref[:, 4:5])
+    blocks = []
+    for side in range(2):
+        layers = [field[pl.ds(side * rows + c, face, stride=NODES), :] for c in range(NODES)]
+        for i in range(2):
+            blocks.append(
+                jnp.concatenate([t[:, i * width : (i + 1) * width] for t in layers], axis=1)
+            )
+    dealt = move_lanes(jnp.concatenate(blocks, axis=0), gather_ref[...])
+    half = dealt.shape[1] // 2
+    for i in range(parts):
+        held[i, 0] = dealt[i * face : (i + 1) * face, :half]
+        held[i, 1] = dealt[i * face : (i + 1) * face, half:]
     for q, ref in enumerate((q0, q1, q2, q3)):
-        ref[...] = held[lax.rem(shift_ref[0] - q + parts, parts)]
+        ref[...] = held[message_part(place_ref, q)]
 
 
 def call(kernel, name, out_shapes, args, scratch=(), smem_args=0):
@@ -709,7 +828,7 @@
         in_specs=specs,
         out_specs=[pl.BlockSpec(memory_space=VMEM)] * len(out_shapes),
         scratch_shapes=list(scratch),
-        compiler_params=pltpu.CompilerParams(vmem_limit_bytes=24 * 1024 * 1024),
+        compiler_params=pltpu.CompilerParams(vmem_limit_bytes=12 * 1024 * 1024),
     )(*args)
 
 
@@ -726,20 +845,19 @@
     face = nodes * nodes
     devices = gx_count * gy_count
     tables = {k: jnp.asarray(v) for k, v in constant_tables(ez_count, lanes).items()}
-    ring = device_ring(gx_count, gy_count)
-    place = np.zeros(devices, np.int32)
-    for position, device in enumerate(ring):
-        place[device] = position
-    gx_index, gy_index = lax.axis_index("gx"), lax.axis_index("gy")
-    position = jnp.asarray(place)[gx_index * gy_count + gy_index]
-    shift = lax.rem(position, parts)
-    shift_arr = shift[None].astype(jnp.int32)
+    ring, send, part, group = placement(gx_count, gy_count)
+    groups = [int(g) for g in group]
+    facts = np.concatenate([send, part, group[:, None], np.argsort(send, axis=1)], axis=1)
+    device = lax.axis_index("gx") * gy_count + lax.axis_index("gy")
+    place = lax.dynamic_index_in_dim(
+        jnp.asarray(facts.astype(np.int32)), device, 0, keepdims=False
+    )
     up = [(ring[i], ring[(i + 1) % devices]) for i in range(devices)]
     down = [(target, origin) for origin, target in up]
 
     def spread(q):
         return [
-            (i * gy_count + j, ring[parts * j + (q + i) % parts])
+            (i * gy_count + j, ring[parts * j + int(send[i * gy_count + j, q])])
             for i in range(gx_count)
             for j in range(gy_count)
         ]
@@ -747,34 +865,17 @@
     def halo(low, high):
         return lax.ppermute(high, axes, up), lax.ppermute(low, axes, down)
 
-    def chunk(stack, q):
-        return lax.dynamic_index_in_dim(stack, lax.rem(q + gx_index, parts), 0, keepdims=False)
-
-    force = source + jnp.repeat(disc_mask.astype(f32) * thrust, nodes, axis=2)[None, None]
-    force = force.reshape(nodes, nodes, elem_x, elem_y, ez_count, nodes)
-    force = force.transpose(3, 1, 0, 5, 2, 4).reshape(elem_y, face, nodes * width)
-    sizes = geometry.transpose(2, 0, 1, 3).reshape(elem_y, 3, width)
-    sizes = jnp.pad(sizes, ((0, 0), (0, 0), (0, nodes * width - width)))
-    live = (jnp.arange(cols)[None, :] < col_count).astype(f32).reshape(1, 1, levels * cols)
-    live = jnp.pad(live, ((0, 0), (0, 0), (0, nodes * width - levels * cols)))
-    live = jnp.broadcast_to(live, (elem_y, 1, nodes * width))
-    packed = jnp.concatenate(
-        [force, sizes, live, jnp.zeros((elem_y, 4, nodes * width), f32)], axis=1
-    )
-    received = [lax.ppermute(chunk(packed, q), axes, spread(q)) for q in range(parts)]
-
-    factor = xxt_factor.reshape(levels * cols, 4 * elem_x, elem_y, 2 * ez_count)
-    factor = factor.transpose(2, 0, 1, 3).reshape(elem_y, levels * cols, 8 * width)
-    factors = [lax.ppermute(chunk(factor, q), axes, spread(q)) for q in range(parts)]
-
+    count = levels * cols
+    moved = source.transpose(3, 2, 1, 0, 4).reshape(elem_y, elem_x * face, z_count)
+    message = (elem_x * face + 8 + 2 * count, z_count)
+    packed = call(
+        pack_kernel, "pack", [message] * parts,
+        [place, col_count, moved, geometry, disc_mask, thrust,
+         xxt_factor.reshape(count, -1)],
+        (), 2,
+    )
+    received = [lax.ppermute(packed[q], axes, spread(q)) for q in range(parts)]
     inner_levels = gy_count.bit_length() - 1
-    level_of = np.minimum(np.arange(256) // cols, 31)
-    group_of = place // parts
-    member = (
-        jnp.right_shift(jnp.asarray(group_of)[:, None], jnp.asarray(level_of)[None])
-        == jnp.right_shift(position // parts, jnp.asarray(level_of))[None]
-    ) & (np.arange(256) < levels * cols)[None]
-    member = jnp.tile(member.astype(f32), (1, parts)).reshape(devices, 2 * parts, 128)
 
     fshape = (rows, lanes)
     sshape = (2 * rows, lanes // 2)
@@ -782,8 +883,8 @@
     w, low, high, inv, den, live_tile = call(
         functools.partial(entry_kernel, ez_count), "entry",
         [sshape, hshape, hshape, fshape, fshape, (2 * parts, 128)],
-        [shift_arr, *received, tables["spectrum"], tables["root3"]],
-        [VMEM((parts, face + 8, nodes * width), f32)], 1,
+        [place, *received, tables["columns"], tables["deal"]],
+        [VMEM((parts, 2 * face + 8, z_count), f32)], 1,
     )
     fwd, bwd = tables["forward"], tables["backward"]
 
@@ -823,18 +924,17 @@
         x, k, low, high, _ = advance(u, low, high, d, x, keep, gain, False)
         prev, nxt = halo(low, high)
         resid, partial = call(
-            functools.partial(restrict_kernel, ez_count), "restrict",
-            [fshape, (2 * parts, 128)],
-            [shift_arr, k, prev, nxt, resid, tables["restrict"], tables["swap"], *factors],
+            functools.partial(restrict_kernel, ez_count, count), "restrict",
+            [fshape, (devices, 2 * parts, 128)],
+            [place, k, prev, nxt, resid, tables["restrict"], tables["swaps"], *received],
             [VMEM((parts, 8, 2 * width), f32), VMEM((parts, 256, 2 * width), f32)], 1,
         )
-        everyone = lax.all_to_all(
-            jnp.broadcast_to(partial[None], (devices,) + partial.shape), axes, 0, 0
-        )
+        everyone = lax.all_to_all(partial, axes, 0, 0)
         f, low, high = call(
-            functools.partial(prolong_kernel, ez_count, inner_levels, cols), "prolong",
+            functools.partial(prolong_kernel, ez_count, count, inner_levels, cols, groups), "prolong",
             [sshape, hshape, hshape],
-            [shift_arr, everyone, member, live_tile, tables["unswap"], tables["prolong"], *factors],
+            [place, everyone, live_tile, tables["swaps"], tables["columns"],
+             *received],
             [VMEM((parts, 256, 2 * width), f32), VMEM((parts, 8, 2 * width), f32)], 1,
         )
         x, k, low, high, _ = advance(f, low, high, None, x, 0.0, 1.0, False)
@@ -846,18 +946,22 @@
     prev, nxt = halo(low, high)
     chunks = call(
         functools.partial(exit_kernel, keep, gain), "exit",
-        [(face, nodes * width)] * parts,
-        [shift_arr, u, prev, nxt, d, x, tables["inv_root3"]],
-        [VMEM(sshape, f32), VMEM((parts, face, nodes * width), f32)], 1,
+        [(2, face, z_count)] * parts,
+        [place, u, prev, nxt, d, x, tables["columns"], tables["gather"]],
+        [VMEM(sshape, f32), VMEM((parts, 2, face, z_count), f32)], 1,
     )
     back = [
         lax.ppermute(chunks[q], axes, [(t, s) for s, t in spread(q)]) for q in range(parts)
     ]
-    stacked = jnp.stack(back + back)
-    start = lax.rem(parts - gx_index, parts)
-    by_ey = lax.dynamic_slice_in_dim(stacked, start, parts, 0)
-    by_ey = by_ey.reshape(elem_y, nodes, nodes, nodes, elem_x, ez_count)
-    return by_ey.transpose(2, 1, 4, 0, 5, 3).reshape(source.shape)
+    stacked = jnp.stack(back)
+    by_ey = jnp.stack(
+        [
+            lax.dynamic_index_in_dim(stacked, place[9 + ey], 0, keepdims=False)
+            for ey in range(parts)
+        ]
+    )
+    by_ey = by_ey.reshape(elem_y, elem_x, nodes, nodes, z_count)
+    return by_ey.transpose(3, 2, 1, 0, 4)
 
 
 def is_fast(mesh, source, geometry, xxt_factor):
@@ -866,8 +970,8 @@
     ez_count = geometry.shape[3]
     levels, cols, _ = xxt_factor.shape
     return (
-        gx_count == 4 and elem_y == gx_count and gy_count % 2 == 0 and gy_count >= 4
-        and gy_count & (gy_count - 1) == 0 and elem_x == 2 and nodes == NODES
+        gx_count == 4 and elem_y == gx_count and gy_count % 4 == 0 and gy_count >= 8
+        and gy_count & (gy_count - 1) == 0 and elem_x == 2 and nodes == NODES and z_count == 256
         and 2 * elem_x * ez_count == 128 and levels * cols <= 256
         and 4 * elem_x * ez_count == 256 and levels == (gx_count * gy_count).bit_length() and (levels * cols) % 8 == 0
     )

time: 270 us -> 194 us (0.72)
  the two profiles are of different devices: /device:TPU:26 before, /device:TPU:0 now
where the time goes in v2:
time: 194 us; the launch traced here: 193 us
  starting transfers between devices  66 us (34%)
  waiting for transfers between devices  55 us (28%)
  Pallas kernels  30.8 us (16%)
  blocking collectives  25.3 us (13%)
  local copies, waits for them, and re-layouts  8.21 us (4%)
  between operations  7.82 us (4%)
    ppermute x40, starting transfers between devices, halo(): return (lax.ppermute(high, axes, up), lax.ppermute(low, axes, down))  41.5 us
    ppermute x40, waiting for transfers between devices, halo(): return (lax.ppermute(high, axes, up), lax.ppermute(low, axes, down))  38.2 us
    pallas_call x24, Pallas kernels, call(): pl.pallas_call(kernel, name=name, out_shape=[jax.ShapeDtypeStruct(s, f32)...  30.8 us
    all_to_all x2, blocking collectives, fast_device(): everyone = lax.all_to_all(partial, axes, 0, 0)  25.3 us
    ppermute x4, waiting for transfers between devices, fast_device(): received = [lax.ppermute(packed[q], axes, spread(q)) for q in range(parts)]  16.7 us
    ppermute x4, starting transfers between devices, fast_device(): received = [lax.ppermute(packed[q], axes, spread(q)) for q in range(parts)]  13.5 us
    ppermute x4, starting transfers between devices, fast_device(): lax.ppermute(chunks[q], axes, [(t, s) for s, t in spread(q)])  10.9 us
    unnamed x23, local copies, waits for them, and re-layouts  4.26 us
  transfers between devices with their start and end apart: 48, of which 27 were waited for; matrix products, arithmetic and copies ran while one was open for 0% of the time, Pallas kernels for 0%

profile of v2, /device:TPU:0, one launch (start us, length us, event | category | flops | bytes accessed | tf_op | source)
XLA Modules:
  0.0 193.2 jit_solution(17352342570033143211)
XLA Ops:
  0.0 1.4 copy.15
  2.9 1.4 copy-done.4
  6.4 1.4 pack.1
  7.8 6.0 %collective-permute-start = (f32[520,256]{1,0:T(8,128)S(1)}, f32[520,256]{1,0:T(8,128)S(1)}, u32[]{:S(2)}, u32[]{:S(2)}) collective-permute-start(f32[520,256]{1,0:T(8,128)S(1)} %get-tuple-element.100), channel_id=1, source_target_pairs={{0,18},{1,0},{2,26},{3,10},{4,4},{5,28},{6,14},{7,22},{8,16},{9,8}... | collective-permute-start | bytes 1597448 | tf_op jit(solution)/shard_map/ppermute | solution.py:877
  13.8 1.9 collective-permute-start.1
  15.8 3.3 %collective-permute-start.2 = (f32[520,256]{1,0:T(8,128)S(1)}, f32[520,256]{1,0:T(8,128)S(1)}, u32[]{:S(2)}, u32[]{:S(2)}) collective-permute-start(f32[520,256]{1,0:T(8,128)S(1)} %get-tuple-element.102), channel_id=1, source_target_pairs={{0,16},{1,8},{2,24},{3,2},{4,12},{5,30},{6,6},{7,20},{8,18},{9,0},... | collective-permute-start | bytes 1597448 | tf_op jit(solution)/shard_map/ppermute | solution.py:877
  19.1 2.3 %collective-permute-start.3 = (f32[520,256]{1,0:T(8,128)S(1)}, f32[520,256]{1,0:T(8,128)S(1)}, u32[]{:S(2)}, u32[]{:S(2)}) collective-permute-start(f32[520,256]{1,0:T(8,128)S(1)} %get-tuple-element.103), channel_id=1, source_target_pairs={{0,17},{1,9},{2,25},{3,3},{4,13},{5,31},{6,7},{7,21},{8,19},{9,1},... | collective-permute-start | bytes 1597448 | tf_op jit(solution)/shard_map/ppermute | solution.py:877
  21.4 10.0 %collective-permute-done.1.refs_2_.refs_8_.refs_6_ = f32[520,256]{1,0:T(8,128)S(1)} collective-permute-done((f32[520,256]{1,0:T(8,128)S(1)}, f32[520,256]{1,0:T(8,128)S(1)}, u32[]{:S(2)}, u32[]{:S(2)}) %collective-permute-start.1) | collective-permute-done | bytes 532512 | tf_op jit(solution)/shard_map/ppermute | solution.py:877
  32.1 6.0 %collective-permute-done.3.refs_4_.refs_10_.refs_8_ = f32[520,256]{1,0:T(8,128)S(1)} collective-permute-done((f32[520,256]{1,0:T(8,128)S(1)}, f32[520,256]{1,0:T(8,128)S(1)}, u32[]{:S(2)}, u32[]{:S(2)}) %collective-permute-start.3) | collective-permute-done | bytes 532512 | tf_op jit(solution)/shard_map/ppermute | solution.py:877
  38.1 1.9 entry.1
  40.0 3.5 %collective-permute-start.4 = (f32[64,256]{1,0:T(8,128)S(1)}, f32[64,256]{1,0:T(8,128)S(1)}, u32[]{:S(2)}, u32[]{:S(2)}) collective-permute-start(f32[64,256]{1,0:T(8,128)S(1)} %get-tuple-element.105), channel_id=1, source_target_pairs={{18,19},{19,16},{16,17},{17,0},{0,1},{1,8},{8,9},{9,24},{24,25},{2... | collective-permute-start | bytes 196616 | tf_op jit(solution)/shard_map/ppermute | solution.py:866
  46.4 2.4 %collective-permute-start.6 = (f32[64,256]{1,0:T(8,128)S(1)}, f32[64,256]{1,0:T(8,128)S(1)}, u32[]{:S(2)}, u32[]{:S(2)}) collective-permute-start(f32[64,256]{1,0:T(8,128)S(1)} %get-tuple-element.109), channel_id=1, source_target_pairs={{18,19},{19,16},{16,17},{17,0},{0,1},{1,8},{8,9},{9,24},{24,25},{2... | collective-permute-start | bytes 196616 | tf_op jit(solution)/shard_map/ppermute | solution.py:866
  48.8 1.4 collective-permute-done.6.refs_1_
  51.7 1.9 collective-permute-start.8
  53.6 1.9 collective-permute-done.8.refs_1_
  56.4 3.5 %collective-permute-start.10 = (f32[64,256]{1,0:T(8,128)S(1)}, f32[64,256]{1,0:T(8,128)S(1)}, u32[]{:S(2)}, u32[]{:S(2)}) collective-permute-start(f32[64,256]{1,0:T(8,128)S(1)} %get-tuple-element.117), channel_id=1, source_target_pairs={{18,19},{19,16},{16,17},{17,0},{0,1},{1,8},{8,9},{9,24},{24,25},{2... | collective-permute-start | bytes 196616 | tf_op jit(solution)/shard_map/ppermute | solution.py:866
  62.8 1.9 collective-permute-start.12
  64.7 1.9 collective-permute-done.12.refs_2_
  66.6 2.3 %restrict.2 = (f32[512,256]{1,0:T(8,128)S(1)}, f32[32,8,128]{2,1,0:T(8,128)S(1)}) custom-call(s32[13]{0:T(128)S(1)} %get-tuple-element.200.refs_0_, f32[1024,128]{1,0:T(8,128)S(1)} %get-tuple-element.121.refs_1_, f32[64,256]{1,0:T(8,128)S(1)} %collective-permute-done.12.refs_2_, f32[64,256]{1,0:T(8,128)S(1)} %collective-permute-done.13.refs_3_, ...), custom_call_target="tpu_custom_call" | custom-call | tf_op jit(solution)/shard_map/restrict/pallas_call | solution.py:824
  69.0 14.6 %all_to_all.10.refs_1_ = f32[32,8,128]{2,1,0:T(8,128)S(1)} all-to-all(f32[32,8,128]{2,1,0:T(8,128)S(1)} %get-tuple-element.125), channel_id=1, replica_groups=mesh['gx'=4,'gy'=8] {'gx','gy'}, dimensions={0} | all-to-all | bytes 262144 | tf_op jit(solution)/shard_map/all_to_all | solution.py:932
  83.6 2.2 %prolong.2 = (f32[1024,128]{1,0:T(8,128)S(1)}, f32[64,256]{1,0:T(8,128)S(1)}, f32[64,256]{1,0:T(8,128)S(1)}) custom-call(s32[13]{0:T(128)S(1)} %get-tuple-element.200.refs_0_, f32[32,8,128]{2,1,0:T(8,128)S(1)} %all_to_all.10.refs_1_, f32[8,128]{1,0:T(8,128)S(1)} %get-tuple-element.126.refs_2_, f32[256,128]{1,0:T(8,128)S(1)} %copy-done.3, ...), custom_call_target="tpu_custom_call" | custom-call | tf_op jit(solution)/shard_map/prolong/pallas_call | solution.py:824
  86.1 1.4 collective-permute-start.15
  87.6 1.9 %collective-permute-done.14.refs_1_ = f32[64,256]{1,0:T(8,128)S(1)} collective-permute-done((f32[64,256]{1,0:T(8,128)S(1)}, f32[64,256]{1,0:T(8,128)S(1)}, u32[]{:S(2)}, u32[]{:S(2)}) %collective-permute-start.14) | collective-permute-done | bytes 65568 | tf_op jit(solution)/shard_map/ppermute | solution.py:866
  92.5 1.7 collective-permute-done.16.refs_1_
  97.3 1.9 collective-permute-done.18.refs_1_
  102.1 1.9 collective-permute-done.20.refs_1_
  106.9 1.9 collective-permute-done.22.refs_1_
  111.7 1.9 collective-permute-done.24.refs_1_
  116.5 1.9 collective-permute-done.26.refs_1_
  121.3 1.9 collective-permute-done.28.refs_1_
  126.0 1.9 collective-permute-done.30.refs_1_
  130.8 1.9 collective-permute-done.32.refs_2_
  132.7 2.3 %restrict.3 = (f32[512,256]{1,0:T(8,128)S(1)}, f32[32,8,128]{2,1,0:T(8,128)S(1)}) custom-call(s32[13]{0:T(128)S(1)} %get-tuple-element.200.refs_0_, f32[1024,128]{1,0:T(8,128)S(1)} %get-tuple-element.165.refs_1_, f32[64,256]{1,0:T(8,128)S(1)} %collective-permute-done.32.refs_2_, f32[64,256]{1,0:T(8,128)S(1)} %collective-permute-done.33.refs_3_, ...), custom_call_target="tpu_custom_call" | custom-call | tf_op jit(solution)/shard_map/restrict/pallas_call | solution.py:824
  135.1 10.7 %all_to_all.11.refs_1_ = f32[32,8,128]{2,1,0:T(8,128)S(1)} all-to-all(f32[32,8,128]{2,1,0:T(8,128)S(1)} %get-tuple-element.169), channel_id=1, replica_groups=mesh['gx'=4,'gy'=8] {'gx','gy'}, dimensions={0} | all-to-all | bytes 262144 | tf_op jit(solution)/shard_map/all_to_all | solution.py:932
  145.8 2.2 %prolong.3 = (f32[1024,128]{1,0:T(8,128)S(1)}, f32[64,256]{1,0:T(8,128)S(1)}, f32[64,256]{1,0:T(8,128)S(1)}) custom-call(s32[13]{0:T(128)S(1)} %get-tuple-element.200.refs_0_, f32[32,8,128]{2,1,0:T(8,128)S(1)} %all_to_all.11.refs_1_, f32[8,128]{1,0:T(8,128)S(1)} %get-tuple-element.126.refs_2_, f32[256,128]{1,0:T(8,128)S(1)} %copy-done.3, ...), custom_call_target="tpu_custom_call" | custom-call | tf_op jit(solution)/shard_map/prolong/pallas_call | solution.py:824
  148.4 1.4 collective-permute-start.35
  149.8 1.9 %collective-permute-done.34.refs_1_ = f32[64,256]{1,0:T(8,128)S(1)} collective-permute-done((f32[64,256]{1,0:T(8,128)S(1)}, f32[64,256]{1,0:T(8,128)S(1)}, u32[]{:S(2)}, u32[]{:S(2)}) %collective-permute-start.34) | collective-permute-done | bytes 65568 | tf_op jit(solution)/shard_map/ppermute | solution.py:866
  154.6 1.9 collective-permute-done.36.refs_1_
  159.3 1.9 collective-permute-done.38.refs_1_
  164.1 1.9 collective-permute-done.40.refs_1_
  166.0 1.6 precond.15
  169.4 1.9 %collective-permute-done.42.refs_2_ = f32[64,256]{1,0:T(8,128)S(1)} collective-permute-done((f32[64,256]{1,0:T(8,128)S(1)}, f32[64,256]{1,0:T(8,128)S(1)}, u32[]{:S(2)}, u32[]{:S(2)}) %collective-permute-start.42) | collective-permute-done | bytes 65568 | tf_op jit(solution)/shard_map/ppermute | solution.py:866
  171.4 1.4 exit.1
  172.7 2.8 %collective-permute-start.44 = (f32[2,64,256]{2,1,0:T(8,128)S(1)}, f32[2,64,256]{2,1,0:T(8,128)S(1)}, u32[]{:S(2)}, u32[]{:S(2)}) collective-permute-start(f32[2,64,256]{2,1,0:T(8,128)S(1)} %get-tuple-element.191), channel_id=1, source_target_pairs={{18,0},{0,1},{26,2},{10,3},{4,4},{28,5},{14,6},{22,7},{16,8},{8,9}... | collective-permute-start | bytes 393224 | tf_op jit(solution)/shard_map/ppermute | solution.py:954
  175.6 2.7 %collective-permute-start.45 = (f32[2,64,256]{2,1,0:T(8,128)S(1)}, f32[2,64,256]{2,1,0:T(8,128)S(1)}, u32[]{:S(2)}, u32[]{:S(2)}) collective-permute-start(f32[2,64,256]{2,1,0:T(8,128)S(1)} %get-tuple-element.192), channel_id=1, source_target_pairs={{19,0},{1,1},{27,2},{11,3},{5,4},{29,5},{15,6},{23,7},{17,8},{9,9}... | collective-permute-start | bytes 393224 | tf_op jit(solution)/shard_map/ppermute | solution.py:954
  178.3 1.9 collective-permute-start.46
  180.2 3.4 %collective-permute-start.47 = (f32[2,64,256]{2,1,0:T(8,128)S(1)}, f32[2,64,256]{2,1,0:T(8,128)S(1)}, u32[]{:S(2)}, u32[]{:S(2)}) collective-permute-start(f32[2,64,256]{2,1,0:T(8,128)S(1)} %get-tuple-element.194), channel_id=1, source_target_pairs={{17,0},{9,1},{25,2},{3,3},{13,4},{31,5},{7,6},{21,7},{19,8},{1,9},... | collective-permute-start | bytes 393224 | tf_op jit(solution)/shard_map/ppermute | solution.py:954
  192.0 1.1 copy.19
  (104 shorter events, 50.7 us)
Async XLA Ops:
  7.8 13.6 %collective-permute-start = (f32[520,256]{1,0:T(8,128)S(1)}, f32[520,256]{1,0:T(8,128)S(1)}, u32[]{:S(2)}, u32[]{:S(2)}) collective-permute-start(f32[520,256]{1,0:T(8,128)S(1)} %get-tuple-element.100), channel_id=1, source_target_pairs={{0,18},{1,0},{2,26},{3,10},{4,4},{5,28},{6,14},{7,22},{8,16},{9,8}... | collective-permute-start | bytes 1597448 | tf_op jit(solution)/shard_map/ppermute | solution.py:877
  13.8 17.5 %collective-permute-start.1 = (f32[520,256]{1,0:T(8,128)S(1)}, f32[520,256]{1,0:T(8,128)S(1)}, u32[]{:S(2)}, u32[]{:S(2)}) collective-permute-start(f32[520,256]{1,0:T(8,128)S(1)} %get-tuple-element.101), channel_id=1, source_target_pairs={{0,19},{1,1},{2,27},{3,11},{4,5},{5,29},{6,15},{7,23},{8,17},{9,9}... | collective-permute-start | bytes 1597448 | tf_op jit(solution)/shard_map/ppermute | solution.py:877
  15.8 16.3 %collective-permute-start.2 = (f32[520,256]{1,0:T(8,128)S(1)}, f32[520,256]{1,0:T(8,128)S(1)}, u32[]{:S(2)}, u32[]{:S(2)}) collective-permute-start(f32[520,256]{1,0:T(8,128)S(1)} %get-tuple-element.102), channel_id=1, source_target_pairs={{0,16},{1,8},{2,24},{3,2},{4,12},{5,30},{6,6},{7,20},{8,18},{9,0},... | collective-permute-start | bytes 1597448 | tf_op jit(solution)/shard_map/ppermute | solution.py:877
  19.1 19.1 %collective-permute-start.3 = (f32[520,256]{1,0:T(8,128)S(1)}, f32[520,256]{1,0:T(8,128)S(1)}, u32[]{:S(2)}, u32[]{:S(2)}) collective-permute-start(f32[520,256]{1,0:T(8,128)S(1)} %get-tuple-element.103), channel_id=1, source_target_pairs={{0,17},{1,9},{2,25},{3,3},{4,13},{5,31},{6,7},{7,21},{8,19},{9,1},... | collective-permute-start | bytes 1597448 | tf_op jit(solution)/shard_map/ppermute | solution.py:877
  40.0 4.4 %collective-permute-start.4 = (f32[64,256]{1,0:T(8,128)S(1)}, f32[64,256]{1,0:T(8,128)S(1)}, u32[]{:S(2)}, u32[]{:S(2)}) collective-permute-start(f32[64,256]{1,0:T(8,128)S(1)} %get-tuple-element.105), channel_id=1, source_target_pairs={{18,19},{19,16},{16,17},{17,0},{0,1},{1,8},{8,9},{9,24},{24,25},{2... | collective-permute-start | bytes 196616 | tf_op jit(solution)/shard_map/ppermute | solution.py:866
  43.5 1.9 collective-permute-start.5
  46.4 3.8 %collective-permute-start.6 = (f32[64,256]{1,0:T(8,128)S(1)}, f32[64,256]{1,0:T(8,128)S(1)}, u32[]{:S(2)}, u32[]{:S(2)}) collective-permute-start(f32[64,256]{1,0:T(8,128)S(1)} %get-tuple-element.109), channel_id=1, source_target_pairs={{18,19},{19,16},{16,17},{17,0},{0,1},{1,8},{8,9},{9,24},{24,25},{2... | collective-permute-start | bytes 196616 | tf_op jit(solution)/shard_map/ppermute | solution.py:866
  48.8 1.9 collective-permute-start.7
  51.7 3.8 %collective-permute-start.8 = (f32[64,256]{1,0:T(8,128)S(1)}, f32[64,256]{1,0:T(8,128)S(1)}, u32[]{:S(2)}, u32[]{:S(2)}) collective-permute-start(f32[64,256]{1,0:T(8,128)S(1)} %get-tuple-element.113), channel_id=1, source_target_pairs={{18,19},{19,16},{16,17},{17,0},{0,1},{1,8},{8,9},{9,24},{24,25},{2... | collective-permute-start | bytes 196616 | tf_op jit(solution)/shard_map/ppermute | solution.py:866
  53.6 1.9 collective-permute-start.9
  56.4 4.4 %collective-permute-start.10 = (f32[64,256]{1,0:T(8,128)S(1)}, f32[64,256]{1,0:T(8,128)S(1)}, u32[]{:S(2)}, u32[]{:S(2)}) collective-permute-start(f32[64,256]{1,0:T(8,128)S(1)} %get-tuple-element.117), channel_id=1, source_target_pairs={{18,19},{19,16},{16,17},{17,0},{0,1},{1,8},{8,9},{9,24},{24,25},{2... | collective-permute-start | bytes 196616 | tf_op jit(solution)/shard_map/ppermute | solution.py:866
  59.9 1.9 collective-permute-start.11
  62.8 3.8 %collective-permute-start.12 = (f32[64,256]{1,0:T(8,128)S(1)}, f32[64,256]{1,0:T(8,128)S(1)}, u32[]{:S(2)}, u32[]{:S(2)}) collective-permute-start(f32[64,256]{1,0:T(8,128)S(1)} %get-tuple-element.122), channel_id=1, source_target_pairs={{18,19},{19,16},{16,17},{17,0},{0,1},{1,8},{8,9},{9,24},{24,25},{2... | collective-permute-start | bytes 196616 | tf_op jit(solution)/shard_map/ppermute | solution.py:866
  64.7 1.9 collective-permute-start.13
  85.8 3.7 %collective-permute-start.14 = (f32[64,256]{1,0:T(8,128)S(1)}, f32[64,256]{1,0:T(8,128)S(1)}, u32[]{:S(2)}, u32[]{:S(2)}) collective-permute-start(f32[64,256]{1,0:T(8,128)S(1)} %get-tuple-element.128), channel_id=1, source_target_pairs={{18,19},{19,16},{16,17},{17,0},{0,1},{1,8},{8,9},{9,24},{24,25},{2... | collective-permute-start | bytes 196616 | tf_op jit(solution)/shard_map/ppermute | solution.py:866
  86.1 3.4 %collective-permute-start.15 = (f32[64,256]{1,0:T(8,128)S(1)}, f32[64,256]{1,0:T(8,128)S(1)}, u32[]{:S(2)}, u32[]{:S(2)}) collective-permute-start(f32[64,256]{1,0:T(8,128)S(1)} %get-tuple-element.129), channel_id=1, source_target_pairs={{19,18},{16,19},{17,16},{0,17},{1,0},{8,1},{9,8},{24,9},{25,24},{2... | collective-permute-start | bytes 196616 | tf_op jit(solution)/shard_map/ppermute | solution.py:866
  90.5 3.7 %collective-permute-start.16 = (f32[64,256]{1,0:T(8,128)S(1)}, f32[64,256]{1,0:T(8,128)S(1)}, u32[]{:S(2)}, u32[]{:S(2)}) collective-permute-start(f32[64,256]{1,0:T(8,128)S(1)} %get-tuple-element.132), channel_id=1, source_target_pairs={{18,19},{19,16},{16,17},{17,0},{0,1},{1,8},{8,9},{9,24},{24,25},{2... | collective-permute-start | bytes 196616 | tf_op jit(solution)/shard_map/ppermute | solution.py:866
  91.5 3.0 %collective-permute-start.17 = (f32[64,256]{1,0:T(8,128)S(1)}, f32[64,256]{1,0:T(8,128)S(1)}, u32[]{:S(2)}, u32[]{:S(2)}) collective-permute-start(f32[64,256]{1,0:T(8,128)S(1)} %get-tuple-element.133), channel_id=1, source_target_pairs={{19,18},{16,19},{17,16},{0,17},{1,0},{8,1},{9,8},{24,9},{25,24},{2... | collective-permute-start | bytes 196616 | tf_op jit(solution)/shard_map/ppermute | solution.py:866
  95.4 3.8 %collective-permute-start.18 = (f32[64,256]{1,0:T(8,128)S(1)}, f32[64,256]{1,0:T(8,128)S(1)}, u32[]{:S(2)}, u32[]{:S(2)}) collective-permute-start(f32[64,256]{1,0:T(8,128)S(1)} %get-tuple-element.136), channel_id=1, source_target_pairs={{18,19},{19,16},{16,17},{17,0},{0,1},{1,8},{8,9},{9,24},{24,25},{2... | collective-permute-start | bytes 196616 | tf_op jit(solution)/shard_map/ppermute | solution.py:866
  96.4 2.8 %collective-permute-start.19 = (f32[64,256]{1,0:T(8,128)S(1)}, f32[64,256]{1,0:T(8,128)S(1)}, u32[]{:S(2)}, u32[]{:S(2)}) collective-permute-start(f32[64,256]{1,0:T(8,128)S(1)} %get-tuple-element.137), channel_id=1, source_target_pairs={{19,18},{16,19},{17,16},{0,17},{1,0},{8,1},{9,8},{24,9},{25,24},{2... | collective-permute-start | bytes 196616 | tf_op jit(solution)/shard_map/ppermute | solution.py:866
  100.2 3.8 %collective-permute-start.20 = (f32[64,256]{1,0:T(8,128)S(1)}, f32[64,256]{1,0:T(8,128)S(1)}, u32[]{:S(2)}, u32[]{:S(2)}) collective-permute-start(f32[64,256]{1,0:T(8,128)S(1)} %get-tuple-element.140), channel_id=1, source_target_pairs={{18,19},{19,16},{16,17},{17,0},{0,1},{1,8},{8,9},{9,24},{24,25},{2... | collective-permute-start | bytes 196616 | tf_op jit(solution)/shard_map/ppermute | solution.py:866
  101.2 2.8 %collective-permute-start.21 = (f32[64,256]{1,0:T(8,128)S(1)}, f32[64,256]{1,0:T(8,128)S(1)}, u32[]{:S(2)}, u32[]{:S(2)}) collective-permute-start(f32[64,256]{1,0:T(8,128)S(1)} %get-tuple-element.141), channel_id=1, source_target_pairs={{19,18},{16,19},{17,16},{0,17},{1,0},{8,1},{9,8},{24,9},{25,24},{2... | collective-permute-start | bytes 196616 | tf_op jit(solution)/shard_map/ppermute | solution.py:866
  105.0 3.8 %collective-permute-start.22 = (f32[64,256]{1,0:T(8,128)S(1)}, f32[64,256]{1,0:T(8,128)S(1)}, u32[]{:S(2)}, u32[]{:S(2)}) collective-permute-start(f32[64,256]{1,0:T(8,128)S(1)} %get-tuple-element.144), channel_id=1, source_target_pairs={{18,19},{19,16},{16,17},{17,0},{0,1},{1,8},{8,9},{9,24},{24,25},{2... | collective-permute-start | bytes 196616 | tf_op jit(solution)/shard_map/ppermute | solution.py:866
  106.0 2.8 %collective-permute-start.23 = (f32[64,256]{1,0:T(8,128)S(1)}, f32[64,256]{1,0:T(8,128)S(1)}, u32[]{:S(2)}, u32[]{:S(2)}) collective-permute-start(f32[64,256]{1,0:T(8,128)S(1)} %get-tuple-element.145), channel_id=1, source_target_pairs={{19,18},{16,19},{17,16},{0,17},{1,0},{8,1},{9,8},{24,9},{25,24},{2... | collective-permute-start | bytes 196616 | tf_op jit(solution)/shard_map/ppermute | solution.py:866
  109.8 3.8 %collective-permute-start.24 = (f32[64,256]{1,0:T(8,128)S(1)}, f32[64,256]{1,0:T(8,128)S(1)}, u32[]{:S(2)}, u32[]{:S(2)}) collective-permute-start(f32[64,256]{1,0:T(8,128)S(1)} %get-tuple-element.149), channel_id=1, source_target_pairs={{18,19},{19,16},{16,17},{17,0},{0,1},{1,8},{8,9},{9,24},{24,25},{2... | collective-permute-start | bytes 196616 | tf_op jit(solution)/shard_map/ppermute | solution.py:866
  110.8 2.8 %collective-permute-start.25 = (f32[64,256]{1,0:T(8,128)S(1)}, f32[64,256]{1,0:T(8,128)S(1)}, u32[]{:S(2)}, u32[]{:S(2)}) collective-permute-start(f32[64,256]{1,0:T(8,128)S(1)} %get-tuple-element.150), channel_id=1, source_target_pairs={{19,18},{16,19},{17,16},{0,17},{1,0},{8,1},{9,8},{24,9},{25,24},{2... | collective-permute-start | bytes 196616 | tf_op jit(solution)/shard_map/ppermute | solution.py:866
  114.6 3.8 %collective-permute-start.26 = (f32[64,256]{1,0:T(8,128)S(1)}, f32[64,256]{1,0:T(8,128)S(1)}, u32[]{:S(2)}, u32[]{:S(2)}) collective-permute-start(f32[64,256]{1,0:T(8,128)S(1)} %get-tuple-element.153), channel_id=1, source_target_pairs={{18,19},{19,16},{16,17},{17,0},{0,1},{1,8},{8,9},{9,24},{24,25},{2... | collective-permute-start | bytes 196616 | tf_op jit(solution)/shard_map/ppermute | solution.py:866
  115.6 2.8 %collective-permute-start.27 = (f32[64,256]{1,0:T(8,128)S(1)}, f32[64,256]{1,0:T(8,128)S(1)}, u32[]{:S(2)}, u32[]{:S(2)}) collective-permute-start(f32[64,256]{1,0:T(8,128)S(1)} %get-tuple-element.154), channel_id=1, source_target_pairs={{19,18},{16,19},{17,16},{0,17},{1,0},{8,1},{9,8},{24,9},{25,24},{2... | collective-permute-start | bytes 196616 | tf_op jit(solution)/shard_map/ppermute | solution.py:866
  119.4 3.8 %collective-permute-start.28 = (f32[64,256]{1,0:T(8,128)S(1)}, f32[64,256]{1,0:T(8,128)S(1)}, u32[]{:S(2)}, u32[]{:S(2)}) collective-permute-start(f32[64,256]{1,0:T(8,128)S(1)} %get-tuple-element.157), channel_id=1, source_target_pairs={{18,19},{19,16},{16,17},{17,0},{0,1},{1,8},{8,9},{9,24},{24,25},{2... | collective-permute-start | bytes 196616 | tf_op jit(solution)/shard_map/ppermute | solution.py:866
  120.3 2.8 %collective-permute-start.29 = (f32[64,256]{1,0:T(8,128)S(1)}, f32[64,256]{1,0:T(8,128)S(1)}, u32[]{:S(2)}, u32[]{:S(2)}) collective-permute-start(f32[64,256]{1,0:T(8,128)S(1)} %get-tuple-element.158), channel_id=1, source_target_pairs={{19,18},{16,19},{17,16},{0,17},{1,0},{8,1},{9,8},{24,9},{25,24},{2... | collective-permute-start | bytes 196616 | tf_op jit(solution)/shard_map/ppermute | solution.py:866
  124.1 3.8 %collective-permute-start.30 = (f32[64,256]{1,0:T(8,128)S(1)}, f32[64,256]{1,0:T(8,128)S(1)}, u32[]{:S(2)}, u32[]{:S(2)}) collective-permute-start(f32[64,256]{1,0:T(8,128)S(1)} %get-tuple-element.161), channel_id=1, source_target_pairs={{18,19},{19,16},{16,17},{17,0},{0,1},{1,8},{8,9},{9,24},{24,25},{2... | collective-permute-start | bytes 196616 | tf_op jit(solution)/shard_map/ppermute | solution.py:866
  125.1 2.8 %collective-permute-start.31 = (f32[64,256]{1,0:T(8,128)S(1)}, f32[64,256]{1,0:T(8,128)S(1)}, u32[]{:S(2)}, u32[]{:S(2)}) collective-permute-start(f32[64,256]{1,0:T(8,128)S(1)} %get-tuple-element.162), channel_id=1, source_target_pairs={{19,18},{16,19},{17,16},{0,17},{1,0},{8,1},{9,8},{24,9},{25,24},{2... | collective-permute-start | bytes 196616 | tf_op jit(solution)/shard_map/ppermute | solution.py:866
  128.9 3.8 %collective-permute-start.32 = (f32[64,256]{1,0:T(8,128)S(1)}, f32[64,256]{1,0:T(8,128)S(1)}, u32[]{:S(2)}, u32[]{:S(2)}) collective-permute-start(f32[64,256]{1,0:T(8,128)S(1)} %get-tuple-element.166), channel_id=1, source_target_pairs={{18,19},{19,16},{16,17},{17,0},{0,1},{1,8},{8,9},{9,24},{24,25},{2... | collective-permute-start | bytes 196616 | tf_op jit(solution)/shard_map/ppermute | solution.py:866
  129.9 2.8 %collective-permute-start.33 = (f32[64,256]{1,0:T(8,128)S(1)}, f32[64,256]{1,0:T(8,128)S(1)}, u32[]{:S(2)}, u32[]{:S(2)}) collective-permute-start(f32[64,256]{1,0:T(8,128)S(1)} %get-tuple-element.167), channel_id=1, source_target_pairs={{19,18},{16,19},{17,16},{0,17},{1,0},{8,1},{9,8},{24,9},{25,24},{2... | collective-permute-start | bytes 196616 | tf_op jit(solution)/shard_map/ppermute | solution.py:866
  148.0 3.7 %collective-permute-start.34 = (f32[64,256]{1,0:T(8,128)S(1)}, f32[64,256]{1,0:T(8,128)S(1)}, u32[]{:S(2)}, u32[]{:S(2)}) collective-permute-start(f32[64,256]{1,0:T(8,128)S(1)} %get-tuple-element.171), channel_id=1, source_target_pairs={{18,19},{19,16},{16,17},{17,0},{0,1},{1,8},{8,9},{9,24},{24,25},{2... | collective-permute-start | bytes 196616 | tf_op jit(solution)/shard_map/ppermute | solution.py:866
  148.4 3.4 %collective-permute-start.35 = (f32[64,256]{1,0:T(8,128)S(1)}, f32[64,256]{1,0:T(8,128)S(1)}, u32[]{:S(2)}, u32[]{:S(2)}) collective-permute-start(f32[64,256]{1,0:T(8,128)S(1)} %get-tuple-element.172), channel_id=1, source_target_pairs={{19,18},{16,19},{17,16},{0,17},{1,0},{8,1},{9,8},{24,9},{25,24},{2... | collective-permute-start | bytes 196616 | tf_op jit(solution)/shard_map/ppermute | solution.py:866
  152.7 3.7 %collective-permute-start.36 = (f32[64,256]{1,0:T(8,128)S(1)}, f32[64,256]{1,0:T(8,128)S(1)}, u32[]{:S(2)}, u32[]{:S(2)}) collective-permute-start(f32[64,256]{1,0:T(8,128)S(1)} %get-tuple-element.175), channel_id=1, source_target_pairs={{18,19},{19,16},{16,17},{17,0},{0,1},{1,8},{8,9},{9,24},{24,25},{2... | collective-permute-start | bytes 196616 | tf_op jit(solution)/shard_map/ppermute | solution.py:866
  153.7 2.8 %collective-permute-start.37 = (f32[64,256]{1,0:T(8,128)S(1)}, f32[64,256]{1,0:T(8,128)S(1)}, u32[]{:S(2)}, u32[]{:S(2)}) collective-permute-start(f32[64,256]{1,0:T(8,128)S(1)} %get-tuple-element.176), channel_id=1, source_target_pairs={{19,18},{16,19},{17,16},{0,17},{1,0},{8,1},{9,8},{24,9},{25,24},{2... | collective-permute-start | bytes 196616 | tf_op jit(solution)/shard_map/ppermute | solution.py:866
  157.4 3.8 %collective-permute-start.38 = (f32[64,256]{1,0:T(8,128)S(1)}, f32[64,256]{1,0:T(8,128)S(1)}, u32[]{:S(2)}, u32[]{:S(2)}) collective-permute-start(f32[64,256]{1,0:T(8,128)S(1)} %get-tuple-element.179), channel_id=1, source_target_pairs={{18,19},{19,16},{16,17},{17,0},{0,1},{1,8},{8,9},{9,24},{24,25},{2... | collective-permute-start | bytes 196616 | tf_op jit(solution)/shard_map/ppermute | solution.py:866
  158.4 2.8 %collective-permute-start.39 = (f32[64,256]{1,0:T(8,128)S(1)}, f32[64,256]{1,0:T(8,128)S(1)}, u32[]{:S(2)}, u32[]{:S(2)}) collective-permute-start(f32[64,256]{1,0:T(8,128)S(1)} %get-tuple-element.180), channel_id=1, source_target_pairs={{19,18},{16,19},{17,16},{0,17},{1,0},{8,1},{9,8},{24,9},{25,24},{2... | collective-permute-start | bytes 196616 | tf_op jit(solution)/shard_map/ppermute | solution.py:866
  162.2 3.8 %collective-permute-start.40 = (f32[64,256]{1,0:T(8,128)S(1)}, f32[64,256]{1,0:T(8,128)S(1)}, u32[]{:S(2)}, u32[]{:S(2)}) collective-permute-start(f32[64,256]{1,0:T(8,128)S(1)} %get-tuple-element.183), channel_id=1, source_target_pairs={{18,19},{19,16},{16,17},{17,0},{0,1},{1,8},{8,9},{9,24},{24,25},{2... | collective-permute-start | bytes 196616 | tf_op jit(solution)/shard_map/ppermute | solution.py:866
  163.2 2.8 %collective-permute-start.41 = (f32[64,256]{1,0:T(8,128)S(1)}, f32[64,256]{1,0:T(8,128)S(1)}, u32[]{:S(2)}, u32[]{:S(2)}) collective-permute-start(f32[64,256]{1,0:T(8,128)S(1)} %get-tuple-element.184), channel_id=1, source_target_pairs={{19,18},{16,19},{17,16},{0,17},{1,0},{8,1},{9,8},{24,9},{25,24},{2... | collective-permute-start | bytes 196616 | tf_op jit(solution)/shard_map/ppermute | solution.py:866
  167.6 3.7 %collective-permute-start.42 = (f32[64,256]{1,0:T(8,128)S(1)}, f32[64,256]{1,0:T(8,128)S(1)}, u32[]{:S(2)}, u32[]{:S(2)}) collective-permute-start(f32[64,256]{1,0:T(8,128)S(1)} %get-tuple-element.187), channel_id=1, source_target_pairs={{18,19},{19,16},{16,17},{17,0},{0,1},{1,8},{8,9},{9,24},{24,25},{2... | collective-permute-start | bytes 196616 | tf_op jit(solution)/shard_map/ppermute | solution.py:866
  168.6 2.8 %collective-permute-start.43 = (f32[64,256]{1,0:T(8,128)S(1)}, f32[64,256]{1,0:T(8,128)S(1)}, u32[]{:S(2)}, u32[]{:S(2)}) collective-permute-start(f32[64,256]{1,0:T(8,128)S(1)} %get-tuple-element.188), channel_id=1, source_target_pairs={{19,18},{16,19},{17,16},{0,17},{1,0},{8,1},{9,8},{24,9},{25,24},{2... | collective-permute-start | bytes 196616 | tf_op jit(solution)/shard_map/ppermute | solution.py:866
  172.7 19.1 %collective-permute-start.44 = (f32[2,64,256]{2,1,0:T(8,128)S(1)}, f32[2,64,256]{2,1,0:T(8,128)S(1)}, u32[]{:S(2)}, u32[]{:S(2)}) collective-permute-start(f32[2,64,256]{2,1,0:T(8,128)S(1)} %get-tuple-element.191), channel_id=1, source_target_pairs={{18,0},{0,1},{26,2},{10,3},{4,4},{28,5},{14,6},{22,7},{16,8},{8,9}... | collective-permute-start | bytes 393224 | tf_op jit(solution)/shard_map/ppermute | solution.py:954
  175.6 16.3 %collective-permute-start.45 = (f32[2,64,256]{2,1,0:T(8,128)S(1)}, f32[2,64,256]{2,1,0:T(8,128)S(1)}, u32[]{:S(2)}, u32[]{:S(2)}) collective-permute-start(f32[2,64,256]{2,1,0:T(8,128)S(1)} %get-tuple-element.192), channel_id=1, source_target_pairs={{19,0},{1,1},{27,2},{11,3},{5,4},{29,5},{15,6},{23,7},{17,8},{9,9}... | collective-permute-start | bytes 393224 | tf_op jit(solution)/shard_map/ppermute | solution.py:954
  178.3 13.6 %collective-permute-start.46 = (f32[2,64,256]{2,1,0:T(8,128)S(1)}, f32[2,64,256]{2,1,0:T(8,128)S(1)}, u32[]{:S(2)}, u32[]{:S(2)}) collective-permute-start(f32[2,64,256]{2,1,0:T(8,128)S(1)} %get-tuple-element.193), channel_id=1, source_target_pairs={{16,0},{8,1},{24,2},{2,3},{12,4},{30,5},{6,6},{20,7},{18,8},{0,9},... | collective-permute-start | bytes 393224 | tf_op jit(solution)/shard_map/ppermute | solution.py:954
  180.2 11.6 %collective-permute-start.47 = (f32[2,64,256]{2,1,0:T(8,128)S(1)}, f32[2,64,256]{2,1,0:T(8,128)S(1)}, u32[]{:S(2)}, u32[]{:S(2)}) collective-permute-start(f32[2,64,256]{2,1,0:T(8,128)S(1)} %get-tuple-element.194), channel_id=1, source_target_pairs={{17,0},{9,1},{25,2},{3,3},{13,4},{31,5},{7,6},{21,7},{19,8},{1,9},... | collective-permute-start | bytes 393224 | tf_op jit(solution)/shard_map/ppermute | solution.py:954
  (11 other events, 170.0 us)

commit v3 on v2

--- a/solution.py
+++ b/solution.py
@@ -394,7 +394,15 @@
                 part[ring[gx_count * j + row[i]], q] = i
         for s in range(gx_count):
             group[ring[gx_count * j + s]] = j
-    return ring, send, part, group
+    codes = group.astype(np.int64) << 24
+    for q in range(gx_count):
+        codes |= (send[:, q] << 2 * q) | (part[:, q] << 8 + 2 * q)
+        codes |= np.argsort(send, axis=1)[:, q] << 16 + 2 * q
+    return ring, send, group, [int(c) for c in codes]
+
+
+def field_of(code, at):
+    return lax.shift_right_logical(code, jnp.int32(at)) & 3
 
 
 def split_bf16(values):
@@ -562,65 +570,107 @@
         out_ref[pl.ds(base + NODES - 1, face, stride=NODES), :] = jnp.where(
             layer < ez_count - 1, below, 0.0
         )
-        low_ref[:, span] = out_ref[base : base + face]
-        high_ref[:, span] = out_ref[base + rows - face : base + rows]
-
-
-def joined(w_ref, from_prev_ref, from_next_ref, scale):
-    face = from_prev_ref.shape[0]
+        low = out_ref[base : base + face]
+        high = out_ref[base + rows - face : base + rows]
+        low_ref[:, span] = low
+        high_ref[:, span] = high
+
+
+def joined(w_ref, below_ref, above_ref, scale):
+    face = below_ref.shape[0]
     rows = w_ref.shape[0] // 2
     field = lane_halves(w_ref)
-    low = field[:face] + from_prev_ref[...]
-    high = field[rows - face :] + from_next_ref[...]
+    low = field[:face] + below_ref[...]
+    high = field[rows - face :] + above_ref[...]
     if scale != 1.0:
         low = low * scale
         high = high * scale
     return jnp.concatenate([low, field[face : rows - face], high], axis=0)
 
 
-def pack_kernel(*refs):
-    (place_ref, count_ref, source_ref, geometry_ref, disc_ref, thrust_ref, factor_ref,
-     q0, q1, q2, q3) = refs
-    parts, nodes_rows, lanes = source_ref.shape
+def pack_kernel(cols, codes, *refs):
+    (device_ref, count_ref, source_hbm, geometry_hbm, disc_hbm, thrust_hbm, factor_hbm,
+     q0, q1, q2, q3, place_hbm,
+     held, geometry_ref, disc_ref, thrust_ref, factor_ref, place_ref, sems, row_sems) = refs
+    parts = 4
+    _, nodes, elem_x, _, lanes = source_hbm.shape
+    face = nodes * nodes
+    nodes_rows = elem_x * face
+    copies = [
+        pltpu.make_async_copy(hbm, ref, sems.at[i])
+        for i, (hbm, ref) in enumerate(
+            (
+                (geometry_hbm, geometry_ref),
+                (disc_hbm, disc_ref),
+                (thrust_hbm, thrust_ref),
+                (factor_hbm, factor_ref),
+            )
+        )
+    ]
+    for copy in copies:
+        copy.start()
+    row_copies = []
+    for ey in range(parts):
+        for ex in range(elem_x):
+            for b in range(nodes):
+                row = ex * face + b * nodes
+                row_copies.append(
+                    pltpu.make_async_copy(
+                        source_hbm.at[:, b, ex, ey, :],
+                        held.at[ey, row : row + nodes, :],
+                        row_sems.at[len(row_copies)],
+                    )
+                )
+    for copy in row_copies:
+        copy.start()
+    code = jnp.int32(codes[0])
+    for d in range(1, len(codes)):
+        code = jnp.where(device_ref[0] == d, jnp.int32(codes[d]), code)
+    place_ref[...] = jnp.full(place_ref.shape, code, jnp.int32)
     levels = count_ref.shape[0]
-    count = factor_ref.shape[0]
-    cols = count // levels
-    span = factor_ref.shape[1] // (8 * parts)
     lane = lax.broadcasted_iota(jnp.int32, (1, lanes), 1)
     limit = jnp.zeros((1, lanes), jnp.int32)
     for l in range(levels):
-        limit = jnp.where(lane // cols == l, count_ref[l, 0], limit)
+        limit = jnp.where(lane // cols == l, count_ref[l], limit)
     live = jnp.where(lax.rem(lane, cols) < limit, 1.0, 0.0).astype(f32)
+    for copy in copies:
+        copy.wait()
     push = disc_ref[...].astype(f32) * thrust_ref[...]
     ez_count = push.shape[2]
     blank = jnp.zeros((1, lanes - 2 * ez_count), f32)
-
-    def fill(ref, ey):
-        ref[:nodes_rows] = source_ref[ey]
-        for c in range(3):
-            ref[nodes_rows + c : nodes_rows + c + 1] = jnp.concatenate(
-                [geometry_ref[c, ex, ey : ey + 1] for ex in range(2)] + [blank], axis=1
-            )
-        ref[nodes_rows + 3 : nodes_rows + 4] = jnp.concatenate(
-            [push[ex, ey : ey + 1] for ex in range(2)] + [blank], axis=1
-        )
-        ref[nodes_rows + 4 : nodes_rows + 5] = live
-        ref[nodes_rows + 5 : nodes_rows + 8] = jnp.zeros((3, lanes), f32)
+    count = factor_ref.shape[0]
+    span = factor_ref.shape[1] // (8 * parts)
+    for ey in range(parts):
+        pieces = [
+            jnp.concatenate([geometry_ref[c, ex, ey : ey + 1] for ex in range(2)] + [blank], 1)
+            for c in range(3)
+        ]
+        pieces.append(jnp.concatenate([push[ex, ey : ey + 1] for ex in range(2)] + [blank], 1))
+        pieces.append(live)
+        pieces.append(jnp.zeros((3, lanes), f32))
+        held[ey, nodes_rows : nodes_rows + 8] = jnp.concatenate(pieces, axis=0)
         for pair in range(4):
             at = [(2 * pair + k) * parts * span + ey * span for k in range(2)]
             base = nodes_rows + 8 + (pair // 2) * count
             column = (pair % 2) * 2 * span
-            ref[base : base + count, column : column + 2 * span] = jnp.concatenate(
+            held[ey, base : base + count, column : column + 2 * span] = jnp.concatenate(
                 [factor_ref[:, start : start + span] for start in at], axis=1
             )
-
-    for q, ref in enumerate((q0, q1, q2, q3)):
-        for ey in range(parts):
-            pl.when(place_ref[q] == ey)(functools.partial(fill, ref, ey))
+    for copy in row_copies:
+        copy.wait()
+    outs = [
+        pltpu.make_async_copy(held.at[field_of(code, 2 * q)], ref, sems.at[4 + q])
+        for q, ref in enumerate((q0, q1, q2, q3))
+    ]
+    outs.append(pltpu.make_async_copy(place_ref, place_hbm, sems.at[8]))
+    for copy in outs:
+        copy.start()
+    for copy in outs:
+        copy.wait()
 
 
 def message_part(base_ref, q):
-    return base_ref[4 + q]
+    return field_of(base_ref[0, 0], 8 + 2 * q)
 
 
 def factor_block(ref, count, vu):
@@ -678,13 +728,13 @@
 
 def precond_kernel(ez_count, first, *refs):
     if first:
-        (w_ref, prev_ref, next_ref, fwd_ref, bwd_ref, inv_ref,
+        (w_ref, below_ref, above_ref, fwd_ref, bwd_ref, inv_ref,
          r_ref, u_ref, low_ref, high_ref) = refs
-        resid = joined(w_ref, prev_ref, next_ref, 1.0)
+        resid = joined(w_ref, below_ref, above_ref, 1.0)
     else:
-        (w_ref, prev_ref, next_ref, r_in_ref, fwd_ref, bwd_ref, inv_ref,
+        (w_ref, below_ref, above_ref, r_in_ref, fwd_ref, bwd_ref, inv_ref,
          r_ref, u_ref, low_ref, high_ref) = refs
-        resid = r_in_ref[...] - joined(w_ref, prev_ref, next_ref, 1.0)
+        resid = r_in_ref[...] - joined(w_ref, below_ref, above_ref, 1.0)
     r_ref[...] = resid
     field = spectral_apply(resid, fwd_ref, bwd_ref, inv_ref)
     assemble_local(field, u_ref, low_ref, high_ref, ez_count, True)
@@ -692,9 +742,9 @@
 
 def apply_kernel(ez_count, keep, gain, start, keep_d, *refs):
     refs = list(refs)
-    w_ref, prev_ref, next_ref = refs[:3]
+    w_ref, below_ref, above_ref = refs[:3]
     refs = refs[3:]
-    step = joined(w_ref, prev_ref, next_ref, 0.5)
+    step = joined(w_ref, below_ref, above_ref, 0.5)
     if gain != 1.0:
         step = step * gain
     if keep != 0.0:
@@ -711,12 +761,12 @@
 
 
 def restrict_kernel(ez_count, count, *refs):
-    (place_ref, w_ref, prev_ref, next_ref, r_in_ref, restrict_ref, swaps_ref, x0, x1, x2, x3,
+    (place_ref, w_ref, below_ref, above_ref, r_in_ref, restrict_ref, swaps_ref, x0, x1, x2, x3,
      r_ref, part_ref, coarse, sums) = refs
     lanes = 2 * w_ref.shape[1]
     parts = 4
     width = lanes // parts
-    resid = r_in_ref[...] - joined(w_ref, prev_ref, next_ref, 1.0)
+    resid = r_in_ref[...] - joined(w_ref, below_ref, above_ref, 1.0)
     r_ref[...] = resid
     rows = hp_dot(restrict_ref[...], resid)
     b = rows[:8] + jnp.where(lane_layer((8, lanes), ez_count) == 0, rows[8:], 0.0)
@@ -755,7 +805,7 @@
     row_id = lax.broadcasted_iota(jnp.int32, all_ref.shape[1:], 0)
     lane_id = lax.broadcasted_iota(jnp.int32, all_ref.shape[1:], 1)
     level = (lax.rem(row_id, 2) * 128 + lane_id) // cols
-    mine = lax.shift_right_logical(jnp.full_like(level, place_ref[8]), level)
+    mine = lax.shift_right_logical(jnp.full_like(level, lax.shift_right_logical(place_ref[0, 0], 24)), level)
     base = jnp.zeros(all_ref.shape[1:], f32)
     for source in range(all_ref.shape[0]):
         theirs = lax.shift_right_logical(jnp.full_like(level, groups[source]), level)
@@ -793,14 +843,14 @@
 
 
 def exit_kernel(keep, gain, *refs):
-    (place_ref, w_ref, prev_ref, next_ref, d_ref, x_ref, columns_ref, gather_ref,
+    (place_ref, w_ref, below_ref, above_ref, d_ref, x_ref, columns_ref, gather_ref,
      q0, q1, q2, q3, field, held) = refs
     lanes = 2 * w_ref.shape[1]
     parts = 4
     width = lanes // parts
-    face = prev_ref.shape[0]
+    face = below_ref.shape[0]
     rows = x_ref.shape[0]
-    step = joined(w_ref, prev_ref, next_ref, 0.5) * gain + keep * d_ref[...]
+    step = joined(w_ref, below_ref, above_ref, 0.5) * gain + keep * d_ref[...]
     store_halves(field, (x_ref[...] + step) * columns_ref[:, 4:5])
     blocks = []
     for side in range(2):
@@ -818,14 +868,12 @@
         ref[...] = held[message_part(place_ref, q)]
 
 
-def call(kernel, name, out_shapes, args, scratch=(), smem_args=0):
-    specs = [pl.BlockSpec(memory_space=SMEM)] * smem_args
-    specs += [pl.BlockSpec(memory_space=VMEM)] * (len(args) - smem_args)
+def call(kernel, name, out_shapes, args, scratch=()):
     return pl.pallas_call(
         kernel,
         name=name,
         out_shape=[jax.ShapeDtypeStruct(s, f32) for s in out_shapes],
-        in_specs=specs,
+        in_specs=[pl.BlockSpec(memory_space=VMEM)] * len(args),
         out_specs=[pl.BlockSpec(memory_space=VMEM)] * len(out_shapes),
         scratch_shapes=list(scratch),
         compiler_params=pltpu.CompilerParams(vmem_limit_bytes=12 * 1024 * 1024),
@@ -845,13 +893,9 @@
     face = nodes * nodes
     devices = gx_count * gy_count
     tables = {k: jnp.asarray(v) for k, v in constant_tables(ez_count, lanes).items()}
-    ring, send, part, group = placement(gx_count, gy_count)
+    ring, send, group, codes = placement(gx_count, gy_count)
     groups = [int(g) for g in group]
-    facts = np.concatenate([send, part, group[:, None], np.argsort(send, axis=1)], axis=1)
     device = lax.axis_index("gx") * gy_count + lax.axis_index("gy")
-    place = lax.dynamic_index_in_dim(
-        jnp.asarray(facts.astype(np.int32)), device, 0, keepdims=False
-    )
     up = [(ring[i], ring[(i + 1) % devices]) for i in range(devices)]
     down = [(target, origin) for origin, target in up]
 
@@ -866,13 +910,29 @@
         return lax.ppermute(high, axes, up), lax.ppermute(low, axes, down)
 
     count = levels * cols
-    moved = source.transpose(3, 2, 1, 0, 4).reshape(elem_y, elem_x * face, z_count)
     message = (elem_x * face + 8 + 2 * count, z_count)
-    packed = call(
-        pack_kernel, "pack", [message] * parts,
-        [place, col_count, moved, geometry, disc_mask, thrust,
-         xxt_factor.reshape(count, -1)],
-        (), 2,
+    spec = lambda space: pl.BlockSpec(memory_space=space)
+    *packed, place = pl.pallas_call(
+        functools.partial(pack_kernel, cols, codes),
+        name="pack",
+        out_shape=[jax.ShapeDtypeStruct(message, f32)] * parts
+        + [jax.ShapeDtypeStruct((8, 128), jnp.int32)],
+        in_specs=[spec(SMEM)] * 2 + [spec(pl.ANY)] * 5,
+        out_specs=[spec(pl.ANY)] * (parts + 1),
+        scratch_shapes=[
+            VMEM((parts,) + message, f32),
+            VMEM(geometry.shape, f32),
+            VMEM(disc_mask.shape, jnp.int32),
+            VMEM(thrust.shape, f32),
+            VMEM((count, xxt_factor.shape[2]), f32),
+            VMEM((8, 128), jnp.int32),
+            pltpu.SemaphoreType.DMA((2 * parts + 1,)),
+            pltpu.SemaphoreType.DMA((elem_y * elem_x * nodes,)),
+        ],
+        compiler_params=pltpu.CompilerParams(vmem_limit_bytes=67043328),
+    )(
+        jnp.reshape(device, (1,)), col_count.reshape(levels), source, geometry, disc_mask, thrust,
+        xxt_factor.reshape(count, -1),
     )
     received = [lax.ppermute(packed[q], axes, spread(q)) for q in range(parts)]
     inner_levels = gy_count.bit_length() - 1
@@ -884,7 +944,7 @@
         functools.partial(entry_kernel, ez_count), "entry",
         [sshape, hshape, hshape, fshape, fshape, (2 * parts, 128)],
         [place, *received, tables["columns"], tables["deal"]],
-        [VMEM((parts, 2 * face + 8, z_count), f32)], 1,
+        [VMEM((parts, 2 * face + 8, z_count), f32)],
     )
     fwd, bwd = tables["forward"], tables["backward"]
 
@@ -927,7 +987,7 @@
             functools.partial(restrict_kernel, ez_count, count), "restrict",
             [fshape, (devices, 2 * parts, 128)],
             [place, k, prev, nxt, resid, tables["restrict"], tables["swaps"], *received],
-            [VMEM((parts, 8, 2 * width), f32), VMEM((parts, 256, 2 * width), f32)], 1,
+            [VMEM((parts, 8, 2 * width), f32), VMEM((parts, 256, 2 * width), f32)],
         )
         everyone = lax.all_to_all(partial, axes, 0, 0)
         f, low, high = call(
@@ -935,7 +995,7 @@
             [sshape, hshape, hshape],
             [place, everyone, live_tile, tables["swaps"], tables["columns"],
              *received],
-            [VMEM((parts, 256, 2 * width), f32), VMEM((parts, 8, 2 * width), f32)], 1,
+            [VMEM((parts, 256, 2 * width), f32), VMEM((parts, 8, 2 * width), f32)],
         )
         x, k, low, high, _ = advance(f, low, high, None, x, 0.0, 1.0, False)
         resid, u, low, high = precond(k, low, high, resid)
@@ -948,7 +1008,7 @@
         functools.partial(exit_kernel, keep, gain), "exit",
         [(2, face, z_count)] * parts,
         [place, u, prev, nxt, d, x, tables["columns"], tables["gather"]],
-        [VMEM(sshape, f32), VMEM((parts, 2, face, z_count), f32)], 1,
+        [VMEM(sshape, f32), VMEM((parts, 2, face, z_count), f32)],
     )
     back = [
         lax.ppermute(chunks[q], axes, [(t, s) for s, t in spread(q)]) for q in range(parts)
@@ -956,7 +1016,7 @@
     stacked = jnp.stack(back)
     by_ey = jnp.stack(
         [
-            lax.dynamic_index_in_dim(stacked, place[9 + ey], 0, keepdims=False)
+            lax.dynamic_index_in_dim(stacked, field_of(place[0, 0], 16 + 2 * ey), 0, keepdims=False)
             for ey in range(parts)
         ]
     )

time: 194 us -> 187 us (0.964)
  between operations: 7.82 us -> 2.9 us
  local copies, waits for them, and re-layouts: 8.21 us -> 4.4 us
    pallas_call x0 -> x1, Pallas kernels: none -> 4.68 us  [fast_device(): pl.pallas_call(functools.partial(pack_kernel, cols, codes), name='pack',...]
    pallas_call x24 -> x23, Pallas kernels: 30.8 us -> 26.1 us  [call(): pl.pallas_call(kernel, name=name, out_shape=[jax.ShapeDtypeStruct(s, f32)...]
    unnamed x23 -> x20, local copies, waits for them, and re-layouts: 4.26 us -> 2.71 us
where the time goes in v3:
time: 187 us; the launch traced here: 185 us
  starting transfers between devices  66 us (35%)
  waiting for transfers between devices  55.8 us (30%)
  Pallas kernels  30.8 us (16%)
  blocking collectives  25.3 us (14%)
  local copies, waits for them, and re-layouts  4.4 us (2%)
  between operations  2.9 us (2%)
    ppermute x40, starting transfers between devices, halo(): return (lax.ppermute(high, axes, up), lax.ppermute(low, axes, down))  41.5 us
    ppermute x40, waiting for transfers between devices, halo(): return (lax.ppermute(high, axes, up), lax.ppermute(low, axes, down))  38.2 us
    pallas_call x23, Pallas kernels, call(): pl.pallas_call(kernel, name=name, out_shape=[jax.ShapeDtypeStruct(s, f32)...  26.1 us
    all_to_all x2, blocking collectives, fast_device(): everyone = lax.all_to_all(partial, axes, 0, 0)  25.3 us
    ppermute x4, waiting for transfers between devices, fast_device(): received = [lax.ppermute(packed[q], axes, spread(q)) for q in range(parts)]  17 us
    ppermute x4, starting transfers between devices, fast_device(): received = [lax.ppermute(packed[q], axes, spread(q)) for q in range(parts)]  13.5 us
    ppermute x4, starting transfers between devices, fast_device(): lax.ppermute(chunks[q], axes, [(t, s) for s, t in spread(q)])  10.9 us
    pallas_call x1, Pallas kernels, fast_device(): pl.pallas_call(functools.partial(pack_kernel, cols, codes), name='pack',...  4.68 us
  transfers between devices with their start and end apart: 48, of which 27 were waited for; matrix products, arithmetic and copies ran while one was open for 0% of the time, Pallas kernels for 0%

profile of v3, /device:TPU:0, one launch (start us, length us, event | category | flops | bytes accessed | tf_op | source)
XLA Modules:
  0.0 185.3 jit_solution(16235575816655883146)
XLA Ops:
  0.0 4.7 %pack.1 = (f32[520,256]{1,0:T(8,128)}, f32[520,256]{1,0:T(8,128)}, f32[520,256]{1,0:T(8,128)}, f32[520,256]{1,0:T(8,128)}, s32[8,128]{1,0:T(8,128)}) custom-call(s32[1]{0:T(128)} %bitcast.refs_0_, s32[6]{0:T(128)} %bitcast.21, f32[8,8,2,4,256]{4,3,2,1,0:T(4,128)} %refs_2_.1, f32[3,2,4,32]{3,2,1,0:T(4,128)} %refs_3_.5, s32[2,4,32]{2,1,0:T(4,128)} %refs_4_.17, ...), custom_call_target="tpu_custom_call" | custom-call | tf_op jit(solution)/shard_map/pack/pallas_call | solution.py:915
  4.7 6.0 %collective-permute-start = (f32[520,256]{1,0:T(8,128)}, f32[520,256]{1,0:T(8,128)S(1)}, u32[]{:S(2)}, u32[]{:S(2)}) collective-permute-start(f32[520,256]{1,0:T(8,128)} %get-tuple-element.102), channel_id=1, source_target_pairs={{0,18},{1,0},{2,26},{3,10},{4,4},{5,28},{6,14},{7,22},{8,16},{9,8}... | collective-permute-start | bytes 1597448 | tf_op jit(solution)/shard_map/ppermute | solution.py:937
  10.8 1.9 %collective-permute-start.1 = (f32[520,256]{1,0:T(8,128)}, f32[520,256]{1,0:T(8,128)S(1)}, u32[]{:S(2)}, u32[]{:S(2)}) collective-permute-start(f32[520,256]{1,0:T(8,128)} %get-tuple-element.103), channel_id=1, source_target_pairs={{0,19},{1,1},{2,27},{3,11},{4,5},{5,29},{6,15},{7,23},{8,17},{9,9}... | collective-permute-start | bytes 1597448 | tf_op jit(solution)/shard_map/ppermute | solution.py:937
  12.7 3.3 %collective-permute-start.2 = (f32[520,256]{1,0:T(8,128)}, f32[520,256]{1,0:T(8,128)S(1)}, u32[]{:S(2)}, u32[]{:S(2)}) collective-permute-start(f32[520,256]{1,0:T(8,128)} %get-tuple-element.104), channel_id=1, source_target_pairs={{0,16},{1,8},{2,24},{3,2},{4,12},{5,30},{6,6},{7,20},{8,18},{9,0},... | collective-permute-start | bytes 1597448 | tf_op jit(solution)/shard_map/ppermute | solution.py:937
  16.0 2.3 %collective-permute-start.3 = (f32[520,256]{1,0:T(8,128)}, f32[520,256]{1,0:T(8,128)S(1)}, u32[]{:S(2)}, u32[]{:S(2)}) collective-permute-start(f32[520,256]{1,0:T(8,128)} %get-tuple-element.105), channel_id=1, source_target_pairs={{0,17},{1,9},{2,25},{3,3},{4,13},{5,31},{6,7},{7,21},{8,19},{9,1},... | collective-permute-start | bytes 1597448 | tf_op jit(solution)/shard_map/ppermute | solution.py:937
  18.3 10.3 %collective-permute-done.1.refs_2_.refs_8_.refs_6_ = f32[520,256]{1,0:T(8,128)S(1)} collective-permute-done((f32[520,256]{1,0:T(8,128)}, f32[520,256]{1,0:T(8,128)S(1)}, u32[]{:S(2)}, u32[]{:S(2)}) %collective-permute-start.1) | collective-permute-done | bytes 532512 | tf_op jit(solution)/shard_map/ppermute | solution.py:937
  29.2 6.0 %collective-permute-done.3.refs_4_.refs_10_.refs_8_ = f32[520,256]{1,0:T(8,128)S(1)} collective-permute-done((f32[520,256]{1,0:T(8,128)}, f32[520,256]{1,0:T(8,128)S(1)}, u32[]{:S(2)}, u32[]{:S(2)}) %collective-permute-start.3) | collective-permute-done | bytes 532512 | tf_op jit(solution)/shard_map/ppermute | solution.py:937
  36.2 1.0 copy-done.6
  37.9 1.4 entry.1
  39.3 3.6 %collective-permute-start.4 = (f32[64,256]{1,0:T(8,128)S(1)}, f32[64,256]{1,0:T(8,128)S(1)}, u32[]{:S(2)}, u32[]{:S(2)}) collective-permute-start(f32[64,256]{1,0:T(8,128)S(1)} %get-tuple-element.107), channel_id=1, source_target_pairs={{18,19},{19,16},{16,17},{17,0},{0,1},{1,8},{8,9},{9,24},{24,25},{2... | collective-permute-start | bytes 196616 | tf_op jit(solution)/shard_map/ppermute | solution.py:910
  45.8 2.3 %collective-permute-start.6 = (f32[64,256]{1,0:T(8,128)S(1)}, f32[64,256]{1,0:T(8,128)S(1)}, u32[]{:S(2)}, u32[]{:S(2)}) collective-permute-start(f32[64,256]{1,0:T(8,128)S(1)} %get-tuple-element.111), channel_id=1, source_target_pairs={{18,19},{19,16},{16,17},{17,0},{0,1},{1,8},{8,9},{9,24},{24,25},{2... | collective-permute-start | bytes 196616 | tf_op jit(solution)/shard_map/ppermute | solution.py:910
  48.1 1.5 collective-permute-done.6.refs_1_
  51.0 1.9 %collective-permute-start.8 = (f32[64,256]{1,0:T(8,128)S(1)}, f32[64,256]{1,0:T(8,128)S(1)}, u32[]{:S(2)}, u32[]{:S(2)}) collective-permute-start(f32[64,256]{1,0:T(8,128)S(1)} %get-tuple-element.115), channel_id=1, source_target_pairs={{18,19},{19,16},{16,17},{17,0},{0,1},{1,8},{8,9},{9,24},{24,25},{2... | collective-permute-start | bytes 196616 | tf_op jit(solution)/shard_map/ppermute | solution.py:910
  52.9 1.9 %collective-permute-done.8.refs_1_ = f32[64,256]{1,0:T(8,128)S(1)} collective-permute-done((f32[64,256]{1,0:T(8,128)S(1)}, f32[64,256]{1,0:T(8,128)S(1)}, u32[]{:S(2)}, u32[]{:S(2)}) %collective-permute-start.8) | collective-permute-done | bytes 65568 | tf_op jit(solution)/shard_map/ppermute | solution.py:910
  55.8 3.5 %collective-permute-start.10 = (f32[64,256]{1,0:T(8,128)S(1)}, f32[64,256]{1,0:T(8,128)S(1)}, u32[]{:S(2)}, u32[]{:S(2)}) collective-permute-start(f32[64,256]{1,0:T(8,128)S(1)} %get-tuple-element.119), channel_id=1, source_target_pairs={{18,19},{19,16},{16,17},{17,0},{0,1},{1,8},{8,9},{9,24},{24,25},{2... | collective-permute-start | bytes 196616 | tf_op jit(solution)/shard_map/ppermute | solution.py:910
  62.2 1.9 %collective-permute-start.12 = (f32[64,256]{1,0:T(8,128)S(1)}, f32[64,256]{1,0:T(8,128)S(1)}, u32[]{:S(2)}, u32[]{:S(2)}) collective-permute-start(f32[64,256]{1,0:T(8,128)S(1)} %get-tuple-element.124), channel_id=1, source_target_pairs={{18,19},{19,16},{16,17},{17,0},{0,1},{1,8},{8,9},{9,24},{24,25},{2... | collective-permute-start | bytes 196616 | tf_op jit(solution)/shard_map/ppermute | solution.py:910
  64.1 1.9 %collective-permute-done.12.refs_2_ = f32[64,256]{1,0:T(8,128)S(1)} collective-permute-done((f32[64,256]{1,0:T(8,128)S(1)}, f32[64,256]{1,0:T(8,128)S(1)}, u32[]{:S(2)}, u32[]{:S(2)}) %collective-permute-start.12) | collective-permute-done | bytes 65568 | tf_op jit(solution)/shard_map/ppermute | solution.py:910
  66.0 1.8 restrict.2
  67.8 14.6 %all_to_all.10.refs_1_ = f32[32,8,128]{2,1,0:T(8,128)S(1)} all-to-all(f32[32,8,128]{2,1,0:T(8,128)S(1)} %get-tuple-element.127), channel_id=1, replica_groups=mesh['gx'=4,'gy'=8] {'gx','gy'}, dimensions={0} | all-to-all | bytes 262144 | tf_op jit(solution)/shard_map/all_to_all | solution.py:992
  82.4 1.6 prolong.2
  84.4 1.4 collective-permute-start.15
  85.9 1.9 %collective-permute-done.14.refs_1_ = f32[64,256]{1,0:T(8,128)S(1)} collective-permute-done((f32[64,256]{1,0:T(8,128)S(1)}, f32[64,256]{1,0:T(8,128)S(1)}, u32[]{:S(2)}, u32[]{:S(2)}) %collective-permute-start.14) | collective-permute-done | bytes 65568 | tf_op jit(solution)/shard_map/ppermute | solution.py:910
  90.6 1.9 %collective-permute-done.16.refs_1_ = f32[64,256]{1,0:T(8,128)S(1)} collective-permute-done((f32[64,256]{1,0:T(8,128)S(1)}, f32[64,256]{1,0:T(8,128)S(1)}, u32[]{:S(2)}, u32[]{:S(2)}) %collective-permute-start.16) | collective-permute-done | bytes 65568 | tf_op jit(solution)/shard_map/ppermute | solution.py:910
  93.5 1.0 collective-permute-start.18
  95.4 1.9 %collective-permute-done.18.refs_1_ = f32[64,256]{1,0:T(8,128)S(1)} collective-permute-done((f32[64,256]{1,0:T(8,128)S(1)}, f32[64,256]{1,0:T(8,128)S(1)}, u32[]{:S(2)}, u32[]{:S(2)}) %collective-permute-start.18) | collective-permute-done | bytes 65568 | tf_op jit(solution)/shard_map/ppermute | solution.py:910
  100.2 1.9 %collective-permute-done.20.refs_1_ = f32[64,256]{1,0:T(8,128)S(1)} collective-permute-done((f32[64,256]{1,0:T(8,128)S(1)}, f32[64,256]{1,0:T(8,128)S(1)}, u32[]{:S(2)}, u32[]{:S(2)}) %collective-permute-start.20) | collective-permute-done | bytes 65568 | tf_op jit(solution)/shard_map/ppermute | solution.py:910
  103.0 1.2 collective-permute-start.22
  105.1 1.9 %collective-permute-done.22.refs_1_ = f32[64,256]{1,0:T(8,128)S(1)} collective-permute-done((f32[64,256]{1,0:T(8,128)S(1)}, f32[64,256]{1,0:T(8,128)S(1)}, u32[]{:S(2)}, u32[]{:S(2)}) %collective-permute-start.22) | collective-permute-done | bytes 65568 | tf_op jit(solution)/shard_map/ppermute | solution.py:910
  109.9 1.9 %collective-permute-done.24.refs_1_ = f32[64,256]{1,0:T(8,128)S(1)} collective-permute-done((f32[64,256]{1,0:T(8,128)S(1)}, f32[64,256]{1,0:T(8,128)S(1)}, u32[]{:S(2)}, u32[]{:S(2)}) %collective-permute-start.24) | collective-permute-done | bytes 65568 | tf_op jit(solution)/shard_map/ppermute | solution.py:910
  114.7 1.9 %collective-permute-done.26.refs_1_ = f32[64,256]{1,0:T(8,128)S(1)} collective-permute-done((f32[64,256]{1,0:T(8,128)S(1)}, f32[64,256]{1,0:T(8,128)S(1)}, u32[]{:S(2)}, u32[]{:S(2)}) %collective-permute-start.26) | collective-permute-done | bytes 65568 | tf_op jit(solution)/shard_map/ppermute | solution.py:910
  119.5 1.9 %collective-permute-done.28.refs_1_ = f32[64,256]{1,0:T(8,128)S(1)} collective-permute-done((f32[64,256]{1,0:T(8,128)S(1)}, f32[64,256]{1,0:T(8,128)S(1)}, u32[]{:S(2)}, u32[]{:S(2)}) %collective-permute-start.28) | collective-permute-done | bytes 65568 | tf_op jit(solution)/shard_map/ppermute | solution.py:910
  124.2 1.9 %collective-permute-done.30.refs_1_ = f32[64,256]{1,0:T(8,128)S(1)} collective-permute-done((f32[64,256]{1,0:T(8,128)S(1)}, f32[64,256]{1,0:T(8,128)S(1)}, u32[]{:S(2)}, u32[]{:S(2)}) %collective-permute-start.30) | collective-permute-done | bytes 65568 | tf_op jit(solution)/shard_map/ppermute | solution.py:910
  129.0 1.9 %collective-permute-done.32.refs_2_ = f32[64,256]{1,0:T(8,128)S(1)} collective-permute-done((f32[64,256]{1,0:T(8,128)S(1)}, f32[64,256]{1,0:T(8,128)S(1)}, u32[]{:S(2)}, u32[]{:S(2)}) %collective-permute-start.32) | collective-permute-done | bytes 65568 | tf_op jit(solution)/shard_map/ppermute | solution.py:910
  130.9 1.8 restrict.3
  132.7 10.7 %all_to_all.11.refs_1_ = f32[32,8,128]{2,1,0:T(8,128)S(1)} all-to-all(f32[32,8,128]{2,1,0:T(8,128)S(1)} %get-tuple-element.171), channel_id=1, replica_groups=mesh['gx'=4,'gy'=8] {'gx','gy'}, dimensions={0} | all-to-all | bytes 262144 | tf_op jit(solution)/shard_map/all_to_all | solution.py:992
  143.4 1.6 prolong.3
  145.4 1.4 collective-permute-start.35
  146.9 1.9 %collective-permute-done.34.refs_1_ = f32[64,256]{1,0:T(8,128)S(1)} collective-permute-done((f32[64,256]{1,0:T(8,128)S(1)}, f32[64,256]{1,0:T(8,128)S(1)}, u32[]{:S(2)}, u32[]{:S(2)}) %collective-permute-start.34) | collective-permute-done | bytes 65568 | tf_op jit(solution)/shard_map/ppermute | solution.py:910
  151.7 1.9 %collective-permute-done.36.refs_1_ = f32[64,256]{1,0:T(8,128)S(1)} collective-permute-done((f32[64,256]{1,0:T(8,128)S(1)}, f32[64,256]{1,0:T(8,128)S(1)}, u32[]{:S(2)}, u32[]{:S(2)}) %collective-permute-start.36) | collective-permute-done | bytes 65568 | tf_op jit(solution)/shard_map/ppermute | solution.py:910
  156.4 1.9 %collective-permute-done.38.refs_1_ = f32[64,256]{1,0:T(8,128)S(1)} collective-permute-done((f32[64,256]{1,0:T(8,128)S(1)}, f32[64,256]{1,0:T(8,128)S(1)}, u32[]{:S(2)}, u32[]{:S(2)}) %collective-permute-start.38) | collective-permute-done | bytes 65568 | tf_op jit(solution)/shard_map/ppermute | solution.py:910
  161.2 1.9 %collective-permute-done.40.refs_1_ = f32[64,256]{1,0:T(8,128)S(1)} collective-permute-done((f32[64,256]{1,0:T(8,128)S(1)}, f32[64,256]{1,0:T(8,128)S(1)}, u32[]{:S(2)}, u32[]{:S(2)}) %collective-permute-start.40) | collective-permute-done | bytes 65568 | tf_op jit(solution)/shard_map/ppermute | solution.py:910
  163.1 1.6 precond.15
  166.5 1.9 %collective-permute-done.42.refs_2_ = f32[64,256]{1,0:T(8,128)S(1)} collective-permute-done((f32[64,256]{1,0:T(8,128)S(1)}, f32[64,256]{1,0:T(8,128)S(1)}, u32[]{:S(2)}, u32[]{:S(2)}) %collective-permute-start.42) | collective-permute-done | bytes 65568 | tf_op jit(solution)/shard_map/ppermute | solution.py:910
  169.3 2.8 %collective-permute-start.44 = (f32[2,64,256]{2,1,0:T(8,128)S(1)}, f32[2,64,256]{2,1,0:T(8,128)S(1)}, u32[]{:S(2)}, u32[]{:S(2)}) collective-permute-start(f32[2,64,256]{2,1,0:T(8,128)S(1)} %get-tuple-element.193), channel_id=1, source_target_pairs={{18,0},{0,1},{26,2},{10,3},{4,4},{28,5},{14,6},{22,7},{16,8},{8,9}... | collective-permute-start | bytes 393224 | tf_op jit(solution)/shard_map/ppermute | solution.py:1014
  172.1 2.7 %collective-permute-start.45 = (f32[2,64,256]{2,1,0:T(8,128)S(1)}, f32[2,64,256]{2,1,0:T(8,128)S(1)}, u32[]{:S(2)}, u32[]{:S(2)}) collective-permute-start(f32[2,64,256]{2,1,0:T(8,128)S(1)} %get-tuple-element.194), channel_id=1, source_target_pairs={{19,0},{1,1},{27,2},{11,3},{5,4},{29,5},{15,6},{23,7},{17,8},{9,9}... | collective-permute-start | bytes 393224 | tf_op jit(solution)/shard_map/ppermute | solution.py:1014
  174.9 1.9 %collective-permute-start.46 = (f32[2,64,256]{2,1,0:T(8,128)S(1)}, f32[2,64,256]{2,1,0:T(8,128)S(1)}, u32[]{:S(2)}, u32[]{:S(2)}) collective-permute-start(f32[2,64,256]{2,1,0:T(8,128)S(1)} %get-tuple-element.195), channel_id=1, source_target_pairs={{16,0},{8,1},{24,2},{2,3},{12,4},{30,5},{6,6},{20,7},{18,8},{0,9},... | collective-permute-start | bytes 393224 | tf_op jit(solution)/shard_map/ppermute | solution.py:1014
  176.8 3.4 %collective-permute-start.47 = (f32[2,64,256]{2,1,0:T(8,128)S(1)}, f32[2,64,256]{2,1,0:T(8,128)S(1)}, u32[]{:S(2)}, u32[]{:S(2)}) collective-permute-start(f32[2,64,256]{2,1,0:T(8,128)S(1)} %get-tuple-element.196), channel_id=1, source_target_pairs={{17,0},{9,1},{25,2},{3,3},{13,4},{31,5},{7,6},{21,7},{19,8},{1,9},... | collective-permute-start | bytes 393224 | tf_op jit(solution)/shard_map/ppermute | solution.py:1014
  184.1 1.1 copy.16
  (99 shorter events, 47.5 us)
Async XLA Ops:
  4.7 13.6 %collective-permute-start = (f32[520,256]{1,0:T(8,128)}, f32[520,256]{1,0:T(8,128)S(1)}, u32[]{:S(2)}, u32[]{:S(2)}) collective-permute-start(f32[520,256]{1,0:T(8,128)} %get-tuple-element.102), channel_id=1, source_target_pairs={{0,18},{1,0},{2,26},{3,10},{4,4},{5,28},{6,14},{7,22},{8,16},{9,8}... | collective-permute-start | bytes 1597448 | tf_op jit(solution)/shard_map/ppermute | solution.py:937
  10.8 17.9 %collective-permute-start.1 = (f32[520,256]{1,0:T(8,128)}, f32[520,256]{1,0:T(8,128)S(1)}, u32[]{:S(2)}, u32[]{:S(2)}) collective-permute-start(f32[520,256]{1,0:T(8,128)} %get-tuple-element.103), channel_id=1, source_target_pairs={{0,19},{1,1},{2,27},{3,11},{4,5},{5,29},{6,15},{7,23},{8,17},{9,9}... | collective-permute-start | bytes 1597448 | tf_op jit(solution)/shard_map/ppermute | solution.py:937
  12.7 16.5 %collective-permute-start.2 = (f32[520,256]{1,0:T(8,128)}, f32[520,256]{1,0:T(8,128)S(1)}, u32[]{:S(2)}, u32[]{:S(2)}) collective-permute-start(f32[520,256]{1,0:T(8,128)} %get-tuple-element.104), channel_id=1, source_target_pairs={{0,16},{1,8},{2,24},{3,2},{4,12},{5,30},{6,6},{7,20},{8,18},{9,0},... | collective-permute-start | bytes 1597448 | tf_op jit(solution)/shard_map/ppermute | solution.py:937
  16.0 19.3 %collective-permute-start.3 = (f32[520,256]{1,0:T(8,128)}, f32[520,256]{1,0:T(8,128)S(1)}, u32[]{:S(2)}, u32[]{:S(2)}) collective-permute-start(f32[520,256]{1,0:T(8,128)} %get-tuple-element.105), channel_id=1, source_target_pairs={{0,17},{1,9},{2,25},{3,3},{4,13},{5,31},{6,7},{7,21},{8,19},{9,1},... | collective-permute-start | bytes 1597448 | tf_op jit(solution)/shard_map/ppermute | solution.py:937
  39.3 4.5 %collective-permute-start.4 = (f32[64,256]{1,0:T(8,128)S(1)}, f32[64,256]{1,0:T(8,128)S(1)}, u32[]{:S(2)}, u32[]{:S(2)}) collective-permute-start(f32[64,256]{1,0:T(8,128)S(1)} %get-tuple-element.107), channel_id=1, source_target_pairs={{18,19},{19,16},{16,17},{17,0},{0,1},{1,8},{8,9},{9,24},{24,25},{2... | collective-permute-start | bytes 196616 | tf_op jit(solution)/shard_map/ppermute | solution.py:910
  43.0 1.9 %collective-permute-start.5 = (f32[64,256]{1,0:T(8,128)S(1)}, f32[64,256]{1,0:T(8,128)S(1)}, u32[]{:S(2)}, u32[]{:S(2)}) collective-permute-start(f32[64,256]{1,0:T(8,128)S(1)} %get-tuple-element.108), channel_id=1, source_target_pairs={{19,18},{16,19},{17,16},{0,17},{1,0},{8,1},{9,8},{24,9},{25,24},{2... | collective-permute-start | bytes 196616 | tf_op jit(solution)/shard_map/ppermute | solution.py:910
  45.8 3.8 %collective-permute-start.6 = (f32[64,256]{1,0:T(8,128)S(1)}, f32[64,256]{1,0:T(8,128)S(1)}, u32[]{:S(2)}, u32[]{:S(2)}) collective-permute-start(f32[64,256]{1,0:T(8,128)S(1)} %get-tuple-element.111), channel_id=1, source_target_pairs={{18,19},{19,16},{16,17},{17,0},{0,1},{1,8},{8,9},{9,24},{24,25},{2... | collective-permute-start | bytes 196616 | tf_op jit(solution)/shard_map/ppermute | solution.py:910
  48.1 1.9 %collective-permute-start.7 = (f32[64,256]{1,0:T(8,128)S(1)}, f32[64,256]{1,0:T(8,128)S(1)}, u32[]{:S(2)}, u32[]{:S(2)}) collective-permute-start(f32[64,256]{1,0:T(8,128)S(1)} %get-tuple-element.112), channel_id=1, source_target_pairs={{19,18},{16,19},{17,16},{0,17},{1,0},{8,1},{9,8},{24,9},{25,24},{2... | collective-permute-start | bytes 196616 | tf_op jit(solution)/shard_map/ppermute | solution.py:910
  51.0 3.8 %collective-permute-start.8 = (f32[64,256]{1,0:T(8,128)S(1)}, f32[64,256]{1,0:T(8,128)S(1)}, u32[]{:S(2)}, u32[]{:S(2)}) collective-permute-start(f32[64,256]{1,0:T(8,128)S(1)} %get-tuple-element.115), channel_id=1, source_target_pairs={{18,19},{19,16},{16,17},{17,0},{0,1},{1,8},{8,9},{9,24},{24,25},{2... | collective-permute-start | bytes 196616 | tf_op jit(solution)/shard_map/ppermute | solution.py:910
  52.9 1.9 %collective-permute-start.9 = (f32[64,256]{1,0:T(8,128)S(1)}, f32[64,256]{1,0:T(8,128)S(1)}, u32[]{:S(2)}, u32[]{:S(2)}) collective-permute-start(f32[64,256]{1,0:T(8,128)S(1)} %get-tuple-element.116), channel_id=1, source_target_pairs={{19,18},{16,19},{17,16},{0,17},{1,0},{8,1},{9,8},{24,9},{25,24},{2... | collective-permute-start | bytes 196616 | tf_op jit(solution)/shard_map/ppermute | solution.py:910
  55.8 4.4 %collective-permute-start.10 = (f32[64,256]{1,0:T(8,128)S(1)}, f32[64,256]{1,0:T(8,128)S(1)}, u32[]{:S(2)}, u32[]{:S(2)}) collective-permute-start(f32[64,256]{1,0:T(8,128)S(1)} %get-tuple-element.119), channel_id=1, source_target_pairs={{18,19},{19,16},{16,17},{17,0},{0,1},{1,8},{8,9},{9,24},{24,25},{2... | collective-permute-start | bytes 196616 | tf_op jit(solution)/shard_map/ppermute | solution.py:910
  59.3 1.9 %collective-permute-start.11 = (f32[64,256]{1,0:T(8,128)S(1)}, f32[64,256]{1,0:T(8,128)S(1)}, u32[]{:S(2)}, u32[]{:S(2)}) collective-permute-start(f32[64,256]{1,0:T(8,128)S(1)} %get-tuple-element.120), channel_id=1, source_target_pairs={{19,18},{16,19},{17,16},{0,17},{1,0},{8,1},{9,8},{24,9},{25,24},{2... | collective-permute-start | bytes 196616 | tf_op jit(solution)/shard_map/ppermute | solution.py:910
  62.2 3.8 %collective-permute-start.12 = (f32[64,256]{1,0:T(8,128)S(1)}, f32[64,256]{1,0:T(8,128)S(1)}, u32[]{:S(2)}, u32[]{:S(2)}) collective-permute-start(f32[64,256]{1,0:T(8,128)S(1)} %get-tuple-element.124), channel_id=1, source_target_pairs={{18,19},{19,16},{16,17},{17,0},{0,1},{1,8},{8,9},{9,24},{24,25},{2... | collective-permute-start | bytes 196616 | tf_op jit(solution)/shard_map/ppermute | solution.py:910
  64.1 1.9 %collective-permute-start.13 = (f32[64,256]{1,0:T(8,128)S(1)}, f32[64,256]{1,0:T(8,128)S(1)}, u32[]{:S(2)}, u32[]{:S(2)}) collective-permute-start(f32[64,256]{1,0:T(8,128)S(1)} %get-tuple-element.125), channel_id=1, source_target_pairs={{19,18},{16,19},{17,16},{0,17},{1,0},{8,1},{9,8},{24,9},{25,24},{2... | collective-permute-start | bytes 196616 | tf_op jit(solution)/shard_map/ppermute | solution.py:910
  84.1 3.7 %collective-permute-start.14 = (f32[64,256]{1,0:T(8,128)S(1)}, f32[64,256]{1,0:T(8,128)S(1)}, u32[]{:S(2)}, u32[]{:S(2)}) collective-permute-start(f32[64,256]{1,0:T(8,128)S(1)} %get-tuple-element.130), channel_id=1, source_target_pairs={{18,19},{19,16},{16,17},{17,0},{0,1},{1,8},{8,9},{9,24},{24,25},{2... | collective-permute-start | bytes 196616 | tf_op jit(solution)/shard_map/ppermute | solution.py:910
  84.4 3.4 %collective-permute-start.15 = (f32[64,256]{1,0:T(8,128)S(1)}, f32[64,256]{1,0:T(8,128)S(1)}, u32[]{:S(2)}, u32[]{:S(2)}) collective-permute-start(f32[64,256]{1,0:T(8,128)S(1)} %get-tuple-element.131), channel_id=1, source_target_pairs={{19,18},{16,19},{17,16},{0,17},{1,0},{8,1},{9,8},{24,9},{25,24},{2... | collective-permute-start | bytes 196616 | tf_op jit(solution)/shard_map/ppermute | solution.py:910
  88.8 3.7 %collective-permute-start.16 = (f32[64,256]{1,0:T(8,128)S(1)}, f32[64,256]{1,0:T(8,128)S(1)}, u32[]{:S(2)}, u32[]{:S(2)}) collective-permute-start(f32[64,256]{1,0:T(8,128)S(1)} %get-tuple-element.134), channel_id=1, source_target_pairs={{18,19},{19,16},{16,17},{17,0},{0,1},{1,8},{8,9},{9,24},{24,25},{2... | collective-permute-start | bytes 196616 | tf_op jit(solution)/shard_map/ppermute | solution.py:910
  89.7 2.8 %collective-permute-start.17 = (f32[64,256]{1,0:T(8,128)S(1)}, f32[64,256]{1,0:T(8,128)S(1)}, u32[]{:S(2)}, u32[]{:S(2)}) collective-permute-start(f32[64,256]{1,0:T(8,128)S(1)} %get-tuple-element.135), channel_id=1, source_target_pairs={{19,18},{16,19},{17,16},{0,17},{1,0},{8,1},{9,8},{24,9},{25,24},{2... | collective-permute-start | bytes 196616 | tf_op jit(solution)/shard_map/ppermute | solution.py:910
  93.5 3.8 %collective-permute-start.18 = (f32[64,256]{1,0:T(8,128)S(1)}, f32[64,256]{1,0:T(8,128)S(1)}, u32[]{:S(2)}, u32[]{:S(2)}) collective-permute-start(f32[64,256]{1,0:T(8,128)S(1)} %get-tuple-element.138), channel_id=1, source_target_pairs={{18,19},{19,16},{16,17},{17,0},{0,1},{1,8},{8,9},{9,24},{24,25},{2... | collective-permute-start | bytes 196616 | tf_op jit(solution)/shard_map/ppermute | solution.py:910
  94.5 2.8 %collective-permute-start.19 = (f32[64,256]{1,0:T(8,128)S(1)}, f32[64,256]{1,0:T(8,128)S(1)}, u32[]{:S(2)}, u32[]{:S(2)}) collective-permute-start(f32[64,256]{1,0:T(8,128)S(1)} %get-tuple-element.139), channel_id=1, source_target_pairs={{19,18},{16,19},{17,16},{0,17},{1,0},{8,1},{9,8},{24,9},{25,24},{2... | collective-permute-start | bytes 196616 | tf_op jit(solution)/shard_map/ppermute | solution.py:910
  98.3 3.8 %collective-permute-start.20 = (f32[64,256]{1,0:T(8,128)S(1)}, f32[64,256]{1,0:T(8,128)S(1)}, u32[]{:S(2)}, u32[]{:S(2)}) collective-permute-start(f32[64,256]{1,0:T(8,128)S(1)} %get-tuple-element.142), channel_id=1, source_target_pairs={{18,19},{19,16},{16,17},{17,0},{0,1},{1,8},{8,9},{9,24},{24,25},{2... | collective-permute-start | bytes 196616 | tf_op jit(solution)/shard_map/ppermute | solution.py:910
  99.3 2.8 %collective-permute-start.21 = (f32[64,256]{1,0:T(8,128)S(1)}, f32[64,256]{1,0:T(8,128)S(1)}, u32[]{:S(2)}, u32[]{:S(2)}) collective-permute-start(f32[64,256]{1,0:T(8,128)S(1)} %get-tuple-element.143), channel_id=1, source_target_pairs={{19,18},{16,19},{17,16},{0,17},{1,0},{8,1},{9,8},{24,9},{25,24},{2... | collective-permute-start | bytes 196616 | tf_op jit(solution)/shard_map/ppermute | solution.py:910
  103.0 4.0 %collective-permute-start.22 = (f32[64,256]{1,0:T(8,128)S(1)}, f32[64,256]{1,0:T(8,128)S(1)}, u32[]{:S(2)}, u32[]{:S(2)}) collective-permute-start(f32[64,256]{1,0:T(8,128)S(1)} %get-tuple-element.146), channel_id=1, source_target_pairs={{18,19},{19,16},{16,17},{17,0},{0,1},{1,8},{8,9},{9,24},{24,25},{2... | collective-permute-start | bytes 196616 | tf_op jit(solution)/shard_map/ppermute | solution.py:910
  104.2 2.8 %collective-permute-start.23 = (f32[64,256]{1,0:T(8,128)S(1)}, f32[64,256]{1,0:T(8,128)S(1)}, u32[]{:S(2)}, u32[]{:S(2)}) collective-permute-start(f32[64,256]{1,0:T(8,128)S(1)} %get-tuple-element.147), channel_id=1, source_target_pairs={{19,18},{16,19},{17,16},{0,17},{1,0},{8,1},{9,8},{24,9},{25,24},{2... | collective-permute-start | bytes 196616 | tf_op jit(solution)/shard_map/ppermute | solution.py:910
  108.0 3.8 %collective-permute-start.24 = (f32[64,256]{1,0:T(8,128)S(1)}, f32[64,256]{1,0:T(8,128)S(1)}, u32[]{:S(2)}, u32[]{:S(2)}) collective-permute-start(f32[64,256]{1,0:T(8,128)S(1)} %get-tuple-element.151), channel_id=1, source_target_pairs={{18,19},{19,16},{16,17},{17,0},{0,1},{1,8},{8,9},{9,24},{24,25},{2... | collective-permute-start | bytes 196616 | tf_op jit(solution)/shard_map/ppermute | solution.py:910
  109.0 2.8 %collective-permute-start.25 = (f32[64,256]{1,0:T(8,128)S(1)}, f32[64,256]{1,0:T(8,128)S(1)}, u32[]{:S(2)}, u32[]{:S(2)}) collective-permute-start(f32[64,256]{1,0:T(8,128)S(1)} %get-tuple-element.152), channel_id=1, source_target_pairs={{19,18},{16,19},{17,16},{0,17},{1,0},{8,1},{9,8},{24,9},{25,24},{2... | collective-permute-start | bytes 196616 | tf_op jit(solution)/shard_map/ppermute | solution.py:910
  112.8 3.8 %collective-permute-start.26 = (f32[64,256]{1,0:T(8,128)S(1)}, f32[64,256]{1,0:T(8,128)S(1)}, u32[]{:S(2)}, u32[]{:S(2)}) collective-permute-start(f32[64,256]{1,0:T(8,128)S(1)} %get-tuple-element.155), channel_id=1, source_target_pairs={{18,19},{19,16},{16,17},{17,0},{0,1},{1,8},{8,9},{9,24},{24,25},{2... | collective-permute-start | bytes 196616 | tf_op jit(solution)/shard_map/ppermute | solution.py:910
  113.8 2.8 %collective-permute-start.27 = (f32[64,256]{1,0:T(8,128)S(1)}, f32[64,256]{1,0:T(8,128)S(1)}, u32[]{:S(2)}, u32[]{:S(2)}) collective-permute-start(f32[64,256]{1,0:T(8,128)S(1)} %get-tuple-element.156), channel_id=1, source_target_pairs={{19,18},{16,19},{17,16},{0,17},{1,0},{8,1},{9,8},{24,9},{25,24},{2... | collective-permute-start | bytes 196616 | tf_op jit(solution)/shard_map/ppermute | solution.py:910
  117.6 3.8 %collective-permute-start.28 = (f32[64,256]{1,0:T(8,128)S(1)}, f32[64,256]{1,0:T(8,128)S(1)}, u32[]{:S(2)}, u32[]{:S(2)}) collective-permute-start(f32[64,256]{1,0:T(8,128)S(1)} %get-tuple-element.159), channel_id=1, source_target_pairs={{18,19},{19,16},{16,17},{17,0},{0,1},{1,8},{8,9},{9,24},{24,25},{2... | collective-permute-start | bytes 196616 | tf_op jit(solution)/shard_map/ppermute | solution.py:910
  118.6 2.8 %collective-permute-start.29 = (f32[64,256]{1,0:T(8,128)S(1)}, f32[64,256]{1,0:T(8,128)S(1)}, u32[]{:S(2)}, u32[]{:S(2)}) collective-permute-start(f32[64,256]{1,0:T(8,128)S(1)} %get-tuple-element.160), channel_id=1, source_target_pairs={{19,18},{16,19},{17,16},{0,17},{1,0},{8,1},{9,8},{24,9},{25,24},{2... | collective-permute-start | bytes 196616 | tf_op jit(solution)/shard_map/ppermute | solution.py:910
  122.3 3.8 %collective-permute-start.30 = (f32[64,256]{1,0:T(8,128)S(1)}, f32[64,256]{1,0:T(8,128)S(1)}, u32[]{:S(2)}, u32[]{:S(2)}) collective-permute-start(f32[64,256]{1,0:T(8,128)S(1)} %get-tuple-element.163), channel_id=1, source_target_pairs={{18,19},{19,16},{16,17},{17,0},{0,1},{1,8},{8,9},{9,24},{24,25},{2... | collective-permute-start | bytes 196616 | tf_op jit(solution)/shard_map/ppermute | solution.py:910
  123.3 2.8 %collective-permute-start.31 = (f32[64,256]{1,0:T(8,128)S(1)}, f32[64,256]{1,0:T(8,128)S(1)}, u32[]{:S(2)}, u32[]{:S(2)}) collective-permute-start(f32[64,256]{1,0:T(8,128)S(1)} %get-tuple-element.164), channel_id=1, source_target_pairs={{19,18},{16,19},{17,16},{0,17},{1,0},{8,1},{9,8},{24,9},{25,24},{2... | collective-permute-start | bytes 196616 | tf_op jit(solution)/shard_map/ppermute | solution.py:910
  127.1 3.8 %collective-permute-start.32 = (f32[64,256]{1,0:T(8,128)S(1)}, f32[64,256]{1,0:T(8,128)S(1)}, u32[]{:S(2)}, u32[]{:S(2)}) collective-permute-start(f32[64,256]{1,0:T(8,128)S(1)} %get-tuple-element.168), channel_id=1, source_target_pairs={{18,19},{19,16},{16,17},{17,0},{0,1},{1,8},{8,9},{9,24},{24,25},{2... | collective-permute-start | bytes 196616 | tf_op jit(solution)/shard_map/ppermute | solution.py:910
  128.1 2.8 %collective-permute-start.33 = (f32[64,256]{1,0:T(8,128)S(1)}, f32[64,256]{1,0:T(8,128)S(1)}, u32[]{:S(2)}, u32[]{:S(2)}) collective-permute-start(f32[64,256]{1,0:T(8,128)S(1)} %get-tuple-element.169), channel_id=1, source_target_pairs={{19,18},{16,19},{17,16},{0,17},{1,0},{8,1},{9,8},{24,9},{25,24},{2... | collective-permute-start | bytes 196616 | tf_op jit(solution)/shard_map/ppermute | solution.py:910
  145.1 3.7 %collective-permute-start.34 = (f32[64,256]{1,0:T(8,128)S(1)}, f32[64,256]{1,0:T(8,128)S(1)}, u32[]{:S(2)}, u32[]{:S(2)}) collective-permute-start(f32[64,256]{1,0:T(8,128)S(1)} %get-tuple-element.173), channel_id=1, source_target_pairs={{18,19},{19,16},{16,17},{17,0},{0,1},{1,8},{8,9},{9,24},{24,25},{2... | collective-permute-start | bytes 196616 | tf_op jit(solution)/shard_map/ppermute | solution.py:910
  145.4 3.4 %collective-permute-start.35 = (f32[64,256]{1,0:T(8,128)S(1)}, f32[64,256]{1,0:T(8,128)S(1)}, u32[]{:S(2)}, u32[]{:S(2)}) collective-permute-start(f32[64,256]{1,0:T(8,128)S(1)} %get-tuple-element.174), channel_id=1, source_target_pairs={{19,18},{16,19},{17,16},{0,17},{1,0},{8,1},{9,8},{24,9},{25,24},{2... | collective-permute-start | bytes 196616 | tf_op jit(solution)/shard_map/ppermute | solution.py:910
  149.8 3.7 %collective-permute-start.36 = (f32[64,256]{1,0:T(8,128)S(1)}, f32[64,256]{1,0:T(8,128)S(1)}, u32[]{:S(2)}, u32[]{:S(2)}) collective-permute-start(f32[64,256]{1,0:T(8,128)S(1)} %get-tuple-element.177), channel_id=1, source_target_pairs={{18,19},{19,16},{16,17},{17,0},{0,1},{1,8},{8,9},{9,24},{24,25},{2... | collective-permute-start | bytes 196616 | tf_op jit(solution)/shard_map/ppermute | solution.py:910
  150.8 2.8 %collective-permute-start.37 = (f32[64,256]{1,0:T(8,128)S(1)}, f32[64,256]{1,0:T(8,128)S(1)}, u32[]{:S(2)}, u32[]{:S(2)}) collective-permute-start(f32[64,256]{1,0:T(8,128)S(1)} %get-tuple-element.178), channel_id=1, source_target_pairs={{19,18},{16,19},{17,16},{0,17},{1,0},{8,1},{9,8},{24,9},{25,24},{2... | collective-permute-start | bytes 196616 | tf_op jit(solution)/shard_map/ppermute | solution.py:910
  154.5 3.8 %collective-permute-start.38 = (f32[64,256]{1,0:T(8,128)S(1)}, f32[64,256]{1,0:T(8,128)S(1)}, u32[]{:S(2)}, u32[]{:S(2)}) collective-permute-start(f32[64,256]{1,0:T(8,128)S(1)} %get-tuple-element.181), channel_id=1, source_target_pairs={{18,19},{19,16},{16,17},{17,0},{0,1},{1,8},{8,9},{9,24},{24,25},{2... | collective-permute-start | bytes 196616 | tf_op jit(solution)/shard_map/ppermute | solution.py:910
  155.5 2.8 %collective-permute-start.39 = (f32[64,256]{1,0:T(8,128)S(1)}, f32[64,256]{1,0:T(8,128)S(1)}, u32[]{:S(2)}, u32[]{:S(2)}) collective-permute-start(f32[64,256]{1,0:T(8,128)S(1)} %get-tuple-element.182), channel_id=1, source_target_pairs={{19,18},{16,19},{17,16},{0,17},{1,0},{8,1},{9,8},{24,9},{25,24},{2... | collective-permute-start | bytes 196616 | tf_op jit(solution)/shard_map/ppermute | solution.py:910
  159.3 3.8 %collective-permute-start.40 = (f32[64,256]{1,0:T(8,128)S(1)}, f32[64,256]{1,0:T(8,128)S(1)}, u32[]{:S(2)}, u32[]{:S(2)}) collective-permute-start(f32[64,256]{1,0:T(8,128)S(1)} %get-tuple-element.185), channel_id=1, source_target_pairs={{18,19},{19,16},{16,17},{17,0},{0,1},{1,8},{8,9},{9,24},{24,25},{2... | collective-permute-start | bytes 196616 | tf_op jit(solution)/shard_map/ppermute | solution.py:910
  160.3 2.8 %collective-permute-start.41 = (f32[64,256]{1,0:T(8,128)S(1)}, f32[64,256]{1,0:T(8,128)S(1)}, u32[]{:S(2)}, u32[]{:S(2)}) collective-permute-start(f32[64,256]{1,0:T(8,128)S(1)} %get-tuple-element.186), channel_id=1, source_target_pairs={{19,18},{16,19},{17,16},{0,17},{1,0},{8,1},{9,8},{24,9},{25,24},{2... | collective-permute-start | bytes 196616 | tf_op jit(solution)/shard_map/ppermute | solution.py:910
  164.7 3.7 %collective-permute-start.42 = (f32[64,256]{1,0:T(8,128)S(1)}, f32[64,256]{1,0:T(8,128)S(1)}, u32[]{:S(2)}, u32[]{:S(2)}) collective-permute-start(f32[64,256]{1,0:T(8,128)S(1)} %get-tuple-element.189), channel_id=1, source_target_pairs={{18,19},{19,16},{16,17},{17,0},{0,1},{1,8},{8,9},{9,24},{24,25},{2... | collective-permute-start | bytes 196616 | tf_op jit(solution)/shard_map/ppermute | solution.py:910
  165.7 2.8 %collective-permute-start.43 = (f32[64,256]{1,0:T(8,128)S(1)}, f32[64,256]{1,0:T(8,128)S(1)}, u32[]{:S(2)}, u32[]{:S(2)}) collective-permute-start(f32[64,256]{1,0:T(8,128)S(1)} %get-tuple-element.190), channel_id=1, source_target_pairs={{19,18},{16,19},{17,16},{0,17},{1,0},{8,1},{9,8},{24,9},{25,24},{2... | collective-permute-start | bytes 196616 | tf_op jit(solution)/shard_map/ppermute | solution.py:910
  169.3 14.1 %collective-permute-start.44 = (f32[2,64,256]{2,1,0:T(8,128)S(1)}, f32[2,64,256]{2,1,0:T(8,128)S(1)}, u32[]{:S(2)}, u32[]{:S(2)}) collective-permute-start(f32[2,64,256]{2,1,0:T(8,128)S(1)} %get-tuple-element.193), channel_id=1, source_target_pairs={{18,0},{0,1},{26,2},{10,3},{4,4},{28,5},{14,6},{22,7},{16,8},{8,9}... | collective-permute-start | bytes 393224 | tf_op jit(solution)/shard_map/ppermute | solution.py:1014
  172.1 11.2 %collective-permute-start.45 = (f32[2,64,256]{2,1,0:T(8,128)S(1)}, f32[2,64,256]{2,1,0:T(8,128)S(1)}, u32[]{:S(2)}, u32[]{:S(2)}) collective-permute-start(f32[2,64,256]{2,1,0:T(8,128)S(1)} %get-tuple-element.194), channel_id=1, source_target_pairs={{19,0},{1,1},{27,2},{11,3},{5,4},{29,5},{15,6},{23,7},{17,8},{9,9}... | collective-permute-start | bytes 393224 | tf_op jit(solution)/shard_map/ppermute | solution.py:1014
  174.9 8.5 %collective-permute-start.46 = (f32[2,64,256]{2,1,0:T(8,128)S(1)}, f32[2,64,256]{2,1,0:T(8,128)S(1)}, u32[]{:S(2)}, u32[]{:S(2)}) collective-permute-start(f32[2,64,256]{2,1,0:T(8,128)S(1)} %get-tuple-element.195), channel_id=1, source_target_pairs={{16,0},{8,1},{24,2},{2,3},{12,4},{30,5},{6,6},{20,7},{18,8},{0,9},... | collective-permute-start | bytes 393224 | tf_op jit(solution)/shard_map/ppermute | solution.py:1014
  176.8 7.2 %collective-permute-start.47 = (f32[2,64,256]{2,1,0:T(8,128)S(1)}, f32[2,64,256]{2,1,0:T(8,128)S(1)}, u32[]{:S(2)}, u32[]{:S(2)}) collective-permute-start(f32[2,64,256]{2,1,0:T(8,128)S(1)} %get-tuple-element.196), channel_id=1, source_target_pairs={{17,0},{9,1},{25,2},{3,3},{13,4},{31,5},{7,6},{21,7},{19,8},{1,9},... | collective-permute-start | bytes 393224 | tf_op jit(solution)/shard_map/ppermute | solution.py:1014
  (10 other events, 119.2 us)

commit v4 on v3

--- a/solution.py
+++ b/solution.py
@@ -433,13 +433,15 @@
         blocks.append(np.kron(basis[:half, picked].T, np.kron(basis.T, basis.T)))
     forward = np.stack([wide(m) for m in blocks])
     backward = np.stack([wide(m.T) for m in blocks])
+    face = NODES * NODES
+    forward_face = np.stack([wide(m[:, :face]) for m in blocks])
     order_b = even + odd
     one = np.ones(NODES)
     lam_a = np.kron(one, np.kron(values, one))
     lam_b = np.kron(values[order_b], np.kron(one, one))
     lam_c = np.kron(one, np.kron(one, values))
     root3 = np.kron(root, np.kron(root, root))
-    spectrum = np.stack([lam_a, lam_b, lam_c, root3, 1.0 / root3] + [0 * lam_a] * 3, axis=1)
+    spectrum = np.stack([lam_a, lam_b, lam_c, root3] + [0 * lam_a] * 4, axis=1)
     edge = np.where((np.arange(NODES) == 0) | (np.arange(NODES) == NODES - 1), 0.5, 1.0)
     jw = interp * root[:, None] * edge[:, None]
     first = np.zeros_like(jw)
@@ -474,11 +476,12 @@
     as32 = lambda t: np.asarray(t, np.float32)
     return dict(
         forward=forward,
+        forward_face=forward_face,
         backward=backward,
-        columns=as32(np.concatenate([spectrum, prolong], axis=1)),
-        restrict=as32(restrict),
-        swaps=as32(np.concatenate([swap, swap.T], axis=0)),
-        deal=deal.astype(bf16),
+        columns=wide(np.concatenate([spectrum, prolong], axis=1)),
+        inv_root=as32(1.0 / root3[:, None]),
+        restrict=wide(restrict),
+        swaps=np.concatenate([swap, swap.T], axis=0).astype(bf16),
         gather=deal.T.astype(bf16),
     )
 
@@ -506,7 +509,7 @@
     return jnp.dot(table, stacked, preferred_element_type=f32)
 
 
-def spectral_apply(field, forward_ref, backward_ref, scale_ref):
+def to_modes(field, forward_ref, scale_ref):
     face = field.shape[0] // NODES
     half = field.shape[0] // 2
     top = field[:half]
@@ -515,12 +518,32 @@
     )
     even = wide_dot(forward_ref[0], top + bottom) * scale_ref[:half]
     odd = wide_dot(forward_ref[1], top - bottom) * scale_ref[half:]
-    even = wide_dot(backward_ref[0], even)
-    odd = wide_dot(backward_ref[1], odd)
-    low_half = even + odd
+    return jnp.concatenate([even, odd], axis=0)
+
+
+def from_modes(modes, backward_ref):
+    half = modes.shape[0] // 2
+    face = modes.shape[0] // NODES
+    even = wide_dot(backward_ref[0], modes[:half])
+    odd = wide_dot(backward_ref[1], modes[half:])
     diff = even - odd
-    parts = [low_half] + [diff[b * face : (b + 1) * face] for b in reversed(range(NODES // 2))]
-    return jnp.concatenate(parts, axis=0)
+    parts = [diff[b * face : (b + 1) * face] for b in reversed(range(NODES // 2))]
+    return jnp.concatenate([even + odd] + parts, axis=0)
+
+
+def faces_to_modes(low, high, forward_face_ref, scale_ref):
+    half = scale_ref.shape[0] // 2
+    even = wide_dot(forward_face_ref[0], low + high) * scale_ref[:half]
+    odd = wide_dot(forward_face_ref[1], low - high) * scale_ref[half:]
+    return jnp.concatenate([even, odd], axis=0)
+
+
+def modes_to_faces(modes, backward_ref):
+    half = modes.shape[0] // 2
+    face = modes.shape[0] // NODES
+    even = wide_dot(backward_ref[0, :face], modes[:half])
+    odd = wide_dot(backward_ref[1, :face], modes[half:])
+    return even + odd, even - odd
 
 
 def lane_layer(shape, ez_count):
@@ -538,60 +561,81 @@
     ref[rows:] = field[:, 128:]
 
 
-def assemble_local(field, out_ref, low_ref, high_ref, ez_count, average):
+def sum_pairs(field, work_ref, ez_count, average):
     rows, lanes = field.shape
-    face = rows // NODES
+    face = NODES * NODES
     tile = NODES
-    f4 = field.reshape(NODES, NODES, tile, lanes)
-    a_low = f4[:, 0].reshape(face, lanes)
-    a_high = f4[:, NODES - 1].reshape(face, lanes)
+    count = rows // face
+    f4 = field.reshape(count, NODES, tile, lanes)
+    a_low = f4[:, 0].reshape(count * tile, lanes)
+    a_high = f4[:, NODES - 1].reshape(count * tile, lanes)
     new_low = a_low + pltpu.roll(a_high, ez_count, 1)
     new_high = a_high + pltpu.roll(a_low, lanes - ez_count, 1)
     if average:
         new_low = 0.5 * new_low
         new_high = 0.5 * new_high
-    store_halves(out_ref, field)
-    layer = lane_layer((face, 128), ez_count)
+    store_halves(work_ref, field)
+    spots = rows // NODES
+    layer = lane_layer((spots, 128), ez_count)
     for side in range(2):
         base = side * rows
         span = slice(side * 128, (side + 1) * 128)
-        for b in range(NODES):
+        for b in range(count):
             at = base + b * face
-            out_ref[at : at + tile] = new_low[b * tile : (b + 1) * tile, span]
-            out_ref[at + face - tile : at + face] = new_high[b * tile : (b + 1) * tile, span]
-        c_low = out_ref[pl.ds(base, face, stride=NODES), :]
-        c_high = out_ref[pl.ds(base + NODES - 1, face, stride=NODES), :]
+            work_ref[at : at + tile] = new_low[b * tile : (b + 1) * tile, span]
+            work_ref[at + face - tile : at + face] = new_high[b * tile : (b + 1) * tile, span]
+        c_low = work_ref[pl.ds(base, spots, stride=NODES), :]
+        c_high = work_ref[pl.ds(base + NODES - 1, spots, stride=NODES), :]
         above = c_low + pltpu.roll(c_high, 1, 1)
         below = c_high + pltpu.roll(c_low, 127, 1)
         if average:
             above = 0.5 * above
             below = 0.5 * below
-        out_ref[pl.ds(base, face, stride=NODES), :] = jnp.where(layer > 0, above, c_low)
-        out_ref[pl.ds(base + NODES - 1, face, stride=NODES), :] = jnp.where(
+        work_ref[pl.ds(base, spots, stride=NODES), :] = jnp.where(layer > 0, above, c_low)
+        work_ref[pl.ds(base + NODES - 1, spots, stride=NODES), :] = jnp.where(
             layer < ez_count - 1, below, 0.0
         )
-        low = out_ref[base : base + face]
-        high = out_ref[base + rows - face : base + rows]
-        low_ref[:, span] = low
-        high_ref[:, span] = high
-
-
-def joined(w_ref, below_ref, above_ref, scale):
+
+
+def store_faces(work_ref, low_ref, high_ref):
+    face = low_ref.shape[0]
+    rows = work_ref.shape[0] // 2
+    for side in range(2):
+        span = slice(side * 128, (side + 1) * 128)
+        low_ref[:, span] = work_ref[side * rows : side * rows + face]
+        high_ref[:, span] = work_ref[(side + 1) * rows - face : (side + 1) * rows]
+
+
+def assemble_local(field, out_ref, low_ref, high_ref, ez_count, average):
+    sum_pairs(field, out_ref, ez_count, average)
+    store_faces(out_ref, low_ref, high_ref)
+
+
+def with_faces(field, below_ref, above_ref, scale):
     face = below_ref.shape[0]
-    rows = w_ref.shape[0] // 2
-    field = lane_halves(w_ref)
-    low = field[:face] + below_ref[...]
-    high = field[rows - face :] + above_ref[...]
-    if scale != 1.0:
-        low = low * scale
-        high = high * scale
-    return jnp.concatenate([low, field[face : rows - face], high], axis=0)
-
-
-def pack_kernel(cols, codes, *refs):
+    rows = field.shape[0]
+    return jnp.concatenate(
+        [
+            field[:face] + scale * below_ref[...],
+            field[face : rows - face],
+            field[rows - face :] + scale * above_ref[...],
+        ],
+        axis=0,
+    )
+
+
+def half_faces(field):
+    face = NODES * NODES
+    rows = field.shape[0]
+    return jnp.concatenate(
+        [0.5 * field[:face], field[face : rows - face], 0.5 * field[rows - face :]], axis=0
+    )
+
+
+def pack_kernel(cols, gy_count, codes, *refs):
     (device_ref, count_ref, source_hbm, geometry_hbm, disc_hbm, thrust_hbm, factor_hbm,
-     q0, q1, q2, q3, place_hbm,
-     held, geometry_ref, disc_ref, thrust_ref, factor_ref, place_ref, sems, row_sems) = refs
+     q0, q1, q2, q3,
+     held, geometry_ref, disc_ref, thrust_ref, factor_ref, sems, row_sems) = refs
     parts = 4
     _, nodes, elem_x, _, lanes = source_hbm.shape
     face = nodes * nodes
@@ -626,7 +670,6 @@
     code = jnp.int32(codes[0])
     for d in range(1, len(codes)):
         code = jnp.where(device_ref[0] == d, jnp.int32(codes[d]), code)
-    place_ref[...] = jnp.full(place_ref.shape, code, jnp.int32)
     levels = count_ref.shape[0]
     lane = lax.broadcasted_iota(jnp.int32, (1, lanes), 1)
     limit = jnp.zeros((1, lanes), jnp.int32)
@@ -635,6 +678,9 @@
     live = jnp.where(lax.rem(lane, cols) < limit, 1.0, 0.0).astype(f32)
     for copy in copies:
         copy.wait()
+    own_gx = jnp.full((1, lanes), device_ref[0] // gy_count, jnp.int32).astype(f32)
+    own_gy = jnp.full((1, lanes), lax.rem(device_ref[0], gy_count), jnp.int32).astype(f32)
+    blank_row = jnp.zeros((1, lanes), f32)
     push = disc_ref[...].astype(f32) * thrust_ref[...]
     ez_count = push.shape[2]
     blank = jnp.zeros((1, lanes - 2 * ez_count), f32)
@@ -646,8 +692,7 @@
             for c in range(3)
         ]
         pieces.append(jnp.concatenate([push[ex, ey : ey + 1] for ex in range(2)] + [blank], 1))
-        pieces.append(live)
-        pieces.append(jnp.zeros((3, lanes), f32))
+        pieces += [live, own_gx, own_gy, blank_row]
         held[ey, nodes_rows : nodes_rows + 8] = jnp.concatenate(pieces, axis=0)
         for pair in range(4):
             at = [(2 * pair + k) * parts * span + ey * span for k in range(2)]
@@ -662,15 +707,15 @@
         pltpu.make_async_copy(held.at[field_of(code, 2 * q)], ref, sems.at[4 + q])
         for q, ref in enumerate((q0, q1, q2, q3))
     ]
-    outs.append(pltpu.make_async_copy(place_ref, place_hbm, sems.at[8]))
     for copy in outs:
         copy.start()
     for copy in outs:
         copy.wait()
 
 
-def message_part(base_ref, q):
-    return field_of(base_ref[0, 0], 8 + 2 * q)
+def sender_of(ref, count, row):
+    at = ref.shape[0] - 2 * count - 8 + row
+    return ref[at, 0].astype(jnp.int32)
 
 
 def factor_block(ref, count, vu):
@@ -678,8 +723,8 @@
     return ref[base : base + count, (vu % 2) * 128 : (vu % 2) * 128 + 128]
 
 
-def entry_kernel(ez_count, *refs):
-    (place_ref, q0, q1, q2, q3, columns_ref, deal_ref,
+def entry_kernel(ez_count, count, *refs):
+    (q0, q1, q2, q3, columns_ref,
      w_ref, low_ref, high_ref, inv_ref, den_ref, live_ref, held) = refs
     rows = w_ref.shape[0] // 2
     face = rows // NODES
@@ -687,7 +732,9 @@
     parts = 4
     width = lanes // parts
     for q, ref in enumerate((q0, q1, q2, q3)):
-        held[message_part(place_ref, q)] = ref[: 2 * face + 8]
+        part = sender_of(ref, count, 5)
+        held[part] = ref[: 2 * face + 8]
+        live_ref[8 + q : 9 + q] = jnp.full((1, 128), part, jnp.int32).astype(f32)
     sizes = jnp.concatenate(
         [held[i, 2 * face : 2 * face + 8, :width] for i in range(parts)], axis=1
     )
@@ -697,9 +744,19 @@
     metric_z = len_x * len_y / (2.0 * len_z)
     volume = len_x * len_y * len_z / 8.0
     metrics = jnp.concatenate(
-        [metric_x, metric_y, metric_z, jnp.zeros((5, lanes), f32)], axis=0
-    )
-    stiff = hp_dot(columns_ref[:, :8], metrics)
+        [metric_x, metric_y, metric_z, jnp.zeros((13, lanes), f32)], axis=0
+    )
+    stiff = wide_dot(columns_ref[...], metrics)
+    volumes = jnp.concatenate(
+        [jnp.zeros((3, lanes), f32), volume, jnp.zeros((12, lanes), f32)], axis=0
+    )
+    mass = wide_dot(columns_ref[...], volumes)
+    span = 2 * ez_count * NODES
+    target = lax.broadcasted_iota(jnp.int32, (span, span), 1)
+    origin = lax.rem(target, 2 * ez_count) * NODES + target // (2 * ez_count)
+    deal = jnp.where(
+        lax.broadcasted_iota(jnp.int32, (span, span), 0) == origin, 1.0, 0.0
+    ).astype(bf16)
     den_ref[...] = stiff
     inv_ref[...] = 1.0 / (stiff + shift_ratio * (metric_x + metric_y + metric_z))
     for i in range(parts):
@@ -712,7 +769,7 @@
         ],
         axis=0,
     )
-    dealt = move_lanes(raw, deal_ref[...])
+    dealt = move_lanes(raw, deal)
     for c in range(NODES):
         for side in range(2):
             w_ref[pl.ds(side * rows + c, face, stride=NODES), :] = jnp.concatenate(
@@ -722,73 +779,121 @@
                 ],
                 axis=1,
             )
-    forcing = (lane_halves(w_ref) + push) * (columns_ref[:, 3:4] * volume)
+    forcing = (lane_halves(w_ref) + push) * mass
     assemble_local(forcing, w_ref, low_ref, high_ref, ez_count, False)
 
 
-def precond_kernel(ez_count, first, *refs):
-    if first:
-        (w_ref, below_ref, above_ref, fwd_ref, bwd_ref, inv_ref,
-         r_ref, u_ref, low_ref, high_ref) = refs
-        resid = joined(w_ref, below_ref, above_ref, 1.0)
-    else:
-        (w_ref, below_ref, above_ref, r_in_ref, fwd_ref, bwd_ref, inv_ref,
-         r_ref, u_ref, low_ref, high_ref) = refs
-        resid = r_in_ref[...] - joined(w_ref, below_ref, above_ref, 1.0)
-    r_ref[...] = resid
-    field = spectral_apply(resid, fwd_ref, bwd_ref, inv_ref)
-    assemble_local(field, u_ref, low_ref, high_ref, ez_count, True)
-
-
-def apply_kernel(ez_count, keep, gain, start, keep_d, *refs):
+def face_kernel(ez_count, average, scale, *refs):
+    (below_ref, above_ref, own_low_ref, own_high_ref, scale_ref, forward_face_ref, backward_ref,
+     low_ref, high_ref, modes_ref, work) = refs
+    modes = faces_to_modes(
+        scale * below_ref[...], scale * above_ref[...], forward_face_ref, scale_ref
+    )
+    modes_ref[...] = modes
+    low, high = modes_to_faces(modes, backward_ref)
+    field = jnp.concatenate([own_low_ref[...] + low, own_high_ref[...] + high], axis=0)
+    sum_pairs(field, work, ez_count, average)
+    store_faces(work, low_ref, high_ref)
+
+
+def open_kernel(halve, *refs):
+    (w_ref, forward_ref, backward_ref, scale_ref,
+     base_ref, modes_ref, low_ref, high_ref) = refs
+    base = lane_halves(w_ref)
+    if halve:
+        base = half_faces(base)
+    base_ref[...] = base
+    modes = to_modes(base, forward_ref, scale_ref)
+    modes_ref[...] = modes
+    low_ref[...], high_ref[...] = modes_to_faces(modes, backward_ref)
+
+
+def rest_precond_kernel(ez_count, sign, keep, gain, *refs):
     refs = list(refs)
-    w_ref, below_ref, above_ref = refs[:3]
-    refs = refs[3:]
-    step = joined(w_ref, below_ref, above_ref, 0.5)
-    if gain != 1.0:
-        step = step * gain
+    below_ref, above_ref, base_ref, own_ref, more_ref = refs[:5]
+    refs = refs[5:]
+    old_ref = refs.pop(0) if keep != 0.0 else None
+    (forward_ref, backward_ref, scale_ref,
+     r_ref, step_ref, modes_ref, low_ref, high_ref, work) = refs
+    r_ref[...] = with_faces(base_ref[...], below_ref, above_ref, sign)
+    sum_pairs(from_modes(own_ref[...] + more_ref[...], backward_ref), work, ez_count, True)
+    step = half_faces(lane_halves(work)) * gain
     if keep != 0.0:
-        step = step + keep * refs.pop(0)[...]
-    total = step if start else refs.pop(0)[...] + step
-    fwd_ref, bwd_ref, den_ref = refs[:3]
-    refs = refs[3:]
-    x_ref, k_ref, low_ref, high_ref = refs[:4]
-    x_ref[...] = total
+        step = step + keep * old_ref[...]
+    step_ref[...] = step
+    modes = to_modes(step, forward_ref, scale_ref)
+    modes_ref[...] = modes
+    low_ref[...], high_ref[...] = modes_to_faces(modes, backward_ref)
+
+
+def close_kernel(ez_count, keep, gain, *refs):
+    own_ref, more_ref, old_ref, x_ref, backward_ref, total_ref, work = refs
+    sum_pairs(from_modes(own_ref[...] + more_ref[...], backward_ref), work, ez_count, True)
+    step = half_faces(lane_halves(work)) * gain + keep * old_ref[...]
+    total_ref[...] = x_ref[...] + step
+
+
+def rest_apply_kernel(ez_count, scale, start, keep_d, go_on, *refs):
+    refs = list(refs)
+    below_ref, above_ref, step_ref, own_ref, more_ref, r_ref = refs[:6]
+    refs = refs[6:]
+    x_in_ref = None if start else refs.pop(0)
+    backward_ref = refs.pop(0)
+    if go_on:
+        forward_ref, scale_ref = refs[:2]
+        refs = refs[2:]
+    x_ref, base_ref = refs[:2]
+    refs = refs[2:]
+    step = with_faces(step_ref[...], below_ref, above_ref, scale)
+    x_ref[...] = step if start else x_in_ref[...] + step
     if keep_d:
-        refs[4][...] = step
-    field = spectral_apply(step, fwd_ref, bwd_ref, den_ref)
-    assemble_local(field, k_ref, low_ref, high_ref, ez_count, False)
+        refs.pop(0)[...] = step
+    work = refs[-1]
+    sum_pairs(from_modes(own_ref[...] + more_ref[...], backward_ref), work, ez_count, False)
+    base = r_ref[...] - lane_halves(work)
+    base_ref[...] = base
+    if go_on:
+        modes = to_modes(base, forward_ref, scale_ref)
+        refs[0][...] = modes
+        refs[1][...], refs[2][...] = modes_to_faces(modes, backward_ref)
 
 
 def restrict_kernel(ez_count, count, *refs):
-    (place_ref, w_ref, below_ref, above_ref, r_in_ref, restrict_ref, swaps_ref, x0, x1, x2, x3,
+    (below_ref, above_ref, base_ref, restrict_ref, swaps_ref, x0, x1, x2, x3,
      r_ref, part_ref, coarse, sums) = refs
-    lanes = 2 * w_ref.shape[1]
+    lanes = base_ref.shape[1]
     parts = 4
     width = lanes // parts
-    resid = r_in_ref[...] - joined(w_ref, below_ref, above_ref, 1.0)
+    resid = with_faces(base_ref[...], below_ref, above_ref, -1.0)
     r_ref[...] = resid
-    rows = hp_dot(restrict_ref[...], resid)
+    rows = wide_dot(restrict_ref[...], resid)
     b = rows[:8] + jnp.where(lane_layer((8, lanes), ez_count) == 0, rows[8:], 0.0)
+    pairs = []
     for i in range(parts):
         pair = jnp.concatenate(
             [b[:4, i * width : (i + 1) * width], b[4:, i * width : (i + 1) * width]], axis=1
         )
-        coarse[i] = hp_dot(jnp.concatenate([pair, pair], axis=0), swaps_ref[: 2 * width])
+        pairs += [pair, pair]
+    swapped_rows = move_lanes(jnp.concatenate(pairs, axis=0), swaps_ref[: 2 * width])
+    for i in range(parts):
+        coarse[i] = swapped_rows[8 * i : 8 * (i + 1)]
     sums[...] = jnp.zeros_like(sums)
     block = 2 * width
     for q, ref in enumerate((x0, x1, x2, x3)):
-        i = message_part(place_ref, q)
+        i = sender_of(ref, count, 5)
         mine = coarse[i]
         acc = factor_block(ref, count, 0) * mine[0:1]
         for vu in range(1, 4):
             acc = acc + factor_block(ref, count, vu) * mine[vu : vu + 1]
         sums[i, :count] = acc
     flat = sums[...].reshape(parts * sums.shape[1], block)
-    ones = jnp.ones((8, block), f32)
-    row = lax.dot_general(
-        ones, flat, (((1,), (1,)), ((), ())), precision=highest, preferred_element_type=f32
-    )
+    ones = jnp.ones((8, block), bf16)
+    high = flat.astype(bf16)
+    low = (flat - high.astype(f32)).astype(bf16)
+    across = lambda t: lax.dot_general(
+        ones, t, (((1,), (1,)), ((), ())), preferred_element_type=f32
+    )
+    row = across(high) + across(low)
     tile = jnp.concatenate(
         [row[0:1, i * 128 : (i + 1) * 128] for i in range(2 * parts)], axis=0
     )
@@ -796,7 +901,7 @@
 
 
 def prolong_kernel(ez_count, count, inner_levels, cols, groups, *refs):
-    (place_ref, all_ref, live_ref, swaps_ref, columns_ref, x0, x1, x2, x3,
+    (all_ref, live_ref, swaps_ref, columns_ref, x0, x1, x2, x3,
      w_ref, low_ref, high_ref, table, coarse) = refs
     lanes = 2 * w_ref.shape[1]
     parts = 4
@@ -805,7 +910,7 @@
     row_id = lax.broadcasted_iota(jnp.int32, all_ref.shape[1:], 0)
     lane_id = lax.broadcasted_iota(jnp.int32, all_ref.shape[1:], 1)
     level = (lax.rem(row_id, 2) * 128 + lane_id) // cols
-    mine = lax.shift_right_logical(jnp.full_like(level, lax.shift_right_logical(place_ref[0, 0], 24)), level)
+    mine = lax.shift_right_logical(jnp.full_like(level, sender_of(x0, count, 6)), level)
     base = jnp.zeros(all_ref.shape[1:], f32)
     for source in range(all_ref.shape[0]):
         theirs = lax.shift_right_logical(jnp.full_like(level, groups[source]), level)
@@ -820,38 +925,39 @@
         )
         total = jnp.where(level > inner_levels + bit, total + flip, total)
         step *= 2
-    total = total * live_ref[...]
+    total = total * live_ref[:8]
     turned = jnp.transpose(total)
     for i in range(parts):
         table[i, :128] = jnp.broadcast_to(turned[:, 2 * i : 2 * i + 1], (128, block))
         table[i, 128:] = jnp.broadcast_to(turned[:, 2 * i + 1 : 2 * i + 2], (128, block))
     for q, ref in enumerate((x0, x1, x2, x3)):
-        i = message_part(place_ref, q)
+        i = sender_of(ref, count, 5)
         y = table[i, :count]
         for vu in range(4):
             coarse[i, vu : vu + 1] = jnp.sum(
                 factor_block(ref, count, vu) * y, axis=0, keepdims=True
             )
+    unswapped = move_lanes(coarse[...].reshape(parts * 8, block), swaps_ref[2 * width :])
     lows, highs = [], []
     for i in range(parts):
-        pair = hp_dot(coarse[i], swaps_ref[2 * width :])
+        pair = unswapped[8 * i : 8 * (i + 1)]
         lows.append(pair[:4, :width])
         highs.append(pair[:4, width:])
     e = jnp.concatenate([jnp.concatenate(lows, axis=1), jnp.concatenate(highs, axis=1)], axis=0)
-    field = hp_dot(columns_ref[...], jnp.concatenate([jnp.zeros_like(e), e], axis=0))
+    field = wide_dot(columns_ref[...], jnp.concatenate([jnp.zeros_like(e), e], axis=0))
     assemble_local(field, w_ref, low_ref, high_ref, ez_count, True)
 
 
-def exit_kernel(keep, gain, *refs):
-    (place_ref, w_ref, below_ref, above_ref, d_ref, x_ref, columns_ref, gather_ref,
+def exit_kernel(scale, *refs):
+    (place_ref, below_ref, above_ref, x_ref, inv_root_ref, gather_ref,
      q0, q1, q2, q3, field, held) = refs
-    lanes = 2 * w_ref.shape[1]
+    lanes = x_ref.shape[1]
     parts = 4
     width = lanes // parts
     face = below_ref.shape[0]
     rows = x_ref.shape[0]
-    step = joined(w_ref, below_ref, above_ref, 0.5) * gain + keep * d_ref[...]
-    store_halves(field, (x_ref[...] + step) * columns_ref[:, 4:5])
+    final = with_faces(x_ref[...], below_ref, above_ref, scale)
+    store_halves(field, final * inv_root_ref[...])
     blocks = []
     for side in range(2):
         layers = [field[pl.ds(side * rows + c, face, stride=NODES), :] for c in range(NODES)]
@@ -865,7 +971,7 @@
         held[i, 0] = dealt[i * face : (i + 1) * face, :half]
         held[i, 1] = dealt[i * face : (i + 1) * face, half:]
     for q, ref in enumerate((q0, q1, q2, q3)):
-        ref[...] = held[message_part(place_ref, q)]
+        ref[...] = held[place_ref[8 + q, 0].astype(jnp.int32)]
 
 
 def call(kernel, name, out_shapes, args, scratch=()):
@@ -912,21 +1018,19 @@
     count = levels * cols
     message = (elem_x * face + 8 + 2 * count, z_count)
     spec = lambda space: pl.BlockSpec(memory_space=space)
-    *packed, place = pl.pallas_call(
-        functools.partial(pack_kernel, cols, codes),
+    packed = pl.pallas_call(
+        functools.partial(pack_kernel, cols, gy_count, codes),
         name="pack",
-        out_shape=[jax.ShapeDtypeStruct(message, f32)] * parts
-        + [jax.ShapeDtypeStruct((8, 128), jnp.int32)],
+        out_shape=[jax.ShapeDtypeStruct(message, f32)] * parts,
         in_specs=[spec(SMEM)] * 2 + [spec(pl.ANY)] * 5,
-        out_specs=[spec(pl.ANY)] * (parts + 1),
+        out_specs=[spec(pl.ANY)] * parts,
         scratch_shapes=[
             VMEM((parts,) + message, f32),
             VMEM(geometry.shape, f32),
             VMEM(disc_mask.shape, jnp.int32),
             VMEM(thrust.shape, f32),
             VMEM((count, xxt_factor.shape[2]), f32),
-            VMEM((8, 128), jnp.int32),
-            pltpu.SemaphoreType.DMA((2 * parts + 1,)),
+            pltpu.SemaphoreType.DMA((2 * parts,)),
             pltpu.SemaphoreType.DMA((elem_y * elem_x * nodes,)),
         ],
         compiler_params=pltpu.CompilerParams(vmem_limit_bytes=67043328),
@@ -941,30 +1045,51 @@
     sshape = (2 * rows, lanes // 2)
     hshape = (face, lanes)
     w, low, high, inv, den, live_tile = call(
-        functools.partial(entry_kernel, ez_count), "entry",
-        [sshape, hshape, hshape, fshape, fshape, (2 * parts, 128)],
-        [place, *received, tables["columns"], tables["deal"]],
+        functools.partial(entry_kernel, ez_count, count), "entry",
+        [sshape, hshape, hshape, fshape, fshape, (4 * parts, 128)],
+        [*received, tables["columns"]],
         [VMEM((parts, 2 * face + 8, z_count), f32)],
     )
     fwd, bwd = tables["forward"], tables["backward"]
-
-    def precond(w, low, high, resid):
-        prev, nxt = halo(low, high)
-        args = [w, prev, nxt] + ([] if resid is None else [resid]) + [fwd, bwd, inv]
-        return call(
-            functools.partial(precond_kernel, ez_count, resid is None), "precond",
-            [fshape, sshape, hshape, hshape], args,
-        )
-
-    def advance(w, low, high, d, x, keep, gain, keep_d):
-        prev, nxt = halo(low, high)
-        args = [w, prev, nxt] + ([] if keep == 0.0 else [d]) + ([] if x is None else [x])
+    fwd_face = tables["forward_face"]
+    work = [VMEM(sshape, f32)]
+
+    def faces(halos, own, average, scale, spectrum):
+        low, high, modes = call(
+            functools.partial(face_kernel, ez_count, average, scale), "face",
+            [hshape, hshape, fshape], [*halos, *own, spectrum, fwd_face, bwd],
+            [VMEM((4 * face, lanes // 2), f32)],
+        )
+        return halo(low, high), modes
+
+    def opened(field, halve, spectrum):
+        base, modes, *own = call(
+            functools.partial(open_kernel, halve), "open", [fshape, fshape, hshape, hshape],
+            [field, fwd, bwd, spectrum],
+        )
+        return base, modes, own
+
+    def rest_precond(halos, base, modes, more, d, sign, keep, gain):
+        resid, step, modes, *own = call(
+            functools.partial(rest_precond_kernel, ez_count, sign, keep, gain), "rest_precond",
+            [fshape, fshape, fshape, hshape, hshape],
+            [*halos, base, modes, more] + ([] if keep == 0.0 else [d]) + [fwd, bwd, den], work,
+        )
+        return resid, step, modes, own
+
+    def rest_apply(halos, step, modes, more, resid, x, scale, keep_d, go_on):
         out = call(
-            functools.partial(apply_kernel, ez_count, keep, gain, x is None, keep_d), "apply",
-            [fshape, sshape, hshape, hshape] + ([fshape] if keep_d else []),
-            args + [fwd, bwd, den],
-        )
-        return out[0], out[1], out[2], out[3], (out[4] if keep_d else None)
+            functools.partial(rest_apply_kernel, ez_count, scale, x is None, keep_d, go_on),
+            "rest_apply",
+            [fshape] * (2 + keep_d + go_on) + [hshape] * (2 * go_on),
+            [*halos, step, modes, more, resid] + ([] if x is None else [x]) + [bwd]
+            + ([fwd, inv] if go_on else []),
+            work,
+        )
+        x, base = out[:2]
+        d = out[2] if keep_d else None
+        modes, own = (out[2 + keep_d], out[3 + keep_d :]) if go_on else (None, None)
+        return x, base, d, modes, own
 
     center = 0.5 * (bound_high + bound_low)
     radius = 0.5 * (bound_high - bound_low)
@@ -976,47 +1101,72 @@
     gain = 2.0 * rho_new / radius
 
     x = None
-    resid = None
+    sign = 1.0
+    halos = halo(low, high)
+    base, modes, own = opened(w, False, inv)
     for cycle in range(CYCLES):
-        resid, u, low, high = precond(w, low, high, resid)
-        x, k, low, high, d = advance(u, low, high, None, x, 0.0, first_gain, True)
-        resid, u, low, high = precond(k, low, high, resid)
-        x, k, low, high, _ = advance(u, low, high, d, x, keep, gain, False)
-        prev, nxt = halo(low, high)
-        resid, partial = call(
-            functools.partial(restrict_kernel, ez_count, count), "restrict",
-            [fshape, (devices, 2 * parts, 128)],
-            [place, k, prev, nxt, resid, tables["restrict"], tables["swaps"], *received],
-            [VMEM((parts, 8, 2 * width), f32), VMEM((parts, 256, 2 * width), f32)],
-        )
-        everyone = lax.all_to_all(partial, axes, 0, 0)
-        f, low, high = call(
-            functools.partial(prolong_kernel, ez_count, count, inner_levels, cols, groups), "prolong",
-            [sshape, hshape, hshape],
-            [place, everyone, live_tile, tables["swaps"], tables["columns"],
-             *received],
-            [VMEM((parts, 256, 2 * width), f32), VMEM((parts, 8, 2 * width), f32)],
-        )
-        x, k, low, high, _ = advance(f, low, high, None, x, 0.0, 1.0, False)
-        resid, u, low, high = precond(k, low, high, resid)
-        x, k, low, high, d = advance(u, low, high, None, x, 0.0, first_gain, True)
-        resid, u, low, high = precond(k, low, high, resid)
-        if cycle < CYCLES - 1:
-            x, w, low, high, _ = advance(u, low, high, d, x, keep, gain, False)
-    prev, nxt = halo(low, high)
+        for post in (False, True):
+            ahead, more = faces(halos, own, True, sign, inv)
+            resid, step, modes, own = rest_precond(
+                halos, base, modes, more, None, sign, 0.0, first_gain
+            )
+            halos, more = faces(ahead, own, False, 0.5 * first_gain, den)
+            x, base, d, modes, own = rest_apply(
+                ahead, step, modes, more, resid, x, 0.5 * first_gain, True, True
+            )
+            sign = -1.0
+            ahead, more = faces(halos, own, True, sign, inv)
+            if post and cycle == CYCLES - 1:
+                total = call(
+                    functools.partial(close_kernel, ez_count, keep, gain), "close", [fshape],
+                    [modes, more, d, x, bwd], work,
+                )[0]
+                halos = ahead
+                break
+            resid, step, modes, own = rest_precond(
+                halos, base, modes, more, d, sign, keep, gain
+            )
+            halos, more = faces(ahead, own, False, 0.5 * gain, den)
+            x, base, _, modes, own = rest_apply(
+                ahead, step, modes, more, resid, x, 0.5 * gain, False, post
+            )
+            if post:
+                break
+            resid, partial = call(
+                functools.partial(restrict_kernel, ez_count, count), "restrict",
+                [fshape, (devices, 2 * parts, 128)],
+                [*halos, base, tables["restrict"], tables["swaps"], *received],
+                [VMEM((parts, 8, 2 * width), f32), VMEM((parts, 256, 2 * width), f32)],
+            )
+            everyone = lax.all_to_all(partial, axes, 0, 0)
+            f, low, high = call(
+                functools.partial(prolong_kernel, ez_count, count, inner_levels, cols, groups),
+                "prolong", [sshape, hshape, hshape],
+                [everyone, live_tile, tables["swaps"], tables["columns"], *received],
+                [VMEM((parts, 256, 2 * width), f32), VMEM((parts, 8, 2 * width), f32)],
+            )
+            ahead = halo(low, high)
+            step, modes, own = opened(f, True, den)
+            halos, more = faces(ahead, own, False, 0.5, den)
+            x, base, _, modes, own = rest_apply(
+                ahead, step, modes, more, resid, x, 0.5, False, True
+            )
     chunks = call(
-        functools.partial(exit_kernel, keep, gain), "exit",
+        functools.partial(exit_kernel, 0.5 * gain), "exit",
         [(2, face, z_count)] * parts,
-        [place, u, prev, nxt, d, x, tables["columns"], tables["gather"]],
+        [live_tile, *halos, total, tables["inv_root"], tables["gather"]],
         [VMEM(sshape, f32), VMEM((parts, 2, face, z_count), f32)],
     )
     back = [
         lax.ppermute(chunks[q], axes, [(t, s) for s, t in spread(q)]) for q in range(parts)
     ]
+    code = jnp.int32(codes[0])
+    for d in range(1, devices):
+        code = jnp.where(device == d, jnp.int32(codes[d]), code)
     stacked = jnp.stack(back)
     by_ey = jnp.stack(
         [
-            lax.dynamic_index_in_dim(stacked, field_of(place[0, 0], 16 + 2 * ey), 0, keepdims=False)
+            lax.dynamic_index_in_dim(stacked, field_of(code, 16 + 2 * ey), 0, keepdims=False)
             for ey in range(parts)
         ]
     )

time: 187 us -> 179 us (0.957)
  waiting for transfers between devices: 55.8 us -> 40.8 us
  Pallas kernels: 30.8 us -> 43.9 us
  between operations: 2.9 us -> 0.59 us
  local copies, waits for them, and re-layouts: 4.4 us -> 2.12 us
    ppermute x40, waiting for transfers between devices: 38.2 us -> 16.2 us  [halo(): return (lax.ppermute(high, axes, up), lax.ppermute(low, axes, down))]
    pallas_call x23 -> x43, Pallas kernels: 26.1 us -> 39.2 us  [call(): pl.pallas_call(kernel, name=name, out_shape=[jax.ShapeDtypeStruct(s, f32)...]
    ppermute x4, waiting for transfers between devices: 0.62 us -> 7.69 us  [fast_device(): lax.ppermute(chunks[q], axes, [(t, s) for s, t in spread(q)])]
  transfers between devices with their start and end apart: 48 -> 48, of which waited for: 27 -> 29; matrix products, arithmetic and copies ran while one was open for 0% -> 0% of each run, Pallas kernels for 0% -> 12%
where the time goes in v4:
time: 179 us; the launch traced here: 178 us
  starting transfers between devices  65.4 us (37%)
  Pallas kernels  43.9 us (25%)
  waiting for transfers between devices  40.8 us (23%)
  blocking collectives  25.3 us (14%)
  local copies, waits for them, and re-layouts  2.12 us (1%)
    ppermute x40, starting transfers between devices, halo(): return (lax.ppermute(high, axes, up), lax.ppermute(low, axes, down))  41.9 us
    pallas_call x43, Pallas kernels, call(): pl.pallas_call(kernel, name=name, out_shape=[jax.ShapeDtypeStruct(s, f32)...  39.2 us
    all_to_all x2, blocking collectives, fast_device(): everyone = lax.all_to_all(partial, axes, 0, 0)  25.3 us
    ppermute x4, waiting for transfers between devices, fast_device(): received = [lax.ppermute(packed[q], axes, spread(q)) for q in range(parts)]  17 us
    ppermute x40, waiting for transfers between devices, halo(): return (lax.ppermute(high, axes, up), lax.ppermute(low, axes, down))  16.2 us
    ppermute x4, starting transfers between devices, fast_device(): received = [lax.ppermute(packed[q], axes, spread(q)) for q in range(parts)]  13.5 us
    ppermute x4, starting transfers between devices, fast_device(): lax.ppermute(chunks[q], axes, [(t, s) for s, t in spread(q)])  9.98 us
    ppermute x4, waiting for transfers between devices, fast_device(): lax.ppermute(chunks[q], axes, [(t, s) for s, t in spread(q)])  7.69 us
  transfers between devices with their start and end apart: 48, of which 29 were waited for; matrix products, arithmetic and copies ran while one was open for 0% of the time, Pallas kernels for 12%

profile of v4, /device:TPU:0, one launch (start us, length us, event | category | flops | bytes accessed | tf_op | source)
XLA Modules:
  0.0 178.1 jit_solution(5285868354692588350)
XLA Ops:
  0.0 4.7 %pack.1 = (f32[520,256]{1,0:T(8,128)}, f32[520,256]{1,0:T(8,128)}, f32[520,256]{1,0:T(8,128)}, f32[520,256]{1,0:T(8,128)}) custom-call(s32[1]{0:T(128)} %bitcast.refs_0_, s32[6]{0:T(128)} %bitcast.17, f32[8,8,2,4,256]{4,3,2,1,0:T(4,128)} %refs_2_.6, f32[3,2,4,32]{3,2,1,0:T(4,128)} %refs_3_.5, s32[2,4,32]{2,1,0:T(4,128)} %refs_4_.6, f32[2,4,32]{2,1,0:T(4,128)} %refs_5_.23, ...), custom_call_target="tpu_custom_call" | custom-call | tf_op jit(solution)/shard_map/pack/pallas_call | solution.py:1021
  4.7 6.0 %collective-permute-start = (f32[520,256]{1,0:T(8,128)}, f32[520,256]{1,0:T(8,128)S(1)}, u32[]{:S(2)}, u32[]{:S(2)}) collective-permute-start(f32[520,256]{1,0:T(8,128)} %get-tuple-element.169), channel_id=1, source_target_pairs={{0,18},{1,0},{2,26},{3,10},{4,4},{5,28},{6,14},{7,22},{8,16},{9,8}... | collective-permute-start | bytes 1597448 | tf_op jit(solution)/shard_map/ppermute | solution.py:1041
  10.8 1.9 %collective-permute-start.1 = (f32[520,256]{1,0:T(8,128)}, f32[520,256]{1,0:T(8,128)S(1)}, u32[]{:S(2)}, u32[]{:S(2)}) collective-permute-start(f32[520,256]{1,0:T(8,128)} %get-tuple-element.170), channel_id=1, source_target_pairs={{0,19},{1,1},{2,27},{3,11},{4,5},{5,29},{6,15},{7,23},{8,17},{9,9}... | collective-permute-start | bytes 1597448 | tf_op jit(solution)/shard_map/ppermute | solution.py:1041
  12.7 3.3 %collective-permute-start.2 = (f32[520,256]{1,0:T(8,128)}, f32[520,256]{1,0:T(8,128)S(1)}, u32[]{:S(2)}, u32[]{:S(2)}) collective-permute-start(f32[520,256]{1,0:T(8,128)} %get-tuple-element.171), channel_id=1, source_target_pairs={{0,16},{1,8},{2,24},{3,2},{4,12},{5,30},{6,6},{7,20},{8,18},{9,0},... | collective-permute-start | bytes 1597448 | tf_op jit(solution)/shard_map/ppermute | solution.py:1041
  16.0 2.3 %collective-permute-start.3 = (f32[520,256]{1,0:T(8,128)}, f32[520,256]{1,0:T(8,128)S(1)}, u32[]{:S(2)}, u32[]{:S(2)}) collective-permute-start(f32[520,256]{1,0:T(8,128)} %get-tuple-element.172), channel_id=1, source_target_pairs={{0,17},{1,9},{2,25},{3,3},{4,13},{5,31},{6,7},{7,21},{8,19},{9,1},... | collective-permute-start | bytes 1597448 | tf_op jit(solution)/shard_map/ppermute | solution.py:1041
  18.3 10.3 %collective-permute-done.1.refs_1_.refs_6_.refs_5_ = f32[520,256]{1,0:T(8,128)S(1)} collective-permute-done((f32[520,256]{1,0:T(8,128)}, f32[520,256]{1,0:T(8,128)S(1)}, u32[]{:S(2)}, u32[]{:S(2)}) %collective-permute-start.1) | collective-permute-done | bytes 532512 | tf_op jit(solution)/shard_map/ppermute | solution.py:1041
  29.2 6.0 %collective-permute-done.3.refs_3_.refs_8_.refs_7_ = f32[520,256]{1,0:T(8,128)S(1)} collective-permute-done((f32[520,256]{1,0:T(8,128)}, f32[520,256]{1,0:T(8,128)S(1)}, u32[]{:S(2)}, u32[]{:S(2)}) %collective-permute-start.3) | collective-permute-done | bytes 532512 | tf_op jit(solution)/shard_map/ppermute | solution.py:1041
  36.1 1.2 entry.1
  37.4 3.6 %collective-permute-start.4 = (f32[64,256]{1,0:T(8,128)S(1)}, f32[64,256]{1,0:T(8,128)S(1)}, u32[]{:S(2)}, u32[]{:S(2)}) collective-permute-start(f32[64,256]{1,0:T(8,128)S(1)} %get-tuple-element.174), channel_id=1, source_target_pairs={{18,19},{19,16},{16,17},{17,0},{0,1},{1,8},{8,9},{9,24},{24,25},{2... | collective-permute-start | bytes 196616 | tf_op jit(solution)/shard_map/ppermute | solution.py:1016
  43.5 2.3 %collective-permute-start.6 = (f32[64,256]{1,0:T(8,128)S(1)}, f32[64,256]{1,0:T(8,128)S(1)}, u32[]{:S(2)}, u32[]{:S(2)}) collective-permute-start(f32[64,256]{1,0:T(8,128)S(1)} %get-tuple-element.180), channel_id=1, source_target_pairs={{18,19},{19,16},{16,17},{17,0},{0,1},{1,8},{8,9},{9,24},{24,25},{2... | collective-permute-start | bytes 196616 | tf_op jit(solution)/shard_map/ppermute | solution.py:1016
  45.8 1.2 rest_precond.7
  48.4 1.9 %collective-permute-start.8 = (f32[64,256]{1,0:T(8,128)S(1)}, f32[64,256]{1,0:T(8,128)S(1)}, u32[]{:S(2)}, u32[]{:S(2)}) collective-permute-start(f32[64,256]{1,0:T(8,128)S(1)} %get-tuple-element.188), channel_id=1, source_target_pairs={{18,19},{19,16},{16,17},{17,0},{0,1},{1,8},{8,9},{9,24},{24,25},{2... | collective-permute-start | bytes 196616 | tf_op jit(solution)/shard_map/ppermute | solution.py:1016
  50.3 1.3 rest_apply.9
  52.8 3.5 %collective-permute-start.10 = (f32[64,256]{1,0:T(8,128)S(1)}, f32[64,256]{1,0:T(8,128)S(1)}, u32[]{:S(2)}, u32[]{:S(2)}) collective-permute-start(f32[64,256]{1,0:T(8,128)S(1)} %get-tuple-element.196), channel_id=1, source_target_pairs={{18,19},{19,16},{16,17},{17,0},{0,1},{1,8},{8,9},{9,24},{24,25},{2... | collective-permute-start | bytes 196616 | tf_op jit(solution)/shard_map/ppermute | solution.py:1016
  56.3 1.3 rest_precond.8
  58.8 1.9 %collective-permute-start.12 = (f32[64,256]{1,0:T(8,128)S(1)}, f32[64,256]{1,0:T(8,128)S(1)}, u32[]{:S(2)}, u32[]{:S(2)}) collective-permute-start(f32[64,256]{1,0:T(8,128)S(1)} %get-tuple-element.204), channel_id=1, source_target_pairs={{18,19},{19,16},{16,17},{17,0},{0,1},{1,8},{8,9},{9,24},{24,25},{2... | collective-permute-start | bytes 196616 | tf_op jit(solution)/shard_map/ppermute | solution.py:1016
  61.5 1.2 collective-permute-done.12.refs_0_
  62.7 1.1 restrict.2
  63.8 14.6 %all_to_all.10.refs_0_ = f32[32,8,128]{2,1,0:T(8,128)S(1)} all-to-all(f32[32,8,128]{2,1,0:T(8,128)S(1)} %get-tuple-element.212), channel_id=1, replica_groups=mesh['gx'=4,'gy'=8] {'gx','gy'}, dimensions={0} | all-to-all | bytes 262144 | tf_op jit(solution)/shard_map/all_to_all | solution.py:1141
  78.4 1.2 prolong.2
  79.9 1.4 collective-permute-start.15
  82.0 1.3 collective-permute-done.14.refs_0_
  85.8 1.3 rest_apply.11
  90.4 1.3 rest_precond.9
  94.9 1.3 rest_apply.12
  99.3 1.3 rest_precond.10
  103.8 1.3 rest_apply.13
  108.2 1.3 rest_precond.11
  112.7 1.3 rest_apply.14
  117.1 1.3 rest_precond.12
  122.2 1.2 collective-permute-done.32.refs_0_
  123.5 1.1 restrict.3
  124.6 10.7 %all_to_all.11.refs_0_ = f32[32,8,128]{2,1,0:T(8,128)S(1)} all-to-all(f32[32,8,128]{2,1,0:T(8,128)S(1)} %get-tuple-element.292), channel_id=1, replica_groups=mesh['gx'=4,'gy'=8] {'gx','gy'}, dimensions={0} | all-to-all | bytes 262144 | tf_op jit(solution)/shard_map/all_to_all | solution.py:1141
  135.3 1.2 prolong.3
  136.8 1.4 collective-permute-start.35
  138.9 1.3 collective-permute-done.34.refs_0_
  141.8 1.1 collective-permute-start.37
  142.9 1.3 rest_apply.16
  147.4 1.3 rest_precond.13
  151.8 1.5 rest_apply.17
  156.9 1.2 collective-permute-done.42.refs_1_
  159.0 2.9 %collective-permute-start.47 = (f32[2,64,256]{2,1,0:T(8,128)S(1)}, f32[2,64,256]{2,1,0:T(8,128)S(1)}, u32[]{:S(2)}, u32[]{:S(2)}) collective-permute-start(f32[2,64,256]{2,1,0:T(8,128)S(1)} %get-tuple-element.332), channel_id=1, source_target_pairs={{17,0},{9,1},{25,2},{3,3},{13,4},{31,5},{7,6},{21,7},{19,8},{1,9},... | collective-permute-start | bytes 393224 | tf_op jit(solution)/shard_map/ppermute | solution.py:1161
  161.9 3.3 %collective-permute-start.46 = (f32[2,64,256]{2,1,0:T(8,128)S(1)}, f32[2,64,256]{2,1,0:T(8,128)S(1)}, u32[]{:S(2)}, u32[]{:S(2)}) collective-permute-start(f32[2,64,256]{2,1,0:T(8,128)S(1)} %get-tuple-element.331), channel_id=1, source_target_pairs={{16,0},{8,1},{24,2},{2,3},{12,4},{30,5},{6,6},{20,7},{18,8},{0,9},... | collective-permute-start | bytes 393224 | tf_op jit(solution)/shard_map/ppermute | solution.py:1161
  165.2 1.9 %collective-permute-start.45 = (f32[2,64,256]{2,1,0:T(8,128)S(1)}, f32[2,64,256]{2,1,0:T(8,128)S(1)}, u32[]{:S(2)}, u32[]{:S(2)}) collective-permute-start(f32[2,64,256]{2,1,0:T(8,128)S(1)} %get-tuple-element.330), channel_id=1, source_target_pairs={{19,0},{1,1},{27,2},{11,3},{5,4},{29,5},{15,6},{23,7},{17,8},{9,9}... | collective-permute-start | bytes 393224 | tf_op jit(solution)/shard_map/ppermute | solution.py:1161
  167.1 1.9 %collective-permute-start.44 = (f32[2,64,256]{2,1,0:T(8,128)S(1)}, f32[2,64,256]{2,1,0:T(8,128)S(1)}, u32[]{:S(2)}, u32[]{:S(2)}) collective-permute-start(f32[2,64,256]{2,1,0:T(8,128)S(1)} %get-tuple-element.329), channel_id=1, source_target_pairs={{18,0},{0,1},{26,2},{10,3},{4,4},{28,5},{14,6},{22,7},{16,8},{8,9}... | collective-permute-start | bytes 393224 | tf_op jit(solution)/shard_map/ppermute | solution.py:1161
  169.2 4.5 %collective-permute-done.45 = f32[2,64,256]{2,1,0:T(8,128)S(1)} collective-permute-done((f32[2,64,256]{2,1,0:T(8,128)S(1)}, f32[2,64,256]{2,1,0:T(8,128)S(1)}, u32[]{:S(2)}, u32[]{:S(2)}) %collective-permute-start.45) | collective-permute-done | bytes 131104 | tf_op jit(solution)/shard_map/ppermute | solution.py:1161
  173.7 3.2 %collective-permute-done.44 = f32[2,64,256]{2,1,0:T(8,128)S(1)} collective-permute-done((f32[2,64,256]{2,1,0:T(8,128)S(1)}, f32[2,64,256]{2,1,0:T(8,128)S(1)}, u32[]{:S(2)}, u32[]{:S(2)}) %collective-permute-start.44) | collective-permute-done | bytes 131104 | tf_op jit(solution)/shard_map/ppermute | solution.py:1161
  177.0 1.1 copy.17
  (116 shorter events, 51.8 us)
Async XLA Ops:
  4.7 13.6 %collective-permute-start = (f32[520,256]{1,0:T(8,128)}, f32[520,256]{1,0:T(8,128)S(1)}, u32[]{:S(2)}, u32[]{:S(2)}) collective-permute-start(f32[520,256]{1,0:T(8,128)} %get-tuple-element.169), channel_id=1, source_target_pairs={{0,18},{1,0},{2,26},{3,10},{4,4},{5,28},{6,14},{7,22},{8,16},{9,8}... | collective-permute-start | bytes 1597448 | tf_op jit(solution)/shard_map/ppermute | solution.py:1041
  10.8 17.9 %collective-permute-start.1 = (f32[520,256]{1,0:T(8,128)}, f32[520,256]{1,0:T(8,128)S(1)}, u32[]{:S(2)}, u32[]{:S(2)}) collective-permute-start(f32[520,256]{1,0:T(8,128)} %get-tuple-element.170), channel_id=1, source_target_pairs={{0,19},{1,1},{2,27},{3,11},{4,5},{5,29},{6,15},{7,23},{8,17},{9,9}... | collective-permute-start | bytes 1597448 | tf_op jit(solution)/shard_map/ppermute | solution.py:1041
  12.7 16.5 %collective-permute-start.2 = (f32[520,256]{1,0:T(8,128)}, f32[520,256]{1,0:T(8,128)S(1)}, u32[]{:S(2)}, u32[]{:S(2)}) collective-permute-start(f32[520,256]{1,0:T(8,128)} %get-tuple-element.171), channel_id=1, source_target_pairs={{0,16},{1,8},{2,24},{3,2},{4,12},{5,30},{6,6},{7,20},{8,18},{9,0},... | collective-permute-start | bytes 1597448 | tf_op jit(solution)/shard_map/ppermute | solution.py:1041
  16.0 19.3 %collective-permute-start.3 = (f32[520,256]{1,0:T(8,128)}, f32[520,256]{1,0:T(8,128)S(1)}, u32[]{:S(2)}, u32[]{:S(2)}) collective-permute-start(f32[520,256]{1,0:T(8,128)} %get-tuple-element.172), channel_id=1, source_target_pairs={{0,17},{1,9},{2,25},{3,3},{4,13},{5,31},{6,7},{7,21},{8,19},{9,1},... | collective-permute-start | bytes 1597448 | tf_op jit(solution)/shard_map/ppermute | solution.py:1041
  37.4 4.5 %collective-permute-start.4 = (f32[64,256]{1,0:T(8,128)S(1)}, f32[64,256]{1,0:T(8,128)S(1)}, u32[]{:S(2)}, u32[]{:S(2)}) collective-permute-start(f32[64,256]{1,0:T(8,128)S(1)} %get-tuple-element.174), channel_id=1, source_target_pairs={{18,19},{19,16},{16,17},{17,0},{0,1},{1,8},{8,9},{9,24},{24,25},{2... | collective-permute-start | bytes 196616 | tf_op jit(solution)/shard_map/ppermute | solution.py:1016
  41.0 1.9 %collective-permute-start.5 = (f32[64,256]{1,0:T(8,128)S(1)}, f32[64,256]{1,0:T(8,128)S(1)}, u32[]{:S(2)}, u32[]{:S(2)}) collective-permute-start(f32[64,256]{1,0:T(8,128)S(1)} %get-tuple-element.175), channel_id=1, source_target_pairs={{19,18},{16,19},{17,16},{0,17},{1,0},{8,1},{9,8},{24,9},{25,24},{2... | collective-permute-start | bytes 196616 | tf_op jit(solution)/shard_map/ppermute | solution.py:1016
  43.5 3.8 %collective-permute-start.6 = (f32[64,256]{1,0:T(8,128)S(1)}, f32[64,256]{1,0:T(8,128)S(1)}, u32[]{:S(2)}, u32[]{:S(2)}) collective-permute-start(f32[64,256]{1,0:T(8,128)S(1)} %get-tuple-element.180), channel_id=1, source_target_pairs={{18,19},{19,16},{16,17},{17,0},{0,1},{1,8},{8,9},{9,24},{24,25},{2... | collective-permute-start | bytes 196616 | tf_op jit(solution)/shard_map/ppermute | solution.py:1016
  45.8 1.9 %collective-permute-start.7 = (f32[64,256]{1,0:T(8,128)S(1)}, f32[64,256]{1,0:T(8,128)S(1)}, u32[]{:S(2)}, u32[]{:S(2)}) collective-permute-start(f32[64,256]{1,0:T(8,128)S(1)} %get-tuple-element.181), channel_id=1, source_target_pairs={{19,18},{16,19},{17,16},{0,17},{1,0},{8,1},{9,8},{24,9},{25,24},{2... | collective-permute-start | bytes 196616 | tf_op jit(solution)/shard_map/ppermute | solution.py:1016
  48.4 3.8 %collective-permute-start.8 = (f32[64,256]{1,0:T(8,128)S(1)}, f32[64,256]{1,0:T(8,128)S(1)}, u32[]{:S(2)}, u32[]{:S(2)}) collective-permute-start(f32[64,256]{1,0:T(8,128)S(1)} %get-tuple-element.188), channel_id=1, source_target_pairs={{18,19},{19,16},{16,17},{17,0},{0,1},{1,8},{8,9},{9,24},{24,25},{2... | collective-permute-start | bytes 196616 | tf_op jit(solution)/shard_map/ppermute | solution.py:1016
  50.3 1.9 %collective-permute-start.9 = (f32[64,256]{1,0:T(8,128)S(1)}, f32[64,256]{1,0:T(8,128)S(1)}, u32[]{:S(2)}, u32[]{:S(2)}) collective-permute-start(f32[64,256]{1,0:T(8,128)S(1)} %get-tuple-element.189), channel_id=1, source_target_pairs={{19,18},{16,19},{17,16},{0,17},{1,0},{8,1},{9,8},{24,9},{25,24},{2... | collective-permute-start | bytes 196616 | tf_op jit(solution)/shard_map/ppermute | solution.py:1016
  52.8 4.8 %collective-permute-start.10 = (f32[64,256]{1,0:T(8,128)S(1)}, f32[64,256]{1,0:T(8,128)S(1)}, u32[]{:S(2)}, u32[]{:S(2)}) collective-permute-start(f32[64,256]{1,0:T(8,128)S(1)} %get-tuple-element.196), channel_id=1, source_target_pairs={{18,19},{19,16},{16,17},{17,0},{0,1},{1,8},{8,9},{9,24},{24,25},{2... | collective-permute-start | bytes 196616 | tf_op jit(solution)/shard_map/ppermute | solution.py:1016
  56.3 1.9 %collective-permute-start.11 = (f32[64,256]{1,0:T(8,128)S(1)}, f32[64,256]{1,0:T(8,128)S(1)}, u32[]{:S(2)}, u32[]{:S(2)}) collective-permute-start(f32[64,256]{1,0:T(8,128)S(1)} %get-tuple-element.197), channel_id=1, source_target_pairs={{19,18},{16,19},{17,16},{0,17},{1,0},{8,1},{9,8},{24,9},{25,24},{2... | collective-permute-start | bytes 196616 | tf_op jit(solution)/shard_map/ppermute | solution.py:1016
  58.8 3.8 %collective-permute-start.12 = (f32[64,256]{1,0:T(8,128)S(1)}, f32[64,256]{1,0:T(8,128)S(1)}, u32[]{:S(2)}, u32[]{:S(2)}) collective-permute-start(f32[64,256]{1,0:T(8,128)S(1)} %get-tuple-element.204), channel_id=1, source_target_pairs={{18,19},{19,16},{16,17},{17,0},{0,1},{1,8},{8,9},{9,24},{24,25},{2... | collective-permute-start | bytes 196616 | tf_op jit(solution)/shard_map/ppermute | solution.py:1016
  60.8 1.9 %collective-permute-start.13 = (f32[64,256]{1,0:T(8,128)S(1)}, f32[64,256]{1,0:T(8,128)S(1)}, u32[]{:S(2)}, u32[]{:S(2)}) collective-permute-start(f32[64,256]{1,0:T(8,128)S(1)} %get-tuple-element.205), channel_id=1, source_target_pairs={{19,18},{16,19},{17,16},{0,17},{1,0},{8,1},{9,8},{24,9},{25,24},{2... | collective-permute-start | bytes 196616 | tf_op jit(solution)/shard_map/ppermute | solution.py:1016
  79.6 3.7 %collective-permute-start.14 = (f32[64,256]{1,0:T(8,128)S(1)}, f32[64,256]{1,0:T(8,128)S(1)}, u32[]{:S(2)}, u32[]{:S(2)}) collective-permute-start(f32[64,256]{1,0:T(8,128)S(1)} %get-tuple-element.213), channel_id=1, source_target_pairs={{18,19},{19,16},{16,17},{17,0},{0,1},{1,8},{8,9},{9,24},{24,25},{2... | collective-permute-start | bytes 196616 | tf_op jit(solution)/shard_map/ppermute | solution.py:1016
  79.9 3.4 %collective-permute-start.15 = (f32[64,256]{1,0:T(8,128)S(1)}, f32[64,256]{1,0:T(8,128)S(1)}, u32[]{:S(2)}, u32[]{:S(2)}) collective-permute-start(f32[64,256]{1,0:T(8,128)S(1)} %get-tuple-element.214), channel_id=1, source_target_pairs={{19,18},{16,19},{17,16},{0,17},{1,0},{8,1},{9,8},{24,9},{25,24},{2... | collective-permute-start | bytes 196616 | tf_op jit(solution)/shard_map/ppermute | solution.py:1016
  83.9 3.7 %collective-permute-start.16 = (f32[64,256]{1,0:T(8,128)S(1)}, f32[64,256]{1,0:T(8,128)S(1)}, u32[]{:S(2)}, u32[]{:S(2)}) collective-permute-start(f32[64,256]{1,0:T(8,128)S(1)} %get-tuple-element.218), channel_id=1, source_target_pairs={{18,19},{19,16},{16,17},{17,0},{0,1},{1,8},{8,9},{9,24},{24,25},{2... | collective-permute-start | bytes 196616 | tf_op jit(solution)/shard_map/ppermute | solution.py:1016
  84.9 2.8 %collective-permute-start.17 = (f32[64,256]{1,0:T(8,128)S(1)}, f32[64,256]{1,0:T(8,128)S(1)}, u32[]{:S(2)}, u32[]{:S(2)}) collective-permute-start(f32[64,256]{1,0:T(8,128)S(1)} %get-tuple-element.219), channel_id=1, source_target_pairs={{19,18},{16,19},{17,16},{0,17},{1,0},{8,1},{9,8},{24,9},{25,24},{2... | collective-permute-start | bytes 196616 | tf_op jit(solution)/shard_map/ppermute | solution.py:1016
  88.4 3.8 %collective-permute-start.18 = (f32[64,256]{1,0:T(8,128)S(1)}, f32[64,256]{1,0:T(8,128)S(1)}, u32[]{:S(2)}, u32[]{:S(2)}) collective-permute-start(f32[64,256]{1,0:T(8,128)S(1)} %get-tuple-element.227), channel_id=1, source_target_pairs={{18,19},{19,16},{16,17},{17,0},{0,1},{1,8},{8,9},{9,24},{24,25},{2... | collective-permute-start | bytes 196616 | tf_op jit(solution)/shard_map/ppermute | solution.py:1016
  89.4 3.0 %collective-permute-start.19 = (f32[64,256]{1,0:T(8,128)S(1)}, f32[64,256]{1,0:T(8,128)S(1)}, u32[]{:S(2)}, u32[]{:S(2)}) collective-permute-start(f32[64,256]{1,0:T(8,128)S(1)} %get-tuple-element.228), channel_id=1, source_target_pairs={{19,18},{16,19},{17,16},{0,17},{1,0},{8,1},{9,8},{24,9},{25,24},{2... | collective-permute-start | bytes 196616 | tf_op jit(solution)/shard_map/ppermute | solution.py:1016
  93.0 3.8 %collective-permute-start.20 = (f32[64,256]{1,0:T(8,128)S(1)}, f32[64,256]{1,0:T(8,128)S(1)}, u32[]{:S(2)}, u32[]{:S(2)}) collective-permute-start(f32[64,256]{1,0:T(8,128)S(1)} %get-tuple-element.234), channel_id=1, source_target_pairs={{18,19},{19,16},{16,17},{17,0},{0,1},{1,8},{8,9},{9,24},{24,25},{2... | collective-permute-start | bytes 196616 | tf_op jit(solution)/shard_map/ppermute | solution.py:1016
  94.0 2.8 %collective-permute-start.21 = (f32[64,256]{1,0:T(8,128)S(1)}, f32[64,256]{1,0:T(8,128)S(1)}, u32[]{:S(2)}, u32[]{:S(2)}) collective-permute-start(f32[64,256]{1,0:T(8,128)S(1)} %get-tuple-element.235), channel_id=1, source_target_pairs={{19,18},{16,19},{17,16},{0,17},{1,0},{8,1},{9,8},{24,9},{25,24},{2... | collective-permute-start | bytes 196616 | tf_op jit(solution)/shard_map/ppermute | solution.py:1016
  97.4 3.8 %collective-permute-start.22 = (f32[64,256]{1,0:T(8,128)S(1)}, f32[64,256]{1,0:T(8,128)S(1)}, u32[]{:S(2)}, u32[]{:S(2)}) collective-permute-start(f32[64,256]{1,0:T(8,128)S(1)} %get-tuple-element.243), channel_id=1, source_target_pairs={{18,19},{19,16},{16,17},{17,0},{0,1},{1,8},{8,9},{9,24},{24,25},{2... | collective-permute-start | bytes 196616 | tf_op jit(solution)/shard_map/ppermute | solution.py:1016
  98.5 2.8 %collective-permute-start.23 = (f32[64,256]{1,0:T(8,128)S(1)}, f32[64,256]{1,0:T(8,128)S(1)}, u32[]{:S(2)}, u32[]{:S(2)}) collective-permute-start(f32[64,256]{1,0:T(8,128)S(1)} %get-tuple-element.244), channel_id=1, source_target_pairs={{19,18},{16,19},{17,16},{0,17},{1,0},{8,1},{9,8},{24,9},{25,24},{2... | collective-permute-start | bytes 196616 | tf_op jit(solution)/shard_map/ppermute | solution.py:1016
  101.9 3.8 %collective-permute-start.24 = (f32[64,256]{1,0:T(8,128)S(1)}, f32[64,256]{1,0:T(8,128)S(1)}, u32[]{:S(2)}, u32[]{:S(2)}) collective-permute-start(f32[64,256]{1,0:T(8,128)S(1)} %get-tuple-element.251), channel_id=1, source_target_pairs={{18,19},{19,16},{16,17},{17,0},{0,1},{1,8},{8,9},{9,24},{24,25},{2... | collective-permute-start | bytes 196616 | tf_op jit(solution)/shard_map/ppermute | solution.py:1016
  102.9 2.8 %collective-permute-start.25 = (f32[64,256]{1,0:T(8,128)S(1)}, f32[64,256]{1,0:T(8,128)S(1)}, u32[]{:S(2)}, u32[]{:S(2)}) collective-permute-start(f32[64,256]{1,0:T(8,128)S(1)} %get-tuple-element.252), channel_id=1, source_target_pairs={{19,18},{16,19},{17,16},{0,17},{1,0},{8,1},{9,8},{24,9},{25,24},{2... | collective-permute-start | bytes 196616 | tf_op jit(solution)/shard_map/ppermute | solution.py:1016
  106.3 3.8 %collective-permute-start.26 = (f32[64,256]{1,0:T(8,128)S(1)}, f32[64,256]{1,0:T(8,128)S(1)}, u32[]{:S(2)}, u32[]{:S(2)}) collective-permute-start(f32[64,256]{1,0:T(8,128)S(1)} %get-tuple-element.260), channel_id=1, source_target_pairs={{18,19},{19,16},{16,17},{17,0},{0,1},{1,8},{8,9},{9,24},{24,25},{2... | collective-permute-start | bytes 196616 | tf_op jit(solution)/shard_map/ppermute | solution.py:1016
  107.4 2.8 %collective-permute-start.27 = (f32[64,256]{1,0:T(8,128)S(1)}, f32[64,256]{1,0:T(8,128)S(1)}, u32[]{:S(2)}, u32[]{:S(2)}) collective-permute-start(f32[64,256]{1,0:T(8,128)S(1)} %get-tuple-element.261), channel_id=1, source_target_pairs={{19,18},{16,19},{17,16},{0,17},{1,0},{8,1},{9,8},{24,9},{25,24},{2... | collective-permute-start | bytes 196616 | tf_op jit(solution)/shard_map/ppermute | solution.py:1016
  110.8 3.8 %collective-permute-start.28 = (f32[64,256]{1,0:T(8,128)S(1)}, f32[64,256]{1,0:T(8,128)S(1)}, u32[]{:S(2)}, u32[]{:S(2)}) collective-permute-start(f32[64,256]{1,0:T(8,128)S(1)} %get-tuple-element.267), channel_id=1, source_target_pairs={{18,19},{19,16},{16,17},{17,0},{0,1},{1,8},{8,9},{9,24},{24,25},{2... | collective-permute-start | bytes 196616 | tf_op jit(solution)/shard_map/ppermute | solution.py:1016
  111.8 2.8 %collective-permute-start.29 = (f32[64,256]{1,0:T(8,128)S(1)}, f32[64,256]{1,0:T(8,128)S(1)}, u32[]{:S(2)}, u32[]{:S(2)}) collective-permute-start(f32[64,256]{1,0:T(8,128)S(1)} %get-tuple-element.268), channel_id=1, source_target_pairs={{19,18},{16,19},{17,16},{0,17},{1,0},{8,1},{9,8},{24,9},{25,24},{2... | collective-permute-start | bytes 196616 | tf_op jit(solution)/shard_map/ppermute | solution.py:1016
  115.2 3.8 %collective-permute-start.30 = (f32[64,256]{1,0:T(8,128)S(1)}, f32[64,256]{1,0:T(8,128)S(1)}, u32[]{:S(2)}, u32[]{:S(2)}) collective-permute-start(f32[64,256]{1,0:T(8,128)S(1)} %get-tuple-element.276), channel_id=1, source_target_pairs={{18,19},{19,16},{16,17},{17,0},{0,1},{1,8},{8,9},{9,24},{24,25},{2... | collective-permute-start | bytes 196616 | tf_op jit(solution)/shard_map/ppermute | solution.py:1016
  116.2 2.8 %collective-permute-start.31 = (f32[64,256]{1,0:T(8,128)S(1)}, f32[64,256]{1,0:T(8,128)S(1)}, u32[]{:S(2)}, u32[]{:S(2)}) collective-permute-start(f32[64,256]{1,0:T(8,128)S(1)} %get-tuple-element.277), channel_id=1, source_target_pairs={{19,18},{16,19},{17,16},{0,17},{1,0},{8,1},{9,8},{24,9},{25,24},{2... | collective-permute-start | bytes 196616 | tf_op jit(solution)/shard_map/ppermute | solution.py:1016
  119.7 3.8 %collective-permute-start.32 = (f32[64,256]{1,0:T(8,128)S(1)}, f32[64,256]{1,0:T(8,128)S(1)}, u32[]{:S(2)}, u32[]{:S(2)}) collective-permute-start(f32[64,256]{1,0:T(8,128)S(1)} %get-tuple-element.284), channel_id=1, source_target_pairs={{18,19},{19,16},{16,17},{17,0},{0,1},{1,8},{8,9},{9,24},{24,25},{2... | collective-permute-start | bytes 196616 | tf_op jit(solution)/shard_map/ppermute | solution.py:1016
  120.7 2.8 %collective-permute-start.33 = (f32[64,256]{1,0:T(8,128)S(1)}, f32[64,256]{1,0:T(8,128)S(1)}, u32[]{:S(2)}, u32[]{:S(2)}) collective-permute-start(f32[64,256]{1,0:T(8,128)S(1)} %get-tuple-element.285), channel_id=1, source_target_pairs={{19,18},{16,19},{17,16},{0,17},{1,0},{8,1},{9,8},{24,9},{25,24},{2... | collective-permute-start | bytes 196616 | tf_op jit(solution)/shard_map/ppermute | solution.py:1016
  136.5 3.7 %collective-permute-start.34 = (f32[64,256]{1,0:T(8,128)S(1)}, f32[64,256]{1,0:T(8,128)S(1)}, u32[]{:S(2)}, u32[]{:S(2)}) collective-permute-start(f32[64,256]{1,0:T(8,128)S(1)} %get-tuple-element.293), channel_id=1, source_target_pairs={{18,19},{19,16},{16,17},{17,0},{0,1},{1,8},{8,9},{9,24},{24,25},{2... | collective-permute-start | bytes 196616 | tf_op jit(solution)/shard_map/ppermute | solution.py:1016
  136.8 3.4 %collective-permute-start.35 = (f32[64,256]{1,0:T(8,128)S(1)}, f32[64,256]{1,0:T(8,128)S(1)}, u32[]{:S(2)}, u32[]{:S(2)}) collective-permute-start(f32[64,256]{1,0:T(8,128)S(1)} %get-tuple-element.294), channel_id=1, source_target_pairs={{19,18},{16,19},{17,16},{0,17},{1,0},{8,1},{9,8},{24,9},{25,24},{2... | collective-permute-start | bytes 196616 | tf_op jit(solution)/shard_map/ppermute | solution.py:1016
  140.9 3.7 %collective-permute-start.36 = (f32[64,256]{1,0:T(8,128)S(1)}, f32[64,256]{1,0:T(8,128)S(1)}, u32[]{:S(2)}, u32[]{:S(2)}) collective-permute-start(f32[64,256]{1,0:T(8,128)S(1)} %get-tuple-element.298), channel_id=1, source_target_pairs={{18,19},{19,16},{16,17},{17,0},{0,1},{1,8},{8,9},{9,24},{24,25},{2... | collective-permute-start | bytes 196616 | tf_op jit(solution)/shard_map/ppermute | solution.py:1016
  141.8 3.0 %collective-permute-start.37 = (f32[64,256]{1,0:T(8,128)S(1)}, f32[64,256]{1,0:T(8,128)S(1)}, u32[]{:S(2)}, u32[]{:S(2)}) collective-permute-start(f32[64,256]{1,0:T(8,128)S(1)} %get-tuple-element.299), channel_id=1, source_target_pairs={{19,18},{16,19},{17,16},{0,17},{1,0},{8,1},{9,8},{24,9},{25,24},{2... | collective-permute-start | bytes 196616 | tf_op jit(solution)/shard_map/ppermute | solution.py:1016
  145.5 3.8 %collective-permute-start.38 = (f32[64,256]{1,0:T(8,128)S(1)}, f32[64,256]{1,0:T(8,128)S(1)}, u32[]{:S(2)}, u32[]{:S(2)}) collective-permute-start(f32[64,256]{1,0:T(8,128)S(1)} %get-tuple-element.307), channel_id=1, source_target_pairs={{18,19},{19,16},{16,17},{17,0},{0,1},{1,8},{8,9},{9,24},{24,25},{2... | collective-permute-start | bytes 196616 | tf_op jit(solution)/shard_map/ppermute | solution.py:1016
  146.5 2.8 %collective-permute-start.39 = (f32[64,256]{1,0:T(8,128)S(1)}, f32[64,256]{1,0:T(8,128)S(1)}, u32[]{:S(2)}, u32[]{:S(2)}) collective-permute-start(f32[64,256]{1,0:T(8,128)S(1)} %get-tuple-element.308), channel_id=1, source_target_pairs={{19,18},{16,19},{17,16},{0,17},{1,0},{8,1},{9,8},{24,9},{25,24},{2... | collective-permute-start | bytes 196616 | tf_op jit(solution)/shard_map/ppermute | solution.py:1016
  149.9 3.8 %collective-permute-start.40 = (f32[64,256]{1,0:T(8,128)S(1)}, f32[64,256]{1,0:T(8,128)S(1)}, u32[]{:S(2)}, u32[]{:S(2)}) collective-permute-start(f32[64,256]{1,0:T(8,128)S(1)} %get-tuple-element.314), channel_id=1, source_target_pairs={{18,19},{19,16},{16,17},{17,0},{0,1},{1,8},{8,9},{9,24},{24,25},{2... | collective-permute-start | bytes 196616 | tf_op jit(solution)/shard_map/ppermute | solution.py:1016
  151.0 2.8 %collective-permute-start.41 = (f32[64,256]{1,0:T(8,128)S(1)}, f32[64,256]{1,0:T(8,128)S(1)}, u32[]{:S(2)}, u32[]{:S(2)}) collective-permute-start(f32[64,256]{1,0:T(8,128)S(1)} %get-tuple-element.315), channel_id=1, source_target_pairs={{19,18},{16,19},{17,16},{0,17},{1,0},{8,1},{9,8},{24,9},{25,24},{2... | collective-permute-start | bytes 196616 | tf_op jit(solution)/shard_map/ppermute | solution.py:1016
  154.4 3.8 %collective-permute-start.42 = (f32[64,256]{1,0:T(8,128)S(1)}, f32[64,256]{1,0:T(8,128)S(1)}, u32[]{:S(2)}, u32[]{:S(2)}) collective-permute-start(f32[64,256]{1,0:T(8,128)S(1)} %get-tuple-element.323), channel_id=1, source_target_pairs={{18,19},{19,16},{16,17},{17,0},{0,1},{1,8},{8,9},{9,24},{24,25},{2... | collective-permute-start | bytes 196616 | tf_op jit(solution)/shard_map/ppermute | solution.py:1016
  155.4 2.8 %collective-permute-start.43 = (f32[64,256]{1,0:T(8,128)S(1)}, f32[64,256]{1,0:T(8,128)S(1)}, u32[]{:S(2)}, u32[]{:S(2)}) collective-permute-start(f32[64,256]{1,0:T(8,128)S(1)} %get-tuple-element.324), channel_id=1, source_target_pairs={{19,18},{16,19},{17,16},{0,17},{1,0},{8,1},{9,8},{24,9},{25,24},{2... | collective-permute-start | bytes 196616 | tf_op jit(solution)/shard_map/ppermute | solution.py:1016
  159.0 10.2 %collective-permute-start.47 = (f32[2,64,256]{2,1,0:T(8,128)S(1)}, f32[2,64,256]{2,1,0:T(8,128)S(1)}, u32[]{:S(2)}, u32[]{:S(2)}) collective-permute-start(f32[2,64,256]{2,1,0:T(8,128)S(1)} %get-tuple-element.332), channel_id=1, source_target_pairs={{17,0},{9,1},{25,2},{3,3},{13,4},{31,5},{7,6},{21,7},{19,8},{1,9},... | collective-permute-start | bytes 393224 | tf_op jit(solution)/shard_map/ppermute | solution.py:1161
  161.9 7.3 %collective-permute-start.46 = (f32[2,64,256]{2,1,0:T(8,128)S(1)}, f32[2,64,256]{2,1,0:T(8,128)S(1)}, u32[]{:S(2)}, u32[]{:S(2)}) collective-permute-start(f32[2,64,256]{2,1,0:T(8,128)S(1)} %get-tuple-element.331), channel_id=1, source_target_pairs={{16,0},{8,1},{24,2},{2,3},{12,4},{30,5},{6,6},{20,7},{18,8},{0,9},... | collective-permute-start | bytes 393224 | tf_op jit(solution)/shard_map/ppermute | solution.py:1161
  165.2 8.5 %collective-permute-start.45 = (f32[2,64,256]{2,1,0:T(8,128)S(1)}, f32[2,64,256]{2,1,0:T(8,128)S(1)}, u32[]{:S(2)}, u32[]{:S(2)}) collective-permute-start(f32[2,64,256]{2,1,0:T(8,128)S(1)} %get-tuple-element.330), channel_id=1, source_target_pairs={{19,0},{1,1},{27,2},{11,3},{5,4},{29,5},{15,6},{23,7},{17,8},{9,9}... | collective-permute-start | bytes 393224 | tf_op jit(solution)/shard_map/ppermute | solution.py:1161
  167.1 9.8 %collective-permute-start.44 = (f32[2,64,256]{2,1,0:T(8,128)S(1)}, f32[2,64,256]{2,1,0:T(8,128)S(1)}, u32[]{:S(2)}, u32[]{:S(2)}) collective-permute-start(f32[2,64,256]{2,1,0:T(8,128)S(1)} %get-tuple-element.329), channel_id=1, source_target_pairs={{18,0},{0,1},{26,2},{10,3},{4,4},{28,5},{14,6},{22,7},{16,8},{8,9}... | collective-permute-start | bytes 393224 | tf_op jit(solution)/shard_map/ppermute | solution.py:1161
  (9 other events, 102.4 us)

commit v5 on v4

--- a/solution.py
+++ b/solution.py
@@ -387,7 +387,7 @@
     for j in range(gy_count):
         far = [[hops(i, j, gx_count * j + s) for s in range(gx_count)] for i in range(gx_count)]
         cost = lambda rows: [max(far[i][row[i]] for i in range(gx_count)) for row in rows]
-        best = min(squares, key=lambda rows: (sum(cost(rows)), cost(rows)))
+        best = min(squares, key=lambda rows: (sum(cost(rows)), cost(rows)[::-1]))
         for q, row in enumerate(best):
             for i in range(gx_count):
                 send[i * gy_count + j, q] = row[i]

time: 179 us -> 177 us (0.989)
  blocking collectives: 25.3 us -> 23.3 us
    all_to_all x2, blocking collectives: 25.3 us -> 23.3 us  [fast_device(): everyone = lax.all_to_all(partial, axes, 0, 0)]
where the time goes in v5:
time: 177 us
  starting transfers between devices  64.5 us (36%)
  Pallas kernels  43.9 us (25%)
  waiting for transfers between devices  42.1 us (24%)
  blocking collectives  23.3 us (13%)
  local copies, waits for them, and re-layouts  2.12 us (1%)
    ppermute x40, starting transfers between devices, halo(): return (lax.ppermute(high, axes, up), lax.ppermute(low, axes, down))  40.6 us
    pallas_call x43, Pallas kernels, call(): pl.pallas_call(kernel, name=name, out_shape=[jax.ShapeDtypeStruct(s, f32)...  39.2 us
    all_to_all x2, blocking collectives, fast_device(): everyone = lax.all_to_all(partial, axes, 0, 0)  23.3 us
    ppermute x4, waiting for transfers between devices, fast_device(): received = [lax.ppermute(packed[q], axes, spread(q)) for q in range(parts)]  18.6 us
    ppermute x40, waiting for transfers between devices, halo(): return (lax.ppermute(high, axes, up), lax.ppermute(low, axes, down))  16.4 us
    ppermute x4, starting transfers between devices, fast_device(): received = [lax.ppermute(packed[q], axes, spread(q)) for q in range(parts)]  13.9 us
    ppermute x4, starting transfers between devices, fast_device(): lax.ppermute(chunks[q], axes, [(t, s) for s, t in spread(q)])  9.98 us
    ppermute x4, waiting for transfers between devices, fast_device(): lax.ppermute(chunks[q], axes, [(t, s) for s, t in spread(q)])  6.99 us
  transfers between devices with their start and end apart: 48, of which 29 were waited for; matrix products, arithmetic and copies ran while one was open for 0% of the time, Pallas kernels for 12%

profile of v5, /device:TPU:0, one launch (start us, length us, event | category | flops | bytes accessed | tf_op | source)
XLA Modules:
  0.0 176.5 jit_solution(5603233107289809997)
XLA Ops:
  0.0 4.7 %pack.1 = (f32[520,256]{1,0:T(8,128)}, f32[520,256]{1,0:T(8,128)}, f32[520,256]{1,0:T(8,128)}, f32[520,256]{1,0:T(8,128)}) custom-call(s32[1]{0:T(128)} %bitcast.refs_0_, s32[6]{0:T(128)} %bitcast.17, f32[8,8,2,4,256]{4,3,2,1,0:T(4,128)} %refs_2_.6, f32[3,2,4,32]{3,2,1,0:T(4,128)} %refs_3_.5, s32[2,4,32]{2,1,0:T(4,128)} %refs_4_.6, f32[2,4,32]{2,1,0:T(4,128)} %refs_5_.23, ...), custom_call_target="tpu_custom_call" | custom-call | tf_op jit(solution)/shard_map/pack/pallas_call | solution.py:1021
  4.7 6.0 %collective-permute-start = (f32[520,256]{1,0:T(8,128)}, f32[520,256]{1,0:T(8,128)S(1)}, u32[]{:S(2)}, u32[]{:S(2)}) collective-permute-start(f32[520,256]{1,0:T(8,128)} %get-tuple-element.169), channel_id=1, source_target_pairs={{0,18},{1,0},{2,24},{3,10},{4,4},{5,30},{6,14},{7,22},{8,19},{9,8}... | collective-permute-start | bytes 1597448 | tf_op jit(solution)/shard_map/ppermute | solution.py:1041
  10.8 2.5 %collective-permute-start.1 = (f32[520,256]{1,0:T(8,128)}, f32[520,256]{1,0:T(8,128)S(1)}, u32[]{:S(2)}, u32[]{:S(2)}) collective-permute-start(f32[520,256]{1,0:T(8,128)} %get-tuple-element.170), channel_id=1, source_target_pairs={{0,19},{1,1},{2,25},{3,11},{4,5},{5,31},{6,15},{7,23},{8,18},{9,9}... | collective-permute-start | bytes 1597448 | tf_op jit(solution)/shard_map/ppermute | solution.py:1041
  13.3 1.9 %collective-permute-start.2 = (f32[520,256]{1,0:T(8,128)}, f32[520,256]{1,0:T(8,128)S(1)}, u32[]{:S(2)}, u32[]{:S(2)}) collective-permute-start(f32[520,256]{1,0:T(8,128)} %get-tuple-element.171), channel_id=1, source_target_pairs={{0,16},{1,8},{2,26},{3,2},{4,12},{5,28},{6,6},{7,20},{8,17},{9,0},... | collective-permute-start | bytes 1597448 | tf_op jit(solution)/shard_map/ppermute | solution.py:1041
  15.2 3.4 %collective-permute-start.3 = (f32[520,256]{1,0:T(8,128)}, f32[520,256]{1,0:T(8,128)S(1)}, u32[]{:S(2)}, u32[]{:S(2)}) collective-permute-start(f32[520,256]{1,0:T(8,128)} %get-tuple-element.172), channel_id=1, source_target_pairs={{0,17},{1,9},{2,27},{3,3},{4,13},{5,29},{6,7},{7,21},{8,16},{9,1},... | collective-permute-start | bytes 1597448 | tf_op jit(solution)/shard_map/ppermute | solution.py:1041
  18.6 4.4 %collective-permute-done.refs_0_.refs_5_.refs_4_ = f32[520,256]{1,0:T(8,128)S(1)} collective-permute-done((f32[520,256]{1,0:T(8,128)}, f32[520,256]{1,0:T(8,128)S(1)}, u32[]{:S(2)}, u32[]{:S(2)}) %collective-permute-start) | collective-permute-done | bytes 532512 | tf_op jit(solution)/shard_map/ppermute | solution.py:1041
  23.0 11.9 %collective-permute-done.1.refs_1_.refs_6_.refs_5_ = f32[520,256]{1,0:T(8,128)S(1)} collective-permute-done((f32[520,256]{1,0:T(8,128)}, f32[520,256]{1,0:T(8,128)S(1)}, u32[]{:S(2)}, u32[]{:S(2)}) %collective-permute-start.1) | collective-permute-done | bytes 532512 | tf_op jit(solution)/shard_map/ppermute | solution.py:1041
  34.9 2.3 %collective-permute-done.3.refs_3_.refs_8_.refs_7_ = f32[520,256]{1,0:T(8,128)S(1)} collective-permute-done((f32[520,256]{1,0:T(8,128)}, f32[520,256]{1,0:T(8,128)S(1)}, u32[]{:S(2)}, u32[]{:S(2)}) %collective-permute-start.3) | collective-permute-done | bytes 532512 | tf_op jit(solution)/shard_map/ppermute | solution.py:1041
  38.1 1.2 entry.1
  39.4 2.3 %collective-permute-start.4 = (f32[64,256]{1,0:T(8,128)S(1)}, f32[64,256]{1,0:T(8,128)S(1)}, u32[]{:S(2)}, u32[]{:S(2)}) collective-permute-start(f32[64,256]{1,0:T(8,128)S(1)} %get-tuple-element.174), channel_id=1, source_target_pairs={{18,19},{19,16},{16,17},{17,0},{0,1},{1,8},{8,9},{9,24},{24,25},{2... | collective-permute-start | bytes 196616 | tf_op jit(solution)/shard_map/ppermute | solution.py:1016
  44.5 3.0 %collective-permute-start.6 = (f32[64,256]{1,0:T(8,128)S(1)}, f32[64,256]{1,0:T(8,128)S(1)}, u32[]{:S(2)}, u32[]{:S(2)}) collective-permute-start(f32[64,256]{1,0:T(8,128)S(1)} %get-tuple-element.180), channel_id=1, source_target_pairs={{18,19},{19,16},{16,17},{17,0},{0,1},{1,8},{8,9},{9,24},{24,25},{2... | collective-permute-start | bytes 196616 | tf_op jit(solution)/shard_map/ppermute | solution.py:1016
  47.5 1.2 rest_precond.7
  50.1 1.9 %collective-permute-start.8 = (f32[64,256]{1,0:T(8,128)S(1)}, f32[64,256]{1,0:T(8,128)S(1)}, u32[]{:S(2)}, u32[]{:S(2)}) collective-permute-start(f32[64,256]{1,0:T(8,128)S(1)} %get-tuple-element.188), channel_id=1, source_target_pairs={{18,19},{19,16},{16,17},{17,0},{0,1},{1,8},{8,9},{9,24},{24,25},{2... | collective-permute-start | bytes 196616 | tf_op jit(solution)/shard_map/ppermute | solution.py:1016
  52.0 1.3 rest_apply.9
  54.5 2.6 %collective-permute-start.10 = (f32[64,256]{1,0:T(8,128)S(1)}, f32[64,256]{1,0:T(8,128)S(1)}, u32[]{:S(2)}, u32[]{:S(2)}) collective-permute-start(f32[64,256]{1,0:T(8,128)S(1)} %get-tuple-element.196), channel_id=1, source_target_pairs={{18,19},{19,16},{16,17},{17,0},{0,1},{1,8},{8,9},{9,24},{24,25},{2... | collective-permute-start | bytes 196616 | tf_op jit(solution)/shard_map/ppermute | solution.py:1016
  57.1 1.3 rest_precond.8
  59.6 1.9 %collective-permute-start.12 = (f32[64,256]{1,0:T(8,128)S(1)}, f32[64,256]{1,0:T(8,128)S(1)}, u32[]{:S(2)}, u32[]{:S(2)}) collective-permute-start(f32[64,256]{1,0:T(8,128)S(1)} %get-tuple-element.204), channel_id=1, source_target_pairs={{18,19},{19,16},{16,17},{17,0},{0,1},{1,8},{8,9},{9,24},{24,25},{2... | collective-permute-start | bytes 196616 | tf_op jit(solution)/shard_map/ppermute | solution.py:1016
  62.5 1.2 collective-permute-done.12.refs_0_
  63.7 1.1 restrict.2
  64.8 12.6 %all_to_all.10.refs_0_ = f32[32,8,128]{2,1,0:T(8,128)S(1)} all-to-all(f32[32,8,128]{2,1,0:T(8,128)S(1)} %get-tuple-element.212), channel_id=1, replica_groups=mesh['gx'=4,'gy'=8] {'gx','gy'}, dimensions={0} | all-to-all | bytes 262144 | tf_op jit(solution)/shard_map/all_to_all | solution.py:1141
  77.4 1.2 prolong.2
  79.0 1.5 collective-permute-start.15
  81.1 1.3 collective-permute-done.14.refs_0_
  84.9 1.3 rest_apply.11
  89.5 1.3 rest_precond.9
  94.0 1.3 rest_apply.12
  98.4 1.3 rest_precond.10
  102.8 1.3 rest_apply.13
  107.3 1.3 rest_precond.11
  111.7 1.3 rest_apply.14
  116.2 1.3 rest_precond.12
  121.3 1.2 collective-permute-done.32.refs_0_
  123.6 10.7 %all_to_all.11.refs_0_ = f32[32,8,128]{2,1,0:T(8,128)S(1)} all-to-all(f32[32,8,128]{2,1,0:T(8,128)S(1)} %get-tuple-element.292), channel_id=1, replica_groups=mesh['gx'=4,'gy'=8] {'gx','gy'}, dimensions={0} | all-to-all | bytes 262144 | tf_op jit(solution)/shard_map/all_to_all | solution.py:1141
  134.4 1.2 prolong.3
  135.9 1.4 collective-permute-start.35
  138.0 1.3 collective-permute-done.34.refs_0_
  140.9 1.1 collective-permute-start.37
  142.0 1.3 rest_apply.16
  146.5 1.3 rest_precond.13
  150.9 1.5 rest_apply.17
  156.0 1.2 collective-permute-done.42.refs_1_
  158.1 3.7 %collective-permute-start.47 = (f32[2,64,256]{2,1,0:T(8,128)S(1)}, f32[2,64,256]{2,1,0:T(8,128)S(1)}, u32[]{:S(2)}, u32[]{:S(2)}) collective-permute-start(f32[2,64,256]{2,1,0:T(8,128)S(1)} %get-tuple-element.332), channel_id=1, source_target_pairs={{17,0},{9,1},{27,2},{3,3},{13,4},{29,5},{7,6},{21,7},{16,8},{1,9},... | collective-permute-start | bytes 393224 | tf_op jit(solution)/shard_map/ppermute | solution.py:1161
  161.8 2.4 %collective-permute-start.46 = (f32[2,64,256]{2,1,0:T(8,128)S(1)}, f32[2,64,256]{2,1,0:T(8,128)S(1)}, u32[]{:S(2)}, u32[]{:S(2)}) collective-permute-start(f32[2,64,256]{2,1,0:T(8,128)S(1)} %get-tuple-element.331), channel_id=1, source_target_pairs={{16,0},{8,1},{26,2},{2,3},{12,4},{28,5},{6,6},{20,7},{17,8},{0,9},... | collective-permute-start | bytes 393224 | tf_op jit(solution)/shard_map/ppermute | solution.py:1161
  164.2 1.9 %collective-permute-start.45 = (f32[2,64,256]{2,1,0:T(8,128)S(1)}, f32[2,64,256]{2,1,0:T(8,128)S(1)}, u32[]{:S(2)}, u32[]{:S(2)}) collective-permute-start(f32[2,64,256]{2,1,0:T(8,128)S(1)} %get-tuple-element.330), channel_id=1, source_target_pairs={{19,0},{1,1},{25,2},{11,3},{5,4},{31,5},{15,6},{23,7},{18,8},{9,9}... | collective-permute-start | bytes 393224 | tf_op jit(solution)/shard_map/ppermute | solution.py:1161
  166.2 1.9 %collective-permute-start.44 = (f32[2,64,256]{2,1,0:T(8,128)S(1)}, f32[2,64,256]{2,1,0:T(8,128)S(1)}, u32[]{:S(2)}, u32[]{:S(2)}) collective-permute-start(f32[2,64,256]{2,1,0:T(8,128)S(1)} %get-tuple-element.329), channel_id=1, source_target_pairs={{18,0},{0,1},{24,2},{10,3},{4,4},{30,5},{14,6},{22,7},{19,8},{8,9}... | collective-permute-start | bytes 393224 | tf_op jit(solution)/shard_map/ppermute | solution.py:1161
  168.6 3.5 %collective-permute-done.45 = f32[2,64,256]{2,1,0:T(8,128)S(1)} collective-permute-done((f32[2,64,256]{2,1,0:T(8,128)S(1)}, f32[2,64,256]{2,1,0:T(8,128)S(1)}, u32[]{:S(2)}, u32[]{:S(2)}) %collective-permute-start.45) | collective-permute-done | bytes 131104 | tf_op jit(solution)/shard_map/ppermute | solution.py:1161
  172.1 3.1 %collective-permute-done.44 = f32[2,64,256]{2,1,0:T(8,128)S(1)} collective-permute-done((f32[2,64,256]{2,1,0:T(8,128)S(1)}, f32[2,64,256]{2,1,0:T(8,128)S(1)}, u32[]{:S(2)}, u32[]{:S(2)}) %collective-permute-start.44) | collective-permute-done | bytes 131104 | tf_op jit(solution)/shard_map/ppermute | solution.py:1161
  175.4 1.1 copy.17
  (116 shorter events, 53.2 us)
Async XLA Ops:
  4.7 18.3 %collective-permute-start = (f32[520,256]{1,0:T(8,128)}, f32[520,256]{1,0:T(8,128)S(1)}, u32[]{:S(2)}, u32[]{:S(2)}) collective-permute-start(f32[520,256]{1,0:T(8,128)} %get-tuple-element.169), channel_id=1, source_target_pairs={{0,18},{1,0},{2,24},{3,10},{4,4},{5,30},{6,14},{7,22},{8,19},{9,8}... | collective-permute-start | bytes 1597448 | tf_op jit(solution)/shard_map/ppermute | solution.py:1041
  10.8 24.1 %collective-permute-start.1 = (f32[520,256]{1,0:T(8,128)}, f32[520,256]{1,0:T(8,128)S(1)}, u32[]{:S(2)}, u32[]{:S(2)}) collective-permute-start(f32[520,256]{1,0:T(8,128)} %get-tuple-element.170), channel_id=1, source_target_pairs={{0,19},{1,1},{2,25},{3,11},{4,5},{5,31},{6,15},{7,23},{8,18},{9,9}... | collective-permute-start | bytes 1597448 | tf_op jit(solution)/shard_map/ppermute | solution.py:1041
  13.3 21.6 %collective-permute-start.2 = (f32[520,256]{1,0:T(8,128)}, f32[520,256]{1,0:T(8,128)S(1)}, u32[]{:S(2)}, u32[]{:S(2)}) collective-permute-start(f32[520,256]{1,0:T(8,128)} %get-tuple-element.171), channel_id=1, source_target_pairs={{0,16},{1,8},{2,26},{3,2},{4,12},{5,28},{6,6},{7,20},{8,17},{9,0},... | collective-permute-start | bytes 1597448 | tf_op jit(solution)/shard_map/ppermute | solution.py:1041
  15.2 22.0 %collective-permute-start.3 = (f32[520,256]{1,0:T(8,128)}, f32[520,256]{1,0:T(8,128)S(1)}, u32[]{:S(2)}, u32[]{:S(2)}) collective-permute-start(f32[520,256]{1,0:T(8,128)} %get-tuple-element.172), channel_id=1, source_target_pairs={{0,17},{1,9},{2,27},{3,3},{4,13},{5,29},{6,7},{7,21},{8,16},{9,1},... | collective-permute-start | bytes 1597448 | tf_op jit(solution)/shard_map/ppermute | solution.py:1041
  39.4 3.9 %collective-permute-start.4 = (f32[64,256]{1,0:T(8,128)S(1)}, f32[64,256]{1,0:T(8,128)S(1)}, u32[]{:S(2)}, u32[]{:S(2)}) collective-permute-start(f32[64,256]{1,0:T(8,128)S(1)} %get-tuple-element.174), channel_id=1, source_target_pairs={{18,19},{19,16},{16,17},{17,0},{0,1},{1,8},{8,9},{9,24},{24,25},{2... | collective-permute-start | bytes 196616 | tf_op jit(solution)/shard_map/ppermute | solution.py:1016
  41.7 2.2 %collective-permute-start.5 = (f32[64,256]{1,0:T(8,128)S(1)}, f32[64,256]{1,0:T(8,128)S(1)}, u32[]{:S(2)}, u32[]{:S(2)}) collective-permute-start(f32[64,256]{1,0:T(8,128)S(1)} %get-tuple-element.175), channel_id=1, source_target_pairs={{19,18},{16,19},{17,16},{0,17},{1,0},{8,1},{9,8},{24,9},{25,24},{2... | collective-permute-start | bytes 196616 | tf_op jit(solution)/shard_map/ppermute | solution.py:1016
  44.5 4.2 %collective-permute-start.6 = (f32[64,256]{1,0:T(8,128)S(1)}, f32[64,256]{1,0:T(8,128)S(1)}, u32[]{:S(2)}, u32[]{:S(2)}) collective-permute-start(f32[64,256]{1,0:T(8,128)S(1)} %get-tuple-element.180), channel_id=1, source_target_pairs={{18,19},{19,16},{16,17},{17,0},{0,1},{1,8},{8,9},{9,24},{24,25},{2... | collective-permute-start | bytes 196616 | tf_op jit(solution)/shard_map/ppermute | solution.py:1016
  47.5 1.9 %collective-permute-start.7 = (f32[64,256]{1,0:T(8,128)S(1)}, f32[64,256]{1,0:T(8,128)S(1)}, u32[]{:S(2)}, u32[]{:S(2)}) collective-permute-start(f32[64,256]{1,0:T(8,128)S(1)} %get-tuple-element.181), channel_id=1, source_target_pairs={{19,18},{16,19},{17,16},{0,17},{1,0},{8,1},{9,8},{24,9},{25,24},{2... | collective-permute-start | bytes 196616 | tf_op jit(solution)/shard_map/ppermute | solution.py:1016
  50.1 3.8 %collective-permute-start.8 = (f32[64,256]{1,0:T(8,128)S(1)}, f32[64,256]{1,0:T(8,128)S(1)}, u32[]{:S(2)}, u32[]{:S(2)}) collective-permute-start(f32[64,256]{1,0:T(8,128)S(1)} %get-tuple-element.188), channel_id=1, source_target_pairs={{18,19},{19,16},{16,17},{17,0},{0,1},{1,8},{8,9},{9,24},{24,25},{2... | collective-permute-start | bytes 196616 | tf_op jit(solution)/shard_map/ppermute | solution.py:1016
  52.0 1.9 %collective-permute-start.9 = (f32[64,256]{1,0:T(8,128)S(1)}, f32[64,256]{1,0:T(8,128)S(1)}, u32[]{:S(2)}, u32[]{:S(2)}) collective-permute-start(f32[64,256]{1,0:T(8,128)S(1)} %get-tuple-element.189), channel_id=1, source_target_pairs={{19,18},{16,19},{17,16},{0,17},{1,0},{8,1},{9,8},{24,9},{25,24},{2... | collective-permute-start | bytes 196616 | tf_op jit(solution)/shard_map/ppermute | solution.py:1016
  54.5 3.8 %collective-permute-start.10 = (f32[64,256]{1,0:T(8,128)S(1)}, f32[64,256]{1,0:T(8,128)S(1)}, u32[]{:S(2)}, u32[]{:S(2)}) collective-permute-start(f32[64,256]{1,0:T(8,128)S(1)} %get-tuple-element.196), channel_id=1, source_target_pairs={{18,19},{19,16},{16,17},{17,0},{0,1},{1,8},{8,9},{9,24},{24,25},{2... | collective-permute-start | bytes 196616 | tf_op jit(solution)/shard_map/ppermute | solution.py:1016
  57.1 1.9 %collective-permute-start.11 = (f32[64,256]{1,0:T(8,128)S(1)}, f32[64,256]{1,0:T(8,128)S(1)}, u32[]{:S(2)}, u32[]{:S(2)}) collective-permute-start(f32[64,256]{1,0:T(8,128)S(1)} %get-tuple-element.197), channel_id=1, source_target_pairs={{19,18},{16,19},{17,16},{0,17},{1,0},{8,1},{9,8},{24,9},{25,24},{2... | collective-permute-start | bytes 196616 | tf_op jit(solution)/shard_map/ppermute | solution.py:1016
  59.6 4.1 %collective-permute-start.12 = (f32[64,256]{1,0:T(8,128)S(1)}, f32[64,256]{1,0:T(8,128)S(1)}, u32[]{:S(2)}, u32[]{:S(2)}) collective-permute-start(f32[64,256]{1,0:T(8,128)S(1)} %get-tuple-element.204), channel_id=1, source_target_pairs={{18,19},{19,16},{16,17},{17,0},{0,1},{1,8},{8,9},{9,24},{24,25},{2... | collective-permute-start | bytes 196616 | tf_op jit(solution)/shard_map/ppermute | solution.py:1016
  61.5 2.2 %collective-permute-start.13 = (f32[64,256]{1,0:T(8,128)S(1)}, f32[64,256]{1,0:T(8,128)S(1)}, u32[]{:S(2)}, u32[]{:S(2)}) collective-permute-start(f32[64,256]{1,0:T(8,128)S(1)} %get-tuple-element.205), channel_id=1, source_target_pairs={{19,18},{16,19},{17,16},{0,17},{1,0},{8,1},{9,8},{24,9},{25,24},{2... | collective-permute-start | bytes 196616 | tf_op jit(solution)/shard_map/ppermute | solution.py:1016
  78.6 3.7 %collective-permute-start.14 = (f32[64,256]{1,0:T(8,128)S(1)}, f32[64,256]{1,0:T(8,128)S(1)}, u32[]{:S(2)}, u32[]{:S(2)}) collective-permute-start(f32[64,256]{1,0:T(8,128)S(1)} %get-tuple-element.213), channel_id=1, source_target_pairs={{18,19},{19,16},{16,17},{17,0},{0,1},{1,8},{8,9},{9,24},{24,25},{2... | collective-permute-start | bytes 196616 | tf_op jit(solution)/shard_map/ppermute | solution.py:1016
  79.0 3.4 %collective-permute-start.15 = (f32[64,256]{1,0:T(8,128)S(1)}, f32[64,256]{1,0:T(8,128)S(1)}, u32[]{:S(2)}, u32[]{:S(2)}) collective-permute-start(f32[64,256]{1,0:T(8,128)S(1)} %get-tuple-element.214), channel_id=1, source_target_pairs={{19,18},{16,19},{17,16},{0,17},{1,0},{8,1},{9,8},{24,9},{25,24},{2... | collective-permute-start | bytes 196616 | tf_op jit(solution)/shard_map/ppermute | solution.py:1016
  83.0 3.7 %collective-permute-start.16 = (f32[64,256]{1,0:T(8,128)S(1)}, f32[64,256]{1,0:T(8,128)S(1)}, u32[]{:S(2)}, u32[]{:S(2)}) collective-permute-start(f32[64,256]{1,0:T(8,128)S(1)} %get-tuple-element.218), channel_id=1, source_target_pairs={{18,19},{19,16},{16,17},{17,0},{0,1},{1,8},{8,9},{9,24},{24,25},{2... | collective-permute-start | bytes 196616 | tf_op jit(solution)/shard_map/ppermute | solution.py:1016
  84.0 2.8 %collective-permute-start.17 = (f32[64,256]{1,0:T(8,128)S(1)}, f32[64,256]{1,0:T(8,128)S(1)}, u32[]{:S(2)}, u32[]{:S(2)}) collective-permute-start(f32[64,256]{1,0:T(8,128)S(1)} %get-tuple-element.219), channel_id=1, source_target_pairs={{19,18},{16,19},{17,16},{0,17},{1,0},{8,1},{9,8},{24,9},{25,24},{2... | collective-permute-start | bytes 196616 | tf_op jit(solution)/shard_map/ppermute | solution.py:1016
  87.4 3.8 %collective-permute-start.18 = (f32[64,256]{1,0:T(8,128)S(1)}, f32[64,256]{1,0:T(8,128)S(1)}, u32[]{:S(2)}, u32[]{:S(2)}) collective-permute-start(f32[64,256]{1,0:T(8,128)S(1)} %get-tuple-element.227), channel_id=1, source_target_pairs={{18,19},{19,16},{16,17},{17,0},{0,1},{1,8},{8,9},{9,24},{24,25},{2... | collective-permute-start | bytes 196616 | tf_op jit(solution)/shard_map/ppermute | solution.py:1016
  88.4 3.0 %collective-permute-start.19 = (f32[64,256]{1,0:T(8,128)S(1)}, f32[64,256]{1,0:T(8,128)S(1)}, u32[]{:S(2)}, u32[]{:S(2)}) collective-permute-start(f32[64,256]{1,0:T(8,128)S(1)} %get-tuple-element.228), channel_id=1, source_target_pairs={{19,18},{16,19},{17,16},{0,17},{1,0},{8,1},{9,8},{24,9},{25,24},{2... | collective-permute-start | bytes 196616 | tf_op jit(solution)/shard_map/ppermute | solution.py:1016
  92.0 3.8 %collective-permute-start.20 = (f32[64,256]{1,0:T(8,128)S(1)}, f32[64,256]{1,0:T(8,128)S(1)}, u32[]{:S(2)}, u32[]{:S(2)}) collective-permute-start(f32[64,256]{1,0:T(8,128)S(1)} %get-tuple-element.234), channel_id=1, source_target_pairs={{18,19},{19,16},{16,17},{17,0},{0,1},{1,8},{8,9},{9,24},{24,25},{2... | collective-permute-start | bytes 196616 | tf_op jit(solution)/shard_map/ppermute | solution.py:1016
  93.1 2.8 %collective-permute-start.21 = (f32[64,256]{1,0:T(8,128)S(1)}, f32[64,256]{1,0:T(8,128)S(1)}, u32[]{:S(2)}, u32[]{:S(2)}) collective-permute-start(f32[64,256]{1,0:T(8,128)S(1)} %get-tuple-element.235), channel_id=1, source_target_pairs={{19,18},{16,19},{17,16},{0,17},{1,0},{8,1},{9,8},{24,9},{25,24},{2... | collective-permute-start | bytes 196616 | tf_op jit(solution)/shard_map/ppermute | solution.py:1016
  96.5 3.8 %collective-permute-start.22 = (f32[64,256]{1,0:T(8,128)S(1)}, f32[64,256]{1,0:T(8,128)S(1)}, u32[]{:S(2)}, u32[]{:S(2)}) collective-permute-start(f32[64,256]{1,0:T(8,128)S(1)} %get-tuple-element.243), channel_id=1, source_target_pairs={{18,19},{19,16},{16,17},{17,0},{0,1},{1,8},{8,9},{9,24},{24,25},{2... | collective-permute-start | bytes 196616 | tf_op jit(solution)/shard_map/ppermute | solution.py:1016
  97.5 2.8 %collective-permute-start.23 = (f32[64,256]{1,0:T(8,128)S(1)}, f32[64,256]{1,0:T(8,128)S(1)}, u32[]{:S(2)}, u32[]{:S(2)}) collective-permute-start(f32[64,256]{1,0:T(8,128)S(1)} %get-tuple-element.244), channel_id=1, source_target_pairs={{19,18},{16,19},{17,16},{0,17},{1,0},{8,1},{9,8},{24,9},{25,24},{2... | collective-permute-start | bytes 196616 | tf_op jit(solution)/shard_map/ppermute | solution.py:1016
  100.9 3.8 %collective-permute-start.24 = (f32[64,256]{1,0:T(8,128)S(1)}, f32[64,256]{1,0:T(8,128)S(1)}, u32[]{:S(2)}, u32[]{:S(2)}) collective-permute-start(f32[64,256]{1,0:T(8,128)S(1)} %get-tuple-element.251), channel_id=1, source_target_pairs={{18,19},{19,16},{16,17},{17,0},{0,1},{1,8},{8,9},{9,24},{24,25},{2... | collective-permute-start | bytes 196616 | tf_op jit(solution)/shard_map/ppermute | solution.py:1016
  102.0 2.8 %collective-permute-start.25 = (f32[64,256]{1,0:T(8,128)S(1)}, f32[64,256]{1,0:T(8,128)S(1)}, u32[]{:S(2)}, u32[]{:S(2)}) collective-permute-start(f32[64,256]{1,0:T(8,128)S(1)} %get-tuple-element.252), channel_id=1, source_target_pairs={{19,18},{16,19},{17,16},{0,17},{1,0},{8,1},{9,8},{24,9},{25,24},{2... | collective-permute-start | bytes 196616 | tf_op jit(solution)/shard_map/ppermute | solution.py:1016
  105.4 3.8 %collective-permute-start.26 = (f32[64,256]{1,0:T(8,128)S(1)}, f32[64,256]{1,0:T(8,128)S(1)}, u32[]{:S(2)}, u32[]{:S(2)}) collective-permute-start(f32[64,256]{1,0:T(8,128)S(1)} %get-tuple-element.260), channel_id=1, source_target_pairs={{18,19},{19,16},{16,17},{17,0},{0,1},{1,8},{8,9},{9,24},{24,25},{2... | collective-permute-start | bytes 196616 | tf_op jit(solution)/shard_map/ppermute | solution.py:1016
  106.4 2.8 %collective-permute-start.27 = (f32[64,256]{1,0:T(8,128)S(1)}, f32[64,256]{1,0:T(8,128)S(1)}, u32[]{:S(2)}, u32[]{:S(2)}) collective-permute-start(f32[64,256]{1,0:T(8,128)S(1)} %get-tuple-element.261), channel_id=1, source_target_pairs={{19,18},{16,19},{17,16},{0,17},{1,0},{8,1},{9,8},{24,9},{25,24},{2... | collective-permute-start | bytes 196616 | tf_op jit(solution)/shard_map/ppermute | solution.py:1016
  109.8 3.8 %collective-permute-start.28 = (f32[64,256]{1,0:T(8,128)S(1)}, f32[64,256]{1,0:T(8,128)S(1)}, u32[]{:S(2)}, u32[]{:S(2)}) collective-permute-start(f32[64,256]{1,0:T(8,128)S(1)} %get-tuple-element.267), channel_id=1, source_target_pairs={{18,19},{19,16},{16,17},{17,0},{0,1},{1,8},{8,9},{9,24},{24,25},{2... | collective-permute-start | bytes 196616 | tf_op jit(solution)/shard_map/ppermute | solution.py:1016
  110.8 2.8 %collective-permute-start.29 = (f32[64,256]{1,0:T(8,128)S(1)}, f32[64,256]{1,0:T(8,128)S(1)}, u32[]{:S(2)}, u32[]{:S(2)}) collective-permute-start(f32[64,256]{1,0:T(8,128)S(1)} %get-tuple-element.268), channel_id=1, source_target_pairs={{19,18},{16,19},{17,16},{0,17},{1,0},{8,1},{9,8},{24,9},{25,24},{2... | collective-permute-start | bytes 196616 | tf_op jit(solution)/shard_map/ppermute | solution.py:1016
  114.3 3.8 %collective-permute-start.30 = (f32[64,256]{1,0:T(8,128)S(1)}, f32[64,256]{1,0:T(8,128)S(1)}, u32[]{:S(2)}, u32[]{:S(2)}) collective-permute-start(f32[64,256]{1,0:T(8,128)S(1)} %get-tuple-element.276), channel_id=1, source_target_pairs={{18,19},{19,16},{16,17},{17,0},{0,1},{1,8},{8,9},{9,24},{24,25},{2... | collective-permute-start | bytes 196616 | tf_op jit(solution)/shard_map/ppermute | solution.py:1016
  115.3 2.8 %collective-permute-start.31 = (f32[64,256]{1,0:T(8,128)S(1)}, f32[64,256]{1,0:T(8,128)S(1)}, u32[]{:S(2)}, u32[]{:S(2)}) collective-permute-start(f32[64,256]{1,0:T(8,128)S(1)} %get-tuple-element.277), channel_id=1, source_target_pairs={{19,18},{16,19},{17,16},{0,17},{1,0},{8,1},{9,8},{24,9},{25,24},{2... | collective-permute-start | bytes 196616 | tf_op jit(solution)/shard_map/ppermute | solution.py:1016
  118.7 3.8 %collective-permute-start.32 = (f32[64,256]{1,0:T(8,128)S(1)}, f32[64,256]{1,0:T(8,128)S(1)}, u32[]{:S(2)}, u32[]{:S(2)}) collective-permute-start(f32[64,256]{1,0:T(8,128)S(1)} %get-tuple-element.284), channel_id=1, source_target_pairs={{18,19},{19,16},{16,17},{17,0},{0,1},{1,8},{8,9},{9,24},{24,25},{2... | collective-permute-start | bytes 196616 | tf_op jit(solution)/shard_map/ppermute | solution.py:1016
  119.7 2.8 %collective-permute-start.33 = (f32[64,256]{1,0:T(8,128)S(1)}, f32[64,256]{1,0:T(8,128)S(1)}, u32[]{:S(2)}, u32[]{:S(2)}) collective-permute-start(f32[64,256]{1,0:T(8,128)S(1)} %get-tuple-element.285), channel_id=1, source_target_pairs={{19,18},{16,19},{17,16},{0,17},{1,0},{8,1},{9,8},{24,9},{25,24},{2... | collective-permute-start | bytes 196616 | tf_op jit(solution)/shard_map/ppermute | solution.py:1016
  135.5 3.7 %collective-permute-start.34 = (f32[64,256]{1,0:T(8,128)S(1)}, f32[64,256]{1,0:T(8,128)S(1)}, u32[]{:S(2)}, u32[]{:S(2)}) collective-permute-start(f32[64,256]{1,0:T(8,128)S(1)} %get-tuple-element.293), channel_id=1, source_target_pairs={{18,19},{19,16},{16,17},{17,0},{0,1},{1,8},{8,9},{9,24},{24,25},{2... | collective-permute-start | bytes 196616 | tf_op jit(solution)/shard_map/ppermute | solution.py:1016
  135.9 3.4 %collective-permute-start.35 = (f32[64,256]{1,0:T(8,128)S(1)}, f32[64,256]{1,0:T(8,128)S(1)}, u32[]{:S(2)}, u32[]{:S(2)}) collective-permute-start(f32[64,256]{1,0:T(8,128)S(1)} %get-tuple-element.294), channel_id=1, source_target_pairs={{19,18},{16,19},{17,16},{0,17},{1,0},{8,1},{9,8},{24,9},{25,24},{2... | collective-permute-start | bytes 196616 | tf_op jit(solution)/shard_map/ppermute | solution.py:1016
  139.9 3.7 %collective-permute-start.36 = (f32[64,256]{1,0:T(8,128)S(1)}, f32[64,256]{1,0:T(8,128)S(1)}, u32[]{:S(2)}, u32[]{:S(2)}) collective-permute-start(f32[64,256]{1,0:T(8,128)S(1)} %get-tuple-element.298), channel_id=1, source_target_pairs={{18,19},{19,16},{16,17},{17,0},{0,1},{1,8},{8,9},{9,24},{24,25},{2... | collective-permute-start | bytes 196616 | tf_op jit(solution)/shard_map/ppermute | solution.py:1016
  140.9 3.0 %collective-permute-start.37 = (f32[64,256]{1,0:T(8,128)S(1)}, f32[64,256]{1,0:T(8,128)S(1)}, u32[]{:S(2)}, u32[]{:S(2)}) collective-permute-start(f32[64,256]{1,0:T(8,128)S(1)} %get-tuple-element.299), channel_id=1, source_target_pairs={{19,18},{16,19},{17,16},{0,17},{1,0},{8,1},{9,8},{24,9},{25,24},{2... | collective-permute-start | bytes 196616 | tf_op jit(solution)/shard_map/ppermute | solution.py:1016
  144.6 3.8 %collective-permute-start.38 = (f32[64,256]{1,0:T(8,128)S(1)}, f32[64,256]{1,0:T(8,128)S(1)}, u32[]{:S(2)}, u32[]{:S(2)}) collective-permute-start(f32[64,256]{1,0:T(8,128)S(1)} %get-tuple-element.307), channel_id=1, source_target_pairs={{18,19},{19,16},{16,17},{17,0},{0,1},{1,8},{8,9},{9,24},{24,25},{2... | collective-permute-start | bytes 196616 | tf_op jit(solution)/shard_map/ppermute | solution.py:1016
  145.6 2.8 %collective-permute-start.39 = (f32[64,256]{1,0:T(8,128)S(1)}, f32[64,256]{1,0:T(8,128)S(1)}, u32[]{:S(2)}, u32[]{:S(2)}) collective-permute-start(f32[64,256]{1,0:T(8,128)S(1)} %get-tuple-element.308), channel_id=1, source_target_pairs={{19,18},{16,19},{17,16},{0,17},{1,0},{8,1},{9,8},{24,9},{25,24},{2... | collective-permute-start | bytes 196616 | tf_op jit(solution)/shard_map/ppermute | solution.py:1016
  149.0 3.8 %collective-permute-start.40 = (f32[64,256]{1,0:T(8,128)S(1)}, f32[64,256]{1,0:T(8,128)S(1)}, u32[]{:S(2)}, u32[]{:S(2)}) collective-permute-start(f32[64,256]{1,0:T(8,128)S(1)} %get-tuple-element.314), channel_id=1, source_target_pairs={{18,19},{19,16},{16,17},{17,0},{0,1},{1,8},{8,9},{9,24},{24,25},{2... | collective-permute-start | bytes 196616 | tf_op jit(solution)/shard_map/ppermute | solution.py:1016
  150.0 2.8 %collective-permute-start.41 = (f32[64,256]{1,0:T(8,128)S(1)}, f32[64,256]{1,0:T(8,128)S(1)}, u32[]{:S(2)}, u32[]{:S(2)}) collective-permute-start(f32[64,256]{1,0:T(8,128)S(1)} %get-tuple-element.315), channel_id=1, source_target_pairs={{19,18},{16,19},{17,16},{0,17},{1,0},{8,1},{9,8},{24,9},{25,24},{2... | collective-permute-start | bytes 196616 | tf_op jit(solution)/shard_map/ppermute | solution.py:1016
  153.4 3.8 %collective-permute-start.42 = (f32[64,256]{1,0:T(8,128)S(1)}, f32[64,256]{1,0:T(8,128)S(1)}, u32[]{:S(2)}, u32[]{:S(2)}) collective-permute-start(f32[64,256]{1,0:T(8,128)S(1)} %get-tuple-element.323), channel_id=1, source_target_pairs={{18,19},{19,16},{16,17},{17,0},{0,1},{1,8},{8,9},{9,24},{24,25},{2... | collective-permute-start | bytes 196616 | tf_op jit(solution)/shard_map/ppermute | solution.py:1016
  154.5 2.8 %collective-permute-start.43 = (f32[64,256]{1,0:T(8,128)S(1)}, f32[64,256]{1,0:T(8,128)S(1)}, u32[]{:S(2)}, u32[]{:S(2)}) collective-permute-start(f32[64,256]{1,0:T(8,128)S(1)} %get-tuple-element.324), channel_id=1, source_target_pairs={{19,18},{16,19},{17,16},{0,17},{1,0},{8,1},{9,8},{24,9},{25,24},{2... | collective-permute-start | bytes 196616 | tf_op jit(solution)/shard_map/ppermute | solution.py:1016
  158.1 10.2 %collective-permute-start.47 = (f32[2,64,256]{2,1,0:T(8,128)S(1)}, f32[2,64,256]{2,1,0:T(8,128)S(1)}, u32[]{:S(2)}, u32[]{:S(2)}) collective-permute-start(f32[2,64,256]{2,1,0:T(8,128)S(1)} %get-tuple-element.332), channel_id=1, source_target_pairs={{17,0},{9,1},{27,2},{3,3},{13,4},{29,5},{7,6},{21,7},{16,8},{1,9},... | collective-permute-start | bytes 393224 | tf_op jit(solution)/shard_map/ppermute | solution.py:1161
  161.8 6.9 %collective-permute-start.46 = (f32[2,64,256]{2,1,0:T(8,128)S(1)}, f32[2,64,256]{2,1,0:T(8,128)S(1)}, u32[]{:S(2)}, u32[]{:S(2)}) collective-permute-start(f32[2,64,256]{2,1,0:T(8,128)S(1)} %get-tuple-element.331), channel_id=1, source_target_pairs={{16,0},{8,1},{26,2},{2,3},{12,4},{28,5},{6,6},{20,7},{17,8},{0,9},... | collective-permute-start | bytes 393224 | tf_op jit(solution)/shard_map/ppermute | solution.py:1161
  164.2 7.9 %collective-permute-start.45 = (f32[2,64,256]{2,1,0:T(8,128)S(1)}, f32[2,64,256]{2,1,0:T(8,128)S(1)}, u32[]{:S(2)}, u32[]{:S(2)}) collective-permute-start(f32[2,64,256]{2,1,0:T(8,128)S(1)} %get-tuple-element.330), channel_id=1, source_target_pairs={{19,0},{1,1},{25,2},{11,3},{5,4},{31,5},{15,6},{23,7},{18,8},{9,9}... | collective-permute-start | bytes 393224 | tf_op jit(solution)/shard_map/ppermute | solution.py:1161
  166.2 9.1 %collective-permute-start.44 = (f32[2,64,256]{2,1,0:T(8,128)S(1)}, f32[2,64,256]{2,1,0:T(8,128)S(1)}, u32[]{:S(2)}, u32[]{:S(2)}) collective-permute-start(f32[2,64,256]{2,1,0:T(8,128)S(1)} %get-tuple-element.329), channel_id=1, source_target_pairs={{18,0},{0,1},{24,2},{10,3},{4,4},{30,5},{14,6},{22,7},{19,8},{8,9}... | collective-permute-start | bytes 393224 | tf_op jit(solution)/shard_map/ppermute | solution.py:1161
  (9 other events, 100.8 us)
